TPU v7x, 32 devices: a whole 2x2x4 slice. The times are simulated.
32 devices in a mesh: dp: 4 (over y, core), row: 2 (over x), col: 4 (over z).
Axes of the slice: x: 2, y: 2, z: 4, core: 2. Of those that a mesh axis runs over, the one named last changes fastest.
Arguments:
- x_prompt: bfloat16 [4, 1024, 1536], P('dp', 'col', 'row'), may hold values from -6 to 6
- x_cont: bfloat16 [4, 8, 128, 1536], P('dp', 'col', None, 'row'), may hold values from -6 to 6
- teacher_prompt: bfloat16 [4, 1024, 1536], P('dp', 'col', 'row'), may hold values from -12 to 12
- teacher_cont: bfloat16 [4, 8, 128, 1536], P('dp', 'col', None, 'row'), may hold values from -12 to 12
- segment_ids: int32 [4, 1024], P('dp'), may hold values from 0 to 3, never falling along the last dimension, each value on 1 to 512 neighbouring positions
- offsets: int32 [4, 8], P('dp'), may hold values from 1 to 1024
- prompt_valid: int32 [4, 1024], P('dp', 'col'), may hold values from 0 to 1
- cont_valid: int32 [4, 8, 128], P('dp', 'col'), may hold values from 0 to 1, as said below
- first_gain: bfloat16 [1536], P('row'), may hold values from 0.5 to 1.5
- w_query: bfloat16 [1536, 1536], P('row', 'col'), may hold values from -0.15625 to 0.15625
- w_key: bfloat16 [1536, 1536], P('row', 'col'), may hold values from -0.15625 to 0.15625
- w_value: bfloat16 [1536, 1536], P('row', 'col'), may hold values from -0.15625 to 0.15625
- w_outgate: bfloat16 [1536, 1536], P('row', 'col'), may hold values from -0.15625 to 0.15625
- w_forget: bfloat16 [1536, 24], P('row', 'col'), may hold values from -0.15625 to 0.15625
- forget_bias: float32 [24], P('col'), may hold values from 2.5 to 7.5
- w_out: bfloat16 [1536, 1536], P('col', 'row'), may hold values from -1.75 to 1.75
- second_gain: bfloat16 [1536], P('row'), may hold values from 0.5 to 1.5
- w_gate: bfloat16 [1536, 4096], P('row', 'col'), may hold values from -0.15625 to 0.15625
- w_up: bfloat16 [1536, 4096], P('row', 'col'), may hold values from -0.15625 to 0.15625
- w_down: bfloat16 [4096, 1536], P('col', 'row'), may hold values from -0.09375 to 0.09375
Outputs:
- loss: float32 [], replicated
- grad_prompt: float32 [4, 1024, 1536], P('dp', 'col', 'row')
- grad_cont: float32 [4, 8, 128, 1536], P('dp', 'col', None, 'row')
- grad_first_gain: float32 [1536], P('row')
- grad_query: float32 [1536, 1536], P('row', 'col')
- grad_key: float32 [1536, 1536], P('row', 'col')
- grad_value: float32 [1536, 1536], P('row', 'col')
- grad_outgate: float32 [1536, 1536], P('row', 'col')
- grad_forget: float32 [1536, 24], P('row', 'col')
- grad_forget_bias: float32 [24], P('col')
- grad_out: float32 [1536, 1536], P('col', 'row')
- grad_second_gain: float32 [1536], P('row')
- grad_gate: float32 [1536, 4096], P('row', 'col')
- grad_up: float32 [1536, 4096], P('row', 'col')
- grad_down: float32 [4096, 1536], P('col', 'row')
Inputs may be any that keep to these rules, and one draw needn't show every extreme that they name: `segment_ids`: within a group the document numbers never fall, each document has 1 to 512 positions. `cont_valid`: the first token of every continuation is valid.
All inputs are finite; a program needn't handle non-finite values.
Results may differ from a plain program's by a relative error of at most 0.024.
Values may be sent and summed in bfloat16 or wider, within the bound.
A program may use at most 256 MiB of HBM per device.

v0:
```python
import functools
import itertools

import jax
import jax.numpy as jnp
from jax import lax
from jax.experimental import pallas as pl
from jax.experimental.pallas import tpu as pltpu
from jax.sharding import Mesh, PartitionSpec as P

D = 1536
HEADS = 24
HEAD_DIM = 64
PROMPT = 1024
CONTS = 8
CLEN = 128


epsilon = 1e-06
highest = lax.Precision.HIGHEST
masked = -1e30


def matmul(left_op, right_op):
    return jnp.dot(left_op, right_op, preferred_element_type=jnp.float32)


def by_transpose(left_op, right_op):
    return lax.dot_general(
        left_op, right_op, (((1,), (1,)), ((), ())), preferred_element_type=jnp.float32
    )


def inner_rows(left_op, right_op):
    return lax.dot_general(
        left_op, right_op, (((0,), (0,)), ((), ())), preferred_element_type=jnp.float32
    )


def feature_total(partial_sum):
    return lax.psum(partial_sum, "row")


def group_rows(local_rows):
    return lax.all_gather(local_rows, "col", axis=0, tiled=True)


def token_sums(partial_rows):
    return lax.psum_scatter(
        partial_rows.astype(jnp.bfloat16), "col", scatter_dimension=0, tiled=True
    ).astype(jnp.float32)


def row_partials(partial_rows, col_count, blocks, quarter):
    shaped = partial_rows.reshape(
        col_count, blocks, lax.axis_size("row"), quarter, partial_rows.shape[-1]
    )
    return lax.psum_scatter(
        shaped.astype(jnp.bfloat16), "row", scatter_dimension=2, tiled=True
    ).astype(jnp.float32)


def head_rows(own_rows):
    gathered = lax.all_gather(own_rows, "row", axis=2, tiled=True)
    return gathered.reshape(-1, gathered.shape[-1])


def norm_forward(tokens, gain_vec):
    row_total = feature_total(jnp.sum(tokens * tokens, axis=-1))
    factor = lax.rsqrt(row_total / D + epsilon)
    scaled = tokens * factor[:, None]
    return (factor, scaled, (scaled * gain_vec).astype(jnp.bfloat16))


def norm_backward(grad_normed, factor, scaled, gain_vec):
    grad_scaled = grad_normed * gain_vec
    row_total = feature_total(jnp.sum(grad_scaled * scaled, axis=-1))
    gain_grad = jnp.sum(grad_normed * scaled, axis=0)
    return (gain_grad, factor[:, None] * (grad_scaled - scaled * (row_total / D)[:, None]))


def log_total(scores):
    row_top = jnp.max(scores, axis=-1, keepdims=True)
    return row_top + jnp.log(jnp.sum(jnp.exp(scores - row_top), axis=-1, keepdims=True))


def prompt_scores(queries, key_rows, cum_query, cum_key, allowed):
    raw_scores = jnp.einsum("qhd,khd->hqk", queries, key_rows, preferred_element_type=jnp.float32)
    raw_scores = raw_scores * HEAD_DIM ** (-0.5) + cum_query.T[:, :, None] - cum_key.T[:, None, :]
    return jnp.where(allowed[None], raw_scores, masked)


def cont_scores(queries, key_rows, key_cont, cum_query, cum_key, cum_cont, far_ok, near_ok):
    score_scale = HEAD_DIM ** (-0.5)
    query_cum = cum_query.transpose(0, 2, 1)[:, :, :, None]
    far_scores = jnp.einsum("jqhd,khd->jhqk", queries, key_rows, preferred_element_type=jnp.float32)
    far_scores = far_scores * score_scale + query_cum - cum_key.T[None, :, None, :]
    near_scores = jnp.einsum(
        "jqhd,jkhd->jhqk", queries, key_cont, preferred_element_type=jnp.float32
    )
    near_scores = near_scores * score_scale + query_cum - cum_cont.transpose(0, 2, 1)[:, :, None, :]
    far_scores = jnp.where(far_ok[:, None, None, :], far_scores, masked)
    near_scores = jnp.where(near_ok[None, None], near_scores, masked)
    return jnp.concatenate([far_scores, near_scores], axis=-1)


def wide_body(
    x_prompt,
    x_cont,
    teacher_prompt,
    teacher_cont,
    segment_ids,
    offsets,
    prompt_valid,
    cont_valid,
    first_gain,
    w_query,
    w_key,
    w_value,
    w_outgate,
    w_forget,
    forget_bias,
    w_out,
    second_gain,
    w_gate,
    w_up,
    w_down,
):
    row_count = lax.axis_size("row")
    col_count = lax.axis_size("col")
    row_index = lax.axis_index("row")
    local_prompt = x_prompt.shape[1]
    local_conts = x_cont.shape[1]
    quarter = CLEN // row_count
    local_tokens = local_prompt + local_conts * CLEN
    blocks = local_tokens // CLEN
    prompt_blocks = local_prompt // CLEN
    heads_here = w_forget.shape[1]
    width_here = heads_here * HEAD_DIM
    units_here = w_gate.shape[1]
    score_scale = HEAD_DIM ** (-0.5)
    w_project = jnp.concatenate([w_query, w_key, w_value, w_outgate], axis=1)
    w_hidden = jnp.concatenate([w_gate, w_up], axis=1)
    gain_one = first_gain.astype(jnp.float32)
    gain_two = second_gain.astype(jnp.float32)
    position = jnp.arange(PROMPT, dtype=jnp.int32)
    cont_step = jnp.arange(CLEN, dtype=jnp.int32)
    own_step = row_index * quarter + jnp.arange(quarter, dtype=jnp.int32)
    near_ok = cont_step[None, :] <= own_step[:, None]
    own_position = lax.dynamic_index_in_dim(
        position.reshape(col_count, prompt_blocks, row_count, quarter), row_index, 2, keepdims=False
    ).reshape(-1)

    def own_prompt_part(matrix):
        return matrix[:, :prompt_blocks, 0]

    def one_group(carried, group_data):
        (
            acc_project,
            acc_forget,
            acc_bias,
            acc_out,
            acc_hidden,
            acc_down,
            acc_gain_one,
            acc_gain_two,
            error_sum,
            count_sum,
        ) = carried
        (
            prompt_in,
            cont_in,
            teach_prompt,
            teach_cont,
            segment_row,
            offset_row,
            valid_prompt,
            valid_cont,
        ) = group_data
        tokens = jnp.concatenate(
            [prompt_in, cont_in.reshape(local_conts * CLEN, -1)], axis=0
        ).astype(jnp.float32)
        teacher = jnp.concatenate(
            [teach_prompt, teach_cont.reshape(local_conts * CLEN, -1)], axis=0
        ).astype(jnp.float32)
        validity = jnp.concatenate([valid_prompt, valid_cont.reshape(-1)], axis=0).astype(
            jnp.float32
        )
        branch_mask = position[None, :] == offset_row[:, None] - 1
        branch_hot = branch_mask.astype(jnp.float32)
        last_doc = jnp.sum(jnp.where(branch_mask, segment_row[None, :], 0), axis=1)
        far_ok = (position[None, :] < offset_row[:, None]) & (
            segment_row[None, :] == last_doc[:, None]
        )
        own_doc = lax.dynamic_index_in_dim(
            segment_row.reshape(col_count, prompt_blocks, row_count, quarter),
            row_index,
            2,
            keepdims=False,
        ).reshape(-1)
        prompt_ok = (position[None, :] <= own_position[:, None]) & (
            segment_row[None, :] == own_doc[:, None]
        )
        factor_one, scaled_one, normed_one = norm_forward(tokens, gain_one)
        normed_all = group_rows(normed_one)
        project_part = matmul(normed_all, w_project).reshape(
            col_count, blocks, row_count, quarter, 4 * width_here
        )
        forget_part = matmul(normed_all, w_forget).reshape(
            col_count, blocks, row_count, quarter, heads_here
        )
        own_project, own_forget = (
            lax.psum_scatter(project_part, "row", scatter_dimension=2, tiled=True),
            lax.psum_scatter(forget_part, "row", scatter_dimension=2, tiled=True),
        )
        own_query = own_project[..., :width_here].astype(jnp.bfloat16)
        own_kv = own_project[..., width_here : 3 * width_here].astype(jnp.bfloat16)
        gate_logit = own_project[..., 3 * width_here :]
        kv_all, forget_all = (
            lax.all_gather(own_kv, "row", axis=2, tiled=True),
            lax.all_gather(own_forget.astype(jnp.bfloat16), "row", axis=2, tiled=True),
        )
        kv_all = kv_all.reshape(col_count, local_tokens, 2 * width_here)
        pre_gate = (
            forget_all.reshape(col_count, local_tokens, heads_here).astype(jnp.float32)
            + forget_bias
        )
        log_keep = jax.nn.log_sigmoid(pre_gate)
        cum_prompt = jnp.cumsum(log_keep[:, :local_prompt].reshape(PROMPT, heads_here), axis=0)
        branch_cum = jnp.dot(branch_hot, cum_prompt, precision=highest)
        cum_cont = branch_cum[:, None, :] + jnp.cumsum(
            log_keep[:, local_prompt:].reshape(CONTS, CLEN, heads_here), axis=1
        )
        kv_prompt = kv_all[:, :local_prompt].reshape(PROMPT, 2, heads_here, HEAD_DIM)
        key_prompt = kv_prompt[:, 0]
        value_prompt = kv_prompt[:, 1]
        kv_cont = kv_all[:, local_prompt:].reshape(CONTS, CLEN, 2, heads_here, HEAD_DIM)
        key_cont = kv_cont[:, :, 0]
        value_cont = kv_cont[:, :, 1]
        cum_query_prompt = lax.dynamic_index_in_dim(
            cum_prompt.reshape(col_count, prompt_blocks, row_count, quarter, heads_here),
            row_index,
            2,
            keepdims=False,
        ).reshape(-1, heads_here)
        cum_query_cont = lax.dynamic_index_in_dim(
            cum_cont.reshape(CONTS, row_count, quarter, heads_here), row_index, 1, keepdims=False
        )
        query_prompt = own_prompt_part(own_query).reshape(-1, heads_here, HEAD_DIM)
        query_cont = own_query[:, prompt_blocks:, 0].reshape(CONTS, quarter, heads_here, HEAD_DIM)
        scores_prompt = prompt_scores(
            query_prompt, key_prompt, cum_query_prompt, cum_prompt, prompt_ok
        )
        total_prompt = log_total(scores_prompt)
        probs_prompt = jnp.exp(scores_prompt - total_prompt).astype(jnp.bfloat16)
        out_prompt = jnp.einsum(
            "hqk,khd->qhd", probs_prompt, value_prompt, preferred_element_type=jnp.float32
        )
        scores_cont = cont_scores(
            query_cont, key_prompt, key_cont, cum_query_cont, cum_prompt, cum_cont, far_ok, near_ok
        )
        total_cont = log_total(scores_cont)
        probs_cont = jnp.exp(scores_cont - total_cont).astype(jnp.bfloat16)
        out_cont = jnp.einsum(
            "jhqk,khd->jqhd",
            probs_cont[..., :PROMPT],
            value_prompt,
            preferred_element_type=jnp.float32,
        )
        out_cont = out_cont + jnp.einsum(
            "jhqk,jkhd->jqhd",
            probs_cont[..., PROMPT:],
            value_cont,
            preferred_element_type=jnp.float32,
        )
        attended = jnp.concatenate(
            [
                out_prompt.reshape(col_count, prompt_blocks, 1, quarter, width_here),
                out_cont.reshape(col_count, local_conts, 1, quarter, width_here),
            ],
            axis=1,
        )
        gate_sig = jax.nn.sigmoid(gate_logit)
        gated = (attended * gate_sig).astype(jnp.bfloat16)
        gated_all = head_rows(gated)
        residual = tokens + token_sums(matmul(gated_all, w_out))
        factor_two, scaled_two, normed_two = norm_forward(residual, gain_two)
        normed_two_all = group_rows(normed_two)
        hidden_own = row_partials(matmul(normed_two_all, w_hidden), col_count, blocks, quarter)
        gate_rows = hidden_own[..., :units_here]
        up_rows = hidden_own[..., units_here:]
        gate_sig_two = jax.nn.sigmoid(gate_rows)
        silu_rows = gate_rows * gate_sig_two
        hidden_all = head_rows((silu_rows * up_rows).astype(jnp.bfloat16))
        result_rows = residual + token_sums(matmul(hidden_all, w_down))
        deviation = result_rows - teacher
        group_err = 0.5 * jnp.sum(validity[:, None] * deviation * deviation)
        grad_result = validity[:, None] * deviation
        grad_result_all = group_rows(grad_result.astype(jnp.bfloat16))
        grad_down_w = inner_rows(hidden_all, grad_result_all)
        grad_hid = row_partials(by_transpose(grad_result_all, w_down), col_count, blocks, quarter)
        grad_gate = grad_hid * up_rows * gate_sig_two * (1.0 + gate_rows * (1.0 - gate_sig_two))
        grad_up = grad_hid * silu_rows
        grad_hidden_all = head_rows(
            jnp.concatenate([grad_gate, grad_up], axis=-1).astype(jnp.bfloat16)
        )
        grad_hidden_w = inner_rows(normed_two_all, grad_hidden_all)
        grad_normed_two = token_sums(by_transpose(grad_hidden_all, w_hidden))
        gain_two_grad, grad_residual = norm_backward(
            grad_normed_two, factor_two, scaled_two, gain_two
        )
        grad_residual = grad_residual + grad_result
        grad_residual_all = group_rows(grad_residual.astype(jnp.bfloat16))
        grad_out_w = inner_rows(gated_all, grad_residual_all)
        grad_gated = row_partials(
            by_transpose(grad_residual_all, w_out), col_count, blocks, quarter
        )
        grad_attended = (grad_gated * gate_sig).astype(jnp.bfloat16)
        grad_logit = (grad_gated * attended * gate_sig * (1.0 - gate_sig)).astype(jnp.bfloat16)
        grad_att_prompt = own_prompt_part(grad_attended).reshape(-1, heads_here, HEAD_DIM)
        grad_att_cont = grad_attended[:, prompt_blocks:, 0].reshape(
            CONTS, quarter, heads_here, HEAD_DIM
        )
        again_prompt = jnp.exp(
            prompt_scores(query_prompt, key_prompt, cum_query_prompt, cum_prompt, prompt_ok)
            - total_prompt
        )
        grad_prob_prompt = jnp.einsum(
            "qhd,khd->hqk", grad_att_prompt, value_prompt, preferred_element_type=jnp.float32
        )
        grad_score_prompt = (
            again_prompt
            * (grad_prob_prompt - jnp.sum(again_prompt * grad_prob_prompt, axis=-1, keepdims=True))
        ).astype(jnp.bfloat16)
        again_prompt_b = again_prompt.astype(jnp.bfloat16)
        grad_query_prompt = (
            jnp.einsum(
                "hqk,khd->qhd", grad_score_prompt, key_prompt, preferred_element_type=jnp.float32
            )
            * score_scale
        )
        grad_key_prompt = (
            jnp.einsum(
                "hqk,qhd->khd", grad_score_prompt, query_prompt, preferred_element_type=jnp.float32
            )
            * score_scale
        )
        grad_value_prompt = jnp.einsum(
            "hqk,qhd->khd", again_prompt_b, grad_att_prompt, preferred_element_type=jnp.float32
        )
        cum_grad_query_p = jnp.sum(grad_score_prompt, axis=-1, dtype=jnp.float32).T
        cum_grad_key_p = -jnp.sum(grad_score_prompt, axis=1, dtype=jnp.float32).T
        again_cont = jnp.exp(
            cont_scores(
                query_cont,
                key_prompt,
                key_cont,
                cum_query_cont,
                cum_prompt,
                cum_cont,
                far_ok,
                near_ok,
            )
            - total_cont
        )
        grad_prob_cont = jnp.concatenate(
            [
                jnp.einsum(
                    "jqhd,khd->jhqk",
                    grad_att_cont,
                    value_prompt,
                    preferred_element_type=jnp.float32,
                ),
                jnp.einsum(
                    "jqhd,jkhd->jhqk", grad_att_cont, value_cont, preferred_element_type=jnp.float32
                ),
            ],
            axis=-1,
        )
        grad_score_cont = (
            again_cont
            * (grad_prob_cont - jnp.sum(again_cont * grad_prob_cont, axis=-1, keepdims=True))
        ).astype(jnp.bfloat16)
        again_cont_b = again_cont.astype(jnp.bfloat16)
        far_grad = grad_score_cont[..., :PROMPT]
        near_grad = grad_score_cont[..., PROMPT:]
        grad_query_cont = (
            jnp.einsum("jhqk,khd->jqhd", far_grad, key_prompt, preferred_element_type=jnp.float32)
            + jnp.einsum("jhqk,jkhd->jqhd", near_grad, key_cont, preferred_element_type=jnp.float32)
        ) * score_scale
        grad_key_far = (
            jnp.einsum("jhqk,jqhd->khd", far_grad, query_cont, preferred_element_type=jnp.float32)
            * score_scale
        )
        grad_key_near = (
            jnp.einsum("jhqk,jqhd->jkhd", near_grad, query_cont, preferred_element_type=jnp.float32)
            * score_scale
        )
        grad_value_far = jnp.einsum(
            "jhqk,jqhd->khd",
            again_cont_b[..., :PROMPT],
            grad_att_cont,
            preferred_element_type=jnp.float32,
        )
        grad_value_near = jnp.einsum(
            "jhqk,jqhd->jkhd",
            again_cont_b[..., PROMPT:],
            grad_att_cont,
            preferred_element_type=jnp.float32,
        )
        cum_grad_query_c = jnp.sum(grad_score_cont, axis=-1, dtype=jnp.float32).transpose(0, 2, 1)
        cum_grad_key_far = -jnp.sum(far_grad, axis=(0, 2), dtype=jnp.float32).T
        cum_grad_key_near = -jnp.sum(near_grad, axis=2, dtype=jnp.float32).transpose(0, 2, 1)
        kv_grad_prompt = jnp.stack(
            [grad_key_prompt + grad_key_far, grad_value_prompt + grad_value_far], axis=1
        ).reshape(col_count, local_prompt, 2 * width_here)
        kv_grad_cont = jnp.stack([grad_key_near, grad_value_near], axis=2).reshape(
            col_count, local_conts * CLEN, 2 * width_here
        )
        kv_grad_part = jnp.concatenate([kv_grad_prompt, kv_grad_cont], axis=1)
        query_place = lax.dynamic_update_slice_in_dim(
            jnp.zeros((col_count, prompt_blocks, row_count, quarter, heads_here), jnp.float32),
            cum_grad_query_p.reshape(col_count, prompt_blocks, 1, quarter, heads_here),
            row_index,
            axis=2,
        ).reshape(PROMPT, heads_here)
        cont_place = lax.dynamic_update_slice_in_dim(
            jnp.zeros((CONTS, row_count, quarter, heads_here), jnp.float32),
            cum_grad_query_c.reshape(CONTS, 1, quarter, heads_here),
            row_index,
            axis=1,
        ).reshape(CONTS, CLEN, heads_here)
        cum_grad_part = jnp.concatenate(
            [
                (cum_grad_key_p + cum_grad_key_far + query_place).reshape(
                    col_count, local_prompt, heads_here
                ),
                (cum_grad_key_near + cont_place).reshape(col_count, local_conts * CLEN, heads_here),
            ],
            axis=1,
        )
        kv_grad_full, cum_grad_full = lax.psum((kv_grad_part, cum_grad_part), "row")
        cum_grad_cont = cum_grad_full[:, local_prompt:].reshape(CONTS, CLEN, heads_here)
        cum_grad_prompt = cum_grad_full[:, :local_prompt].reshape(PROMPT, heads_here)
        cum_grad_prompt = cum_grad_prompt + jnp.dot(
            branch_hot.T, jnp.sum(cum_grad_cont, axis=1), precision=highest
        )
        log_grad_prompt = lax.cumsum(cum_grad_prompt, axis=0, reverse=True)
        log_grad_cont = lax.cumsum(cum_grad_cont, axis=1, reverse=True)
        log_grad = jnp.concatenate(
            [
                log_grad_prompt.reshape(col_count, local_prompt, heads_here),
                log_grad_cont.reshape(col_count, local_conts * CLEN, heads_here),
            ],
            axis=1,
        )
        pre_grad = log_grad * jax.nn.sigmoid(-pre_gate)
        bias_grad = jnp.sum(pre_grad, axis=(0, 1))
        forget_grad_b = pre_grad.reshape(-1, heads_here).astype(jnp.bfloat16)
        query_grad_own = jnp.concatenate(
            [
                grad_query_prompt.reshape(col_count, prompt_blocks, 1, quarter, width_here),
                grad_query_cont.reshape(col_count, local_conts, 1, quarter, width_here),
            ],
            axis=1,
        )
        qg_grad_all = head_rows(
            jnp.concatenate([query_grad_own.astype(jnp.bfloat16), grad_logit], axis=-1)
        )
        kv_grad_rows = kv_grad_full.reshape(-1, 2 * width_here).astype(jnp.bfloat16)
        project_grad_rows = jnp.concatenate(
            [qg_grad_all[:, :width_here], kv_grad_rows, qg_grad_all[:, width_here:]], axis=-1
        )
        grad_project_w = inner_rows(normed_all, project_grad_rows)
        grad_forget_w = inner_rows(normed_all, forget_grad_b)
        grad_normed_one = token_sums(
            by_transpose(project_grad_rows, w_project) + by_transpose(forget_grad_b, w_forget)
        )
        gain_one_grad, grad_tokens = norm_backward(
            grad_normed_one, factor_one, scaled_one, gain_one
        )
        grad_tokens = grad_tokens + grad_residual
        grad_prompt_one = grad_tokens[:local_prompt]
        grad_cont_one = grad_tokens[local_prompt:].reshape(local_conts, CLEN, -1)
        group_count = jnp.sum(validity) * (row_index == 0).astype(jnp.float32)
        new_carry = (
            acc_project + grad_project_w,
            acc_forget + grad_forget_w,
            acc_bias + bias_grad,
            acc_out + grad_out_w,
            acc_hidden + grad_hidden_w,
            acc_down + grad_down_w,
            acc_gain_one + gain_one_grad,
            acc_gain_two + gain_two_grad,
            error_sum + group_err,
            count_sum + group_count,
        )
        return (new_carry, (grad_prompt_one, grad_cont_one))

    start = (
        jnp.zeros(w_project.shape, jnp.float32),
        jnp.zeros(w_forget.shape, jnp.float32),
        jnp.zeros(forget_bias.shape, jnp.float32),
        jnp.zeros(w_out.shape, jnp.float32),
        jnp.zeros(w_hidden.shape, jnp.float32),
        jnp.zeros(w_down.shape, jnp.float32),
        jnp.zeros(first_gain.shape, jnp.float32),
        jnp.zeros(second_gain.shape, jnp.float32),
        jnp.zeros((), jnp.float32),
        jnp.zeros((), jnp.float32),
    )
    finished, (grad_prompt, grad_cont) = lax.scan(
        one_group,
        start,
        (
            x_prompt,
            x_cont,
            teacher_prompt,
            teacher_cont,
            segment_ids,
            offsets,
            prompt_valid,
            cont_valid,
        ),
    )
    (
        acc_project,
        acc_forget,
        acc_bias,
        acc_out,
        acc_hidden,
        acc_down,
        acc_gain_one,
        acc_gain_two,
        error_sum,
        count_sum,
    ) = finished
    acc_project, acc_forget, acc_bias, acc_out, acc_hidden, acc_down = (
        lax.psum(acc_project.astype(jnp.bfloat16), "dp").astype(jnp.float32),
        lax.psum(acc_forget.astype(jnp.bfloat16), "dp").astype(jnp.float32),
        lax.psum(acc_bias.astype(jnp.bfloat16), "dp").astype(jnp.float32),
        lax.psum(acc_out.astype(jnp.bfloat16), "dp").astype(jnp.float32),
        lax.psum(acc_hidden.astype(jnp.bfloat16), "dp").astype(jnp.float32),
        lax.psum(acc_down.astype(jnp.bfloat16), "dp").astype(jnp.float32),
    )
    gain_one_total, gain_two_total = lax.psum((acc_gain_one, acc_gain_two), ("dp", "col"))
    error_total, count_total = lax.psum((error_sum, count_sum), ("dp", "row", "col"))
    grad_scale = x_prompt.shape[0] * lax.axis_size("dp") * (PROMPT + CONTS * CLEN) / count_total
    loss_value = error_total / (D * count_total)
    width_here = w_query.shape[1]
    units_here = w_gate.shape[1]
    return (
        loss_value,
        grad_prompt * grad_scale,
        grad_cont * grad_scale,
        gain_one_total * grad_scale,
        acc_project[:, :width_here] * grad_scale,
        acc_project[:, width_here : 2 * width_here] * grad_scale,
        acc_project[:, 2 * width_here : 3 * width_here] * grad_scale,
        acc_project[:, 3 * width_here :] * grad_scale,
        acc_forget * grad_scale,
        acc_bias * grad_scale,
        acc_out * grad_scale,
        gain_two_total * grad_scale,
        acc_hidden[:, :units_here] * grad_scale,
        acc_hidden[:, units_here:] * grad_scale,
        acc_down * grad_scale,
    )


AX = ("yo", "y", "c", "x", "zh", "zl")
FAR_PIECE = 18
DOC_LANE = 36
UNIT_LANE = 40
NEVER = 1e12
LANES = 128
BF = jnp.bfloat16
F32 = jnp.float32


class Ring:
    def __init__(self, sizes):
        self.sizes = sizes
        self.zl_count = sizes["zl"]
        self.offsets = [(dy, dz) for dy in range(2) for dz in range(self.zl_count)]
        self.back = [
            self.offsets.index(((-dy) % 2, (-dz) % self.zl_count)) for dy, dz in self.offsets
        ]

    def pairs(self, target, source_ok=None):
        ranges = [range(self.sizes[a]) for a in AX]
        number = {}
        for place, coords in enumerate(itertools.product(*ranges)):
            number[coords] = place
        out = []
        for coords in number:
            here = dict(zip(AX, coords))
            if source_ok is not None and not source_ok(here):
                continue
            there = dict(here, **target(here))
            out.append((number[coords], number[tuple(there[a] for a in AX)]))
        return out

    def move(self, value, target, source_ok=None):
        return lax.ppermute(value, AX, self.pairs(target, source_ok))

    def swap(self, value, axis, source_ok=None):
        return self.move(value, lambda h: {axis: 1 - h[axis]}, source_ok)

    def to_peer(self, value, k):
        dy, dz = self.offsets[k]
        return self.move(
            value, lambda h: {"y": (h["y"] + dy) % 2, "zl": (h["zl"] + dz) % self.zl_count}
        )

    def to_group(self, value, flip):
        return self.move(
            value,
            lambda h: {
                "y": h["zh"],
                "c": h["x"] ^ flip,
                "x": h["y"],
                "zh": h["c"],
            },
        )

    def from_group(self, value, flip):
        return self.move(
            value,
            lambda h: {"y": h["x"], "c": h["zh"], "x": h["c"] ^ flip, "zh": h["y"]},
        )

    def total(self, value):
        for axis in ("c", "y", "x", "zh"):
            value = value + self.swap(value, axis)
        if self.zl_count == 2:
            value = value + self.swap(value, "zl")
        elif self.zl_count > 2:
            value = lax.psum(value, "zl")
        if self.sizes["yo"] > 1:
            value = lax.psum(value, "yo")
        return value

    def gather(self, rows):
        return [rows] + [self.to_peer(rows, k) for k in range(1, len(self.offsets))]

    def scatter_sum(self, partial_of):
        arrived = []
        for k in range(1, len(self.offsets)):
            arrived.append(self.to_peer(partial_of(self.back[k]).astype(BF), k))
        total = partial_of(0)
        for part in arrived:
            total = total + part.astype(F32)
        return total


def nt_dot(left_op, right_op):
    return lax.dot_general(
        left_op, right_op, (((1,), (1,)), ((), ())), preferred_element_type=F32
    )


def tn_dot(left_op, right_op):
    return lax.dot_general(
        left_op, right_op, (((0,), (0,)), ((), ())), preferred_element_type=F32
    )


def nn_dot(left_op, right_op):
    return jnp.dot(left_op, right_op, preferred_element_type=F32)


def split_pieces(values, shift, heads):
    high = values.astype(BF).astype(F32)
    rest = values - high
    mid = rest.astype(BF).astype(F32)
    low = (rest - mid).astype(BF).astype(F32)
    out = None
    for place, piece in enumerate((high, mid, low)):
        amount = shift + place * heads
        moved = pltpu.roll(piece, amount, 1) if amount else piece
        out = moved if out is None else out + moved
    return out


def head_lanes(shape, head, heads):
    lane = lax.broadcasted_iota(jnp.int32, shape, len(shape) - 1)
    keep = lane >= DOC_LANE
    for place in range(3):
        keep = keep | (lane == place * heads + head) | (lane == FAR_PIECE + place * heads + head)
    return keep


def half_lanes(shape, half):
    lane = lax.broadcasted_iota(jnp.int32, shape, len(shape) - 1)
    return (lane >= HEAD_DIM * half) & (lane < HEAD_DIM * (half + 1))


def near_visible(rows):
    key_row = lax.broadcasted_iota(jnp.int32, (rows, rows), 0)
    query_row = lax.broadcasted_iota(jnp.int32, (rows, rows), 1)
    same = (key_row // CLEN) == (query_row // CLEN)
    return same & (key_row <= query_row)


def fill_keys(
    keys, flag, far_own, far_there, kv_near, cum_far, cum_near, far_base, near_base, far_rows, heads
):
    slots = heads // 2

    @pl.when(pl.program_id(0) == 0)
    def _():
        aug = (far_base[...].astype(F32) + split_pieces(-cum_far[...], FAR_PIECE, heads)).astype(BF)
        for s in range(slots):
            keys[s, :far_rows, LANES:] = aug

        @pl.when(flag[0] == 0)
        def _():
            for s in range(slots):
                keys[s, :far_rows, :LANES] = far_own[s][:, :LANES]

        @pl.when(flag[0] != 0)
        def _():
            for s in range(slots):
                keys[s, :far_rows, :LANES] = far_there[s][:, :LANES]

    aug = (near_base[...].astype(F32) + split_pieces(-cum_near[...], FAR_PIECE, heads)).astype(BF)
    for s in range(slots):
        keys[s, far_rows:, :LANES] = kv_near[s][:, :LANES]
        keys[s, far_rows:, LANES:] = aug


def attend_kernel(
    heads,
    flag,
    qg_a,
    qg_b,
    qg_c,
    near_a,
    near_b,
    near_c,
    own_a,
    own_b,
    own_c,
    there_a,
    there_b,
    there_c,
    cum_near,
    cum_far,
    q_base,
    near_base,
    far_base,
    gated_ref,
    att_ref,
    log_ref,
    keys,
    vals,
):
    qg = (qg_a, qg_b, qg_c)
    kv_near = (near_a, near_b, near_c)
    far_own = (own_a, own_b, own_c)
    far_there = (there_a, there_b, there_c)
    rows = qg_a.shape[0]
    far_rows = own_a.shape[0]
    slots = heads // 2
    fill_keys(
        keys,
        flag,
        far_own,
        far_there,
        kv_near,
        cum_far,
        cum_near,
        far_base,
        near_base,
        far_rows,
        heads,
    )

    @pl.when(pl.program_id(0) == 0)
    def _():
        def fill(source):
            for s in range(slots):
                moved = source[s][:, LANES:].T
                for half in range(2):
                    vals[2 * s + half, :HEAD_DIM, :far_rows] = moved[
                        HEAD_DIM * half : HEAD_DIM * (half + 1)
                    ]

        @pl.when(flag[0] == 0)
        def _():
            fill(far_own)

        @pl.when(flag[0] != 0)
        def _():
            fill(far_there)

        for h in range(heads):
            vals[h, HEAD_DIM:, :] = jnp.ones((16, far_rows + rows), BF)

    for s in range(slots):
        moved = kv_near[s][:, LANES:].T
        for half in range(2):
            vals[2 * s + half, :HEAD_DIM, far_rows:] = moved[
                HEAD_DIM * half : HEAD_DIM * (half + 1)
            ]
    q_aug = (q_base[...].astype(F32) + split_pieces(cum_near[...], 0, heads)).astype(BF)
    visible = near_visible(rows)
    outs = []
    logs = []
    for h in range(heads):
        s, half = h // 2, h % 2
        query = qg[s][:, :LANES]
        query = jnp.where(half_lanes(query.shape, half), query * BF(HEAD_DIM**-0.5), BF(0))
        aug = jnp.where(head_lanes(q_aug.shape, h, heads), q_aug, BF(0))
        q_cat = jnp.concatenate([query, aug], axis=1)
        far = nt_dot(keys[s, :far_rows], q_cat)
        near = jnp.where(visible, nt_dot(keys[s, far_rows:], q_cat), -NEVER)
        top = jnp.maximum(
            jnp.max(far, axis=0, keepdims=True), jnp.max(near, axis=0, keepdims=True)
        )
        far_p = jnp.exp(far - top).astype(BF)
        near_p = jnp.exp(near - top).astype(BF)
        out = nn_dot(vals[h, :, :far_rows], far_p) + nn_dot(vals[h, :, far_rows:], near_p)
        total = out[HEAD_DIM : HEAD_DIM + 1]
        outs.append(out[:HEAD_DIM] / total)
        logs.append(top + jnp.log(total))
    att = jnp.concatenate(outs, axis=0).T
    att_ref[...] = att
    for s in range(slots):
        gate = qg[s][:, LANES:].astype(F32)
        cols = slice(s * LANES, (s + 1) * LANES)
        gated_ref[:, cols] = (att[:, cols] * jax.nn.sigmoid(gate)).astype(BF)
    log_rows = jnp.concatenate(logs + [jnp.zeros((LANES - heads, rows), F32)], axis=0)
    log_ref[...] = log_rows.T


def row_block(rows, cols, place=0):
    return pl.BlockSpec((rows, cols), lambda i: (i, place))


def whole_block(rows, cols):
    return pl.BlockSpec((rows, cols), lambda i: (0, 0))


def slot_inputs(flag, projects, kv_there, rows):
    far_rows = projects[0].shape[0]
    specs_in = [pl.BlockSpec(memory_space=pltpu.SMEM)]
    for spec in (
        row_block(rows, 2 * LANES),
        row_block(rows, 2 * LANES, 1),
        pl.BlockSpec((far_rows, 2 * LANES), lambda i: (0, 1)),
        whole_block(far_rows, 2 * LANES),
    ):
        specs_in += [spec] * len(projects)
    return specs_in, [flag, *projects, *projects, *projects, *kv_there]


def cum_specs(rows, far_rows):
    return [
        row_block(rows, LANES),
        whole_block(far_rows, LANES),
        row_block(rows, LANES),
        row_block(rows, LANES),
        whole_block(far_rows, LANES),
    ]


def attend(flag, projects, kv_there, cum_near, cum_far, q_base, near_base, far_base, rows, heads):
    total = projects[0].shape[0]
    width = heads * HEAD_DIM
    steps = total // rows
    flops = 2 * total * (total + rows) * heads * 384
    slot_specs, slot_values = slot_inputs(flag, projects, kv_there, rows)
    return pl.pallas_call(
        functools.partial(attend_kernel, heads),
        grid=(steps,),
        out_shape=(
            jax.ShapeDtypeStruct((total, width), BF),
            jax.ShapeDtypeStruct((total, width), F32),
            jax.ShapeDtypeStruct((total, LANES), F32),
        ),
        in_specs=slot_specs + cum_specs(rows, total),
        out_specs=(row_block(rows, width), row_block(rows, width), row_block(rows, LANES)),
        scratch_shapes=[
            pltpu.VMEM((heads // 2, total + rows, 2 * LANES), BF),
            pltpu.VMEM((heads, HEAD_DIM + 16, total + rows), BF),
        ],
        compiler_params=pltpu.CompilerParams(vmem_limit_bytes=48 << 20),
        cost_estimate=pl.CostEstimate(
            flops=flops, bytes_accessed=total * width * 20, transcendentals=total * total * heads
        ),
    )(*slot_values, cum_near, cum_far, q_base, near_base, far_base)


def attend_back_kernel(
    heads,
    flag,
    qg_a,
    qg_b,
    qg_c,
    near_a,
    near_b,
    near_c,
    own_a,
    own_b,
    own_c,
    there_a,
    there_b,
    there_c,
    cum_near,
    cum_far,
    q_base,
    near_base,
    far_base,
    grad_ref,
    att_ref,
    log_ref,
    dqg_ref,
    near_ref,
    far_out,
    row_ref,
    near_col,
    far_col,
    keys,
    vals,
    far_ref,
):
    qg = (qg_a, qg_b, qg_c)
    kv_near = (near_a, near_b, near_c)
    far_own = (own_a, own_b, own_c)
    far_there = (there_a, there_b, there_c)
    rows = qg_a.shape[0]
    far_rows = own_a.shape[0]
    slots = heads // 2
    fill_keys(
        keys,
        flag,
        far_own,
        far_there,
        kv_near,
        cum_far,
        cum_near,
        far_base,
        near_base,
        far_rows,
        heads,
    )

    @pl.when(pl.program_id(0) == 0)
    def _():
        lane = lax.broadcasted_iota(jnp.int32, (far_rows + rows, LANES), 1)
        ones = (lane < 3).astype(F32).astype(BF)
        for s in range(slots):
            vals[s, :, LANES:] = ones

        @pl.when(flag[0] == 0)
        def _():
            for s in range(slots):
                vals[s, :far_rows, :LANES] = far_own[s][:, LANES:]

        @pl.when(flag[0] != 0)
        def _():
            for s in range(slots):
                vals[s, :far_rows, :LANES] = far_there[s][:, LANES:]

        far_ref[...] = jnp.zeros(far_ref.shape, F32)
        far_col[...] = jnp.zeros(far_col.shape, F32)

    for s in range(slots):
        vals[s, far_rows:, :LANES] = kv_near[s][:, LANES:]
    q_aug = (q_base[...].astype(F32) + split_pieces(cum_near[...] - log_ref[...], 0, heads)).astype(
        BF
    )
    visible = near_visible(rows)
    lane = lax.broadcasted_iota(jnp.int32, (rows, LANES), 1)
    row_total = jnp.zeros((rows, LANES), F32)
    col_total = jnp.zeros((rows, LANES), F32)
    for s in range(slots):
        cols = slice(s * LANES, (s + 1) * LANES)
        kcols = slice(2 * s * LANES, (2 * s + 1) * LANES)
        vcols = slice((2 * s + 1) * LANES, (2 * s + 2) * LANES)
        gate_sig = jax.nn.sigmoid(qg[s][:, LANES:].astype(F32))
        grad = grad_ref[:, cols].astype(F32)
        att = att_ref[:, cols]
        grad_att = (grad * gate_sig).astype(BF)
        dqg_ref[:, vcols] = (grad * att * gate_sig * (1.0 - gate_sig)).astype(BF)
        weighed = grad_att.astype(F32) * att
        dq_total = jnp.zeros((rows, LANES), F32)
        dk_near = jnp.zeros((rows, LANES), F32)
        dv_near = jnp.zeros((rows, LANES), F32)
        for half in range(2):
            h = 2 * s + half
            mine = half_lanes((rows, LANES), half)
            query = jnp.where(mine, qg[s][:, :LANES] * BF(HEAD_DIM**-0.5), BF(0))
            aug = jnp.where(head_lanes(q_aug.shape, h, heads), q_aug, BF(0))
            q_cat = jnp.concatenate([query, aug], axis=1)
            ga = jnp.where(mine, grad_att, BF(0))
            delta = -jnp.sum(jnp.where(mine, weighed, 0.0), axis=1, keepdims=True)
            high = delta.astype(BF).astype(F32)
            mid = (delta - high).astype(BF).astype(F32)
            low = delta - high - mid
            d_aug = jnp.where(
                lane == 0, high, jnp.where(lane == 1, mid, jnp.where(lane == 2, low, 0.0))
            ).astype(BF)
            ga_cat = jnp.concatenate([ga, d_aug], axis=1)
            for part in range(2):
                span = slice(0, far_rows) if part == 0 else slice(far_rows, far_rows + rows)
                prob = jnp.exp(nt_dot(keys[s, span], q_cat))
                if part == 1:
                    prob = jnp.where(visible, prob, 0.0)
                ds = (prob * nt_dot(vals[s, span], ga_cat)).astype(BF)
                dv = nn_dot(prob.astype(BF), ga)
                dk = nn_dot(ds, q_cat)
                dq = tn_dot(ds, keys[s, span])
                dq_total += jnp.where(mine, dq[:, :LANES], 0.0)
                row_total += jnp.where(lane == h, dq[:, LANES:], 0.0)
                if part == 0:
                    far_ref[:, kcols] += dk[:, :LANES]
                    far_ref[:, vcols] += dv
                    far_col[...] += dk[:, LANES:]
                else:
                    dk_near += dk[:, :LANES]
                    dv_near += dv
                    col_total += dk[:, LANES:]
        dqg_ref[:, kcols] = (dq_total * HEAD_DIM**-0.5).astype(BF)
        near_ref[:, kcols] = dk_near
        near_ref[:, vcols] = dv_near
    row_ref[...] = row_total
    near_col[...] = col_total

    @pl.when(pl.program_id(0) == pl.num_programs(0) - 1)
    def _():
        far_out[...] = far_ref[...].astype(BF)


def attend_back(
    flag,
    projects,
    kv_there,
    cum_near,
    cum_far,
    q_base,
    near_base,
    far_base,
    grad,
    att,
    logs,
    rows,
    heads,
):
    total = projects[0].shape[0]
    width = heads * HEAD_DIM
    steps = total // rows
    flops = 2 * total * (total + rows) * heads * 1152
    slot_specs, slot_values = slot_inputs(flag, projects, kv_there, rows)
    return pl.pallas_call(
        functools.partial(attend_back_kernel, heads),
        grid=(steps,),
        out_shape=(
            jax.ShapeDtypeStruct((total, 2 * width), BF),
            jax.ShapeDtypeStruct((total, 2 * width), F32),
            jax.ShapeDtypeStruct((total, 2 * width), BF),
            jax.ShapeDtypeStruct((total, LANES), F32),
            jax.ShapeDtypeStruct((total, LANES), F32),
            jax.ShapeDtypeStruct((total, LANES), F32),
        ),
        in_specs=slot_specs
        + cum_specs(rows, total)
        + [row_block(rows, width), row_block(rows, width), row_block(rows, LANES)],
        out_specs=(
            row_block(rows, 2 * width),
            row_block(rows, 2 * width),
            whole_block(total, 2 * width),
            row_block(rows, LANES),
            row_block(rows, LANES),
            whole_block(total, LANES),
        ),
        scratch_shapes=[
            pltpu.VMEM((heads // 2, total + rows, 2 * LANES), BF),
            pltpu.VMEM((heads // 2, total + rows, 2 * LANES), BF),
            pltpu.VMEM((total, 2 * width), F32),
        ],
        compiler_params=pltpu.CompilerParams(vmem_limit_bytes=56 << 20),
        cost_estimate=pl.CostEstimate(
            flops=flops, bytes_accessed=total * width * 40, transcendentals=total * total * heads
        ),
    )(*slot_values, cum_near, cum_far, q_base, near_base, far_base, grad, att, logs)


def full_norm(tokens, gain_vec):
    factor = lax.rsqrt(jnp.mean(tokens * tokens, axis=-1, keepdims=True) + epsilon)
    scaled = tokens * factor
    return factor, scaled, (scaled * gain_vec).astype(BF)


def full_norm_back(grad_normed, factor, scaled, gain_vec):
    e = grad_normed * gain_vec
    mean = jnp.mean(e * scaled, axis=-1, keepdims=True)
    return jnp.sum(grad_normed * scaled, axis=0), factor * (e - scaled * mean)


MESH_ID = pl.DeviceIdType.MESH


class Here:
    def __init__(self, ring):
        self.ring = ring
        self.at = {a: lax.axis_index(a) for a in AX}

    def other(self, axis):
        return {axis: 1 - self.at[axis]}

    def peer(self, k):
        dy, dz = self.ring.offsets[k]
        return {
            "y": lax.rem(self.at["y"] + dy, 2),
            "zl": lax.rem(self.at["zl"] + dz, self.ring.zl_count),
        }

    def group_to(self, flip):
        at = self.at
        return {"y": at["zh"], "c": at["x"] ^ flip, "x": at["y"], "zh": at["c"]}

    def group_from(self, flip):
        at = self.at
        return {"y": at["x"], "c": at["zh"], "x": at["c"] ^ flip, "zh": at["y"]}

    def group_away(self):
        at = self.at
        return ~((at["y"] == at["zh"]) & (at["y"] == at["x"]) & (at["y"] == at["c"]))

    def greet_group(self, targets):
        away = self.group_away()
        self.greet(
            targets + [self.group_to(1), self.group_from(1)],
            [(self.group_to(0), away), (self.group_from(0), away)],
        )

    def greet(self, targets, extra=()):
        barrier = pltpu.get_barrier_semaphore()
        for target in targets:
            pl.semaphore_signal(barrier, inc=1, device_id=target, device_id_type=MESH_ID)
        count = len(targets)
        for target, away in extra:
            @pl.when(away)
            def _():
                pl.semaphore_signal(barrier, inc=1, device_id=target, device_id_type=MESH_ID)

            count = count + away.astype(jnp.int32)
        pl.semaphore_wait(barrier, count)


def remote(src, dst, send_sem, recv_sem, target):
    return pltpu.make_async_remote_copy(
        src_ref=src,
        dst_ref=dst,
        send_sem=send_sem,
        recv_sem=recv_sem,
        device_id=target,
        device_id_type=MESH_ID,
    )


def last_kernel(
    ring,
    heads,
    dqg_in,
    near_in,
    far_in,
    row_in,
    near_col_in,
    far_col_in,
    weight_in,
    normed_in,
    gated_in,
    mixed_in,
    tokens_in,
    residual_in,
    hid_in,
    down_in,
    gain_ref,
    forget_w,
    sig_ref,
    hot_ref,
    error_ref,
    gain_two_ref,
    valid_ref,
    back_out,
    proj_out,
    gate_out,
    up_out,
    down_out,
    out_out,
    small_out,
    grads,
    near,
    far_own,
    far_land,
    row_sum,
    near_col,
    far_col,
    far_col_land,
    cum,
    tot_send,
    tot_land,
    weight,
    normed,
    gated,
    mixed,
    tokens,
    residual,
    rs_send,
    rs_land,
    total,
    c_send,
    c_land,
    kept,
    x_send,
    x_land,
    z_send,
    z_land,
    final,
    kept_f,
    xf_send,
    xf_land,
    zf_send,
    zf_land,
    final_f,
    yf_land,
    full_f,
    co_send,
    co_land,
    kept_o,
    xo_send,
    xo_land,
    zo_send,
    zo_land,
    final_o,
    blocks,
    gain_sum,
    gain_nat,
    gain_land,
    load_sem,
    local_sem,
    swap_send_sem,
    swap_recv_sem,
    y_send_sem,
    y_recv_sem,
    c2_send_sem,
    c2_recv_sem,
    rs_send_sem,
    rs_recv_sem,
    c_send_sem,
    c_recv_sem,
    x_send_sem,
    x_recv_sem,
    z_send_sem,
    z_recv_sem,
    back_send_sem,
    back_recv_sem,
    gain_send_sem,
    gain_recv_sem,
):
    here = Here(ring)
    y, c, x, zh, zl = (here.at[a] for a in ("y", "c", "x", "zh", "zl"))
    local, features = tokens.shape
    rows_all = normed.shape[0]
    part = features // 4
    slot_w = 4 * LANES
    slots = heads // 2
    all_w = slots * slot_w
    units = down_in.shape[0]
    owner = zh == y
    peers = len(ring.offsets)
    away = here.group_away()
    all_loads = [
        (row_in, row_sum),
        (near_col_in, near_col),
        (far_col_in, far_col),
        (far_in, far_own),
        (near_in, near),
    ]
    for s in range(slots):
        all_loads.append(
            (
                dqg_in.at[:, 2 * s * LANES : 2 * (s + 1) * LANES],
                grads.at[:, s * slot_w : s * slot_w + 2 * LANES],
            )
        )
    all_loads += [
        (normed_in, normed),
        (weight_in, weight),
        (gated_in, gated),
        (mixed_in, mixed),
        (tokens_in, tokens),
        (residual_in, residual),
    ]
    loads = [
        pltpu.make_async_copy(a, b, load_sem.at[i]) for i, (a, b) in enumerate(all_loads)
    ]
    for copy in loads:
        copy.start()
    load_row, load_near_col, load_far_col, load_far, load_near = loads[:5]
    load_dqg = loads[5 : 5 + slots]
    load_normed, load_weight, load_gated, load_mixed, load_tokens, load_residual = loads[5 + slots :]

    here.greet_group(
        [here.peer(k) for k in range(1, peers)]
        + [here.other("c"), here.other("x"), here.other("zh")]
    )
    far_swap = remote(
        far_in, far_land, swap_send_sem.at[0], swap_recv_sem.at[0], here.other("c")
    )
    far_swap.start()
    col_swap = remote(
        far_col_in, far_col_land, swap_send_sem.at[1], swap_recv_sem.at[1], here.other("c")
    )
    col_swap.start()

    lane = lax.broadcasted_iota(jnp.int32, (CLEN, LANES), 1)
    head_lane = lane < heads
    all_units = rows_all // CLEN
    chunk_units = local // CLEN

    def unit_rows(u):
        return slice(u * CLEN, (u + 1) * CLEN)

    load_row.wait()
    load_near_col.wait()
    for u in range(all_units):
        value = row_sum[unit_rows(u), :] - pltpu.roll(
            near_col[unit_rows(u), :], LANES - FAR_PIECE, 1
        )
        value = jnp.where(head_lane, value, 0.0)
        cum[unit_rows(u), :] = value
        tot_send[u : u + 1, :] = jnp.sum(value, axis=0, keepdims=True)
    tot_swap = remote(
        tot_send.at[:all_units],
        tot_land.at[:all_units],
        swap_send_sem.at[2],
        swap_recv_sem.at[2],
        here.other("c"),
    )
    tot_swap.start()

    load_gated.wait()
    load_mixed.wait()
    out_rows = slots * LANES

    def out_tile(s, cols):
        return tn_dot(gated[:, s * LANES : (s + 1) * LANES], mixed[:, cols])

    for s in range(slots):
        co_send[s * LANES : (s + 1) * LANES, :] = out_tile(
            s, slice(2 * part, features)
        ).astype(BF)
    co_copy = remote(co_send, co_land, c_send_sem.at[1], c_recv_sem.at[1], here.other("c"))
    co_copy.start()

    load_far.wait()
    load_near.wait()
    for copy in load_dqg:
        copy.wait()
    far_swap.wait_recv()
    on_prompt = jnp.where(c == 0, 1.0, 0.0)

    def merge(i, carry):
        rows = pl.ds(pl.multiple_of(i * CLEN, CLEN), CLEN)
        value = near[rows, :] + on_prompt * (
            far_own[rows, :].astype(F32) + far_land[rows, :].astype(F32)
        )
        value = value.astype(BF)
        for s in range(slots):
            grads[rows, s * slot_w + 2 * LANES : (s + 1) * slot_w] = value[
                :, 2 * s * LANES : 2 * (s + 1) * LANES
            ]
        return carry

    lax.fori_loop(0, all_units, merge, 0)
    load_far_col.wait()
    col_swap.wait_recv()
    tot_swap.wait_recv()

    @pl.when(c == 0)
    def _():
        for u in range(all_units):
            both = far_col[unit_rows(u), :] + far_col_land[unit_rows(u), :]
            value = cum[unit_rows(u), :] - jnp.where(
                head_lane, pltpu.roll(both, LANES - FAR_PIECE, 1), 0.0
            )
            for j in range(all_units):
                value = value + hot_ref[unit_rows(u), j : j + 1] * tot_land[j : j + 1, :]
            cum[unit_rows(u), :] = value

    step_row = lax.broadcasted_iota(jnp.int32, (CLEN, CLEN), 0)
    step_col = lax.broadcasted_iota(jnp.int32, (CLEN, CLEN), 1)
    tri_back = (step_col >= step_row).astype(F32)
    for u in range(all_units):
        value = jnp.dot(
            tri_back,
            cum[unit_rows(u), :],
            precision=highest,
            preferred_element_type=F32,
        )
        cum[unit_rows(u), :] = value
        tot_send[all_units + u : all_units + u + 1, :] = value[0:1, :]
    places = []
    for dy, dz in ring.offsets:
        place = lax.rem(y + 2 - dy, 2) * ring.zl_count + lax.rem(
            zl + ring.zl_count - dz, ring.zl_count
        )
        for i in range(chunk_units):
            places.append(place * chunk_units + i)
    bias = jnp.zeros((1, LANES), F32)
    for u in range(all_units):
        suffix = jnp.zeros((1, LANES), F32)
        for other in range(all_units):
            if other != u:
                seen = jnp.where((places[other] > places[u]) & (c == 0), 1.0, 0.0)
                suffix = suffix + seen * tot_send[all_units + other : all_units + other + 1, :]
        value = (cum[unit_rows(u), :] + suffix) * sig_ref[unit_rows(u), :]
        grads[unit_rows(u), all_w:] = value.astype(BF)
        bias = bias + jnp.sum(value, axis=0, keepdims=True)

    load_normed.wait()
    tile_r = LANES
    per_part = part // tile_r

    def weight_tile(first, i):
        cols = pl.ds(pl.multiple_of(first + i * tile_r, LANES), tile_r)
        return tn_dot(normed[:, cols], grads[...])

    def c_step(i, carry):
        rows = pl.ds(pl.multiple_of(i * tile_r, tile_r), tile_r)
        c_send[rows, :] = weight_tile(2 * part, i).astype(BF)
        return carry

    lax.fori_loop(0, 2 * per_part, c_step, 0)
    c_copy = remote(c_send, c_land, c_send_sem.at[0], c_recv_sem.at[0], here.other("c"))
    c_copy.start()

    load_weight.wait()
    tiles = 3
    tile_w = features // tiles

    def partial_rows(chunk_no, store):
        rows = slice(chunk_no * local, (chunk_no + 1) * local)

        def step(i, carry):
            cols = pl.ds(pl.multiple_of(i * tile_w, LANES), tile_w)
            value = nn_dot(grads[rows, all_w:], forget_w[:, cols])
            for s in range(slots):
                value = value + nt_dot(
                    grads[rows, s * slot_w : (s + 1) * slot_w], weight[s, cols, :]
                )
            store(cols, value)
            return carry

        lax.fori_loop(0, tiles, step, 0)

    rs = []
    for k in range(peers - 1, 0, -1):

        def store_out(cols, value, k=k):
            rs_send[k - 1, :, cols] = value.astype(BF)

        partial_rows(ring.back[k], store_out)
        copy = remote(
            rs_send.at[k - 1],
            rs_land.at[k - 1],
            rs_send_sem.at[k - 1],
            rs_recv_sem.at[k - 1],
            here.peer(k),
        )
        copy.start()
        rs.append(copy)

    c_copy.wait_recv()

    def x_step(i, carry):
        rows = pl.ds(pl.multiple_of(i * tile_r, tile_r), tile_r)
        land = pl.ds(pl.multiple_of(part + i * tile_r, tile_r), tile_r)
        value = weight_tile(part, i) + c_land[land, :].astype(F32)
        for s in range(slots):
            x_send[s, rows, :] = value[:, s * slot_w : (s + 1) * slot_w].astype(BF)
        xf_send[rows, :] = value[:, all_w:].astype(BF)
        return carry

    lax.fori_loop(0, per_part, x_step, 0)
    x_copies = {}
    for s in (2, 1, 0):
        x_copies[s] = remote(
            x_send.at[s], x_land.at[s], x_send_sem.at[s], x_recv_sem.at[s], here.other("x")
        )
        x_copies[s].start()
    xf_copy = remote(xf_send, xf_land, x_send_sem.at[3], x_recv_sem.at[3], here.other("x"))
    xf_copy.start()
    co_copy.wait_recv()
    for s in range(slots):
        rows = slice(s * LANES, (s + 1) * LANES)
        xo_send[rows, :] = (
            out_tile(s, slice(part, 2 * part)) + co_land[rows, part:].astype(F32)
        ).astype(BF)
    xo_copy = remote(xo_send, xo_land, x_send_sem.at[4], x_recv_sem.at[4], here.other("x"))
    xo_copy.start()

    def own_step(i, carry):
        rows = pl.ds(pl.multiple_of(i * tile_r, tile_r), tile_r)
        value = weight_tile(0, i) + c_land[rows, :].astype(F32)
        for s in range(slots):
            kept[s, rows, :] = value[:, s * slot_w : (s + 1) * slot_w]
        kept_f[rows, :] = value[:, all_w:]
        return carry

    lax.fori_loop(0, per_part, own_step, 0)
    for s in range(slots):
        rows = slice(s * LANES, (s + 1) * LANES)
        kept_o[rows, :] = out_tile(s, slice(0, part)) + co_land[rows, :part].astype(F32)

    def store_own(cols, value):
        total[:, cols] = value

    partial_rows(0, store_own)

    def z_copy(i, src, dst):
        return remote(src, dst, z_send_sem.at[i], z_recv_sem.at[i], here.other("zh"))

    z_first = z_copy(0, z_send.at[0], z_land.at[0])
    z_mid = z_copy(1, z_send.at[1], z_land.at[1])
    z_forget = z_copy(2, zf_send, zf_land)
    zo_first = z_copy(3, zo_send.at[0], zo_land.at[0])
    zo_mid = z_copy(4, zo_send.at[1], zo_land.at[1])
    x_copies[2].wait_recv()
    z_send[0] = (kept[2] + x_land[2].astype(F32)).astype(BF)
    z_first.start()

    load_tokens.wait()
    load_residual.wait()
    for copy in rs:
        copy.wait_recv()
    gain_sum[...] = jnp.zeros(gain_sum.shape, F32)
    tile_n = 32

    def norm_step(i, carry):
        rows = pl.ds(pl.multiple_of(i * tile_n, tile_n), tile_n)
        tok = tokens[rows, :].astype(F32)
        grad = total[rows, :]
        for k in range(peers - 1):
            grad = grad + rs_land[k, rows, :].astype(F32)
        factor = lax.rsqrt(jnp.mean(tok * tok, axis=-1, keepdims=True) + epsilon)
        scaled_tok = tok * factor
        e = grad * gain_ref[...]
        mean = jnp.mean(e * scaled_tok, axis=-1, keepdims=True)
        out = factor * (e - scaled_tok * mean) + residual[rows, :]
        weighed = jnp.sum(grad * scaled_tok, axis=0, keepdims=True)
        for b in range(4):
            blocks[b, rows, :] = out[:, b * part : (b + 1) * part].astype(BF)
            gain_sum[b, 0:1, :] += weighed[:, b * part : (b + 1) * part]
        return carry

    lax.fori_loop(0, local // tile_n, norm_step, 0)

    def block_no(half, low_high):
        return (half ^ x) + 2 * (low_high ^ c)

    def back_copy(flip, p):
        return remote(
            blocks.at[block_no(c ^ flip, p)],
            back_out.at[c, :, p * part : (p + 1) * part],
            back_send_sem.at[flip, p],
            back_recv_sem.at[flip, p],
            here.group_from(flip),
        )

    def back_own(flip, p):
        return pltpu.make_async_copy(
            blocks.at[block_no(c ^ flip, p)],
            back_out.at[c, :, p * part : (p + 1) * part],
            local_sem.at[5 + p],
        )

    for p in range(2):
        back_copy(1, p).start()

    @pl.when(away)
    def _():
        for p in range(2):
            back_copy(0, p).start()

    @pl.when(~away)
    def _():
        for p in range(2):
            back_own(0, p).start()

    row0 = pl.multiple_of(c * part, part)

    def rows_of(ref, col, width):
        return ref.at[pl.ds(row0, part), pl.ds(pl.multiple_of(col, LANES), width)]

    def cols_of(ref, row, height):
        return ref.at[pl.ds(pl.multiple_of(row, LANES), height), pl.ds(row0, part)]

    def y_copy(i, src, dst):
        return remote(src, dst, y_send_sem.at[i], y_recv_sem.at[i], here.other("y"))

    pieces = [
        (hid_in.at[:, :units], rows_of(gate_out, y * units, units)),
        (hid_in.at[:, units:], rows_of(up_out, y * units, units)),
        (down_in, cols_of(down_out, y * units, units)),
    ]
    own_pieces = [
        pltpu.make_async_copy(src, dst, local_sem.at[i]) for i, (src, dst) in enumerate(pieces)
    ]
    y_pieces = [y_copy(i, src, dst) for i, (src, dst) in enumerate(pieces)]
    for copy in own_pieces + y_pieces:
        copy.start()

    x_copies[1].wait_recv()

    @pl.when(~owner)
    def _():
        z_send[1] = (kept[1] + x_land[1].astype(F32)).astype(BF)
        z_mid.start()

    x_copies[0].wait_recv()
    kept[0] += x_land[0].astype(F32)
    xf_copy.wait_recv()
    kept_f[...] += xf_land[...].astype(F32)
    zf_send[...] = kept_f[...].astype(BF)
    z_forget.start()
    xo_copy.wait_recv()
    kept_o[...] += xo_land[...].astype(F32)
    zo_send[0] = kept_o[2 * LANES :, :].astype(BF)
    zo_first.start()

    @pl.when(~owner)
    def _():
        zo_send[1] = kept_o[LANES : 2 * LANES, :].astype(BF)
        zo_mid.start()

    first_dst = rows_of(proj_out, 2 * y * slot_w, slot_w)
    mid_dst = rows_of(proj_out, slot_w, slot_w)
    out_first_dst = cols_of(out_out, 2 * LANES * y, LANES)
    out_mid_dst = cols_of(out_out, LANES, LANES)
    y_first = y_copy(3, final.at[0], first_dst)
    y_mid = y_copy(4, final.at[1], mid_dst)
    y_forget = y_copy(5, final_f, yf_land)
    yo_first = y_copy(6, final_o.at[0], out_first_dst)
    yo_mid = y_copy(7, final_o.at[1], out_mid_dst)
    own_first = pltpu.make_async_copy(final.at[0], first_dst, local_sem.at[8])
    own_mid = pltpu.make_async_copy(final.at[1], mid_dst, local_sem.at[9])
    own_out_first = pltpu.make_async_copy(final_o.at[0], out_first_dst, local_sem.at[10])
    own_out_mid = pltpu.make_async_copy(final_o.at[1], out_mid_dst, local_sem.at[11])
    own_forget = pltpu.make_async_copy(
        full_f, proj_out.at[pl.ds(row0, part), all_w : all_w + LANES], local_sem.at[12]
    )
    z_first.wait_recv()
    final[0] = (kept[0] + z_land[0].astype(F32)).astype(BF)
    y_first.start()
    own_first.start()

    @pl.when(owner)
    def _():
        z_mid.wait_recv()
        final[1] = (kept[1] + x_land[1].astype(F32) + z_land[1].astype(F32)).astype(BF)
        y_mid.start()
        own_mid.start()

    z_forget.wait_recv()
    f_lane = lax.broadcasted_iota(jnp.int32, (part, LANES), 1)
    there_f = zf_land[...].astype(F32)
    edge = jnp.where(f_lane < 2, kept_f[...] + pltpu.roll(there_f, LANES - 4, 1), 0.0)
    edge = jnp.where(y == 0, edge, pltpu.roll(edge, 4, 1))
    mid_f = jnp.where((f_lane >= 2) & (f_lane < 4) & owner, kept_f[...] + there_f, 0.0)
    final_f[...] = (edge + mid_f).astype(BF)
    y_forget.start()
    zo_first.wait_recv()
    final_o[0] = (kept_o[:LANES, :] + zo_land[0].astype(F32)).astype(BF)
    yo_first.start()
    own_out_first.start()

    @pl.when(owner)
    def _():
        zo_mid.wait_recv()
        final_o[1] = (kept_o[LANES : 2 * LANES, :] + zo_land[1].astype(F32)).astype(BF)
        yo_mid.start()
        own_out_mid.start()

    for copy in own_pieces:
        copy.wait()
    for copy in y_pieces:
        copy.wait_recv()
    c2 = []

    def hand_over(i, view):
        copy = remote(view, view, c2_send_sem.at[i], c2_recv_sem.at[i], here.other("c"))
        copy.start()
        c2.append(copy)

    hand_over(0, gate_out.at[pl.ds(row0, part), :])
    hand_over(1, up_out.at[pl.ds(row0, part), :])
    hand_over(2, down_out.at[:, pl.ds(row0, part)])

    for b in range(4):
        gain_sum[b, 1:2, :] = gain_two_ref[0:1, b * part : (b + 1) * part]
    for b in range(4):
        gain_nat[0, b] = gain_sum[block_no(b // 2, b % 2)]
    wide_lane = lax.broadcasted_iota(jnp.int32, (1, part), 1)
    scalars = jnp.where(
        wide_lane == 0, jnp.sum(error_ref[0:1, :], axis=1, keepdims=True), 0.0
    ) + jnp.where(wide_lane == 1, jnp.sum(valid_ref[...], axis=0, keepdims=True), 0.0)
    small_lane = lax.broadcasted_iota(jnp.int32, (1, LANES), 1)
    for j in range(heads):
        if j < 2:
            quarter, head = zh, 4 * y + j
        elif j < 4:
            quarter, head = y, j
        else:
            quarter, head = 1 - zh, 4 * y + j - 4
        dest = 2 + (quarter * ring.zl_count + zl) * heads + head
        value = jnp.sum(jnp.where(small_lane == j, bias, 0.0), axis=1, keepdims=True)
        scalars = scalars + jnp.where(wide_lane == dest, value, 0.0)
    gain_nat[0, 0, 2:3, :] = scalars
    for place, axis in enumerate(("c", "y", "x", "zl", "zh")):
        copy = remote(
            gain_nat.at[place],
            gain_land.at[place],
            gain_send_sem.at[place],
            gain_recv_sem.at[place],
            here.other(axis),
        )
        copy.start()
        copy.wait_recv()
        gain_nat[place + 1] = gain_nat[place] + gain_land[place]
        copy.wait_send()
    gain_copy = pltpu.make_async_copy(gain_nat.at[5], small_out, local_sem.at[7])
    gain_copy.start()

    y_forget.wait_recv()
    full_f[...] = final_f[...] + yf_land[...]
    own_forget.start()
    own_first.wait()
    y_first.wait_recv()
    own_out_first.wait()
    yo_first.wait_recv()
    own_forget.wait()

    @pl.when(owner)
    def _():
        own_mid.wait()
        own_out_mid.wait()

    @pl.when(~owner)
    def _():
        y_mid.wait_recv()
        yo_mid.wait_recv()

    hand_over(3, out_out.at[:, pl.ds(row0, part)])
    hand_over(4, proj_out.at[pl.ds(row0, part), :])

    for copy in c2:
        copy.wait()
    for p in range(2):
        back_copy(1, p).wait()

    @pl.when(away)
    def _():
        for p in range(2):
            back_copy(0, p).wait()

    @pl.when(~away)
    def _():
        for p in range(2):
            back_own(0, p).wait()

    gain_copy.wait()
    for copy in rs + [c_copy, co_copy, x_copies[0], x_copies[1], x_copies[2], xf_copy, xo_copy]:
        copy.wait_send()
    for copy in [far_swap, col_swap, tot_swap, z_first, z_forget, zo_first]:
        copy.wait_send()
    for copy in y_pieces + [y_first, y_forget, yo_first]:
        copy.wait_send()

    @pl.when(owner)
    def _():
        y_mid.wait_send()
        yo_mid.wait_send()

    @pl.when(~owner)
    def _():
        z_mid.wait_send()
        zo_mid.wait_send()


def last_step(ring, heads, large, small):
    near = large[1]
    rows = near.shape[0]
    weight, normed, gated = large[6:9]
    tokens = large[10]
    units = large[13].shape[0]
    local, features = tokens.shape
    part = features // 4
    half = features // 2
    peers = len(ring.offsets)
    slot_w = 4 * LANES
    slots = heads // 2
    all_w = slots * slot_w
    any_spec = pl.BlockSpec(memory_space=pl.ANY)
    dma = pltpu.SemaphoreType.DMA
    vmem = pltpu.VMEM
    return pl.pallas_call(
        functools.partial(last_kernel, ring, heads),
        out_shape=(
            jax.ShapeDtypeStruct((2, local, half), BF),
            jax.ShapeDtypeStruct((half, all_w + LANES), BF),
            jax.ShapeDtypeStruct((half, 2 * units), BF),
            jax.ShapeDtypeStruct((half, 2 * units), BF),
            jax.ShapeDtypeStruct((2 * units, half), BF),
            jax.ShapeDtypeStruct((slots * LANES, half), BF),
            jax.ShapeDtypeStruct((4, 8, part), F32),
        ),
        in_specs=[any_spec] * len(large) + [pl.BlockSpec(memory_space=vmem)] * len(small),
        out_specs=[any_spec] * 7,
        scratch_shapes=[
            vmem((rows, all_w + LANES), BF),
            vmem(near.shape, F32),
            vmem(near.shape, BF),
            vmem(near.shape, BF),
            vmem((rows, LANES), F32),
            vmem((rows, LANES), F32),
            vmem((rows, LANES), F32),
            vmem((rows, LANES), F32),
            vmem((rows, LANES), F32),
            vmem((2 * (rows // CLEN), LANES), F32),
            vmem((2 * (rows // CLEN), LANES), F32),
            vmem(weight.shape, BF),
            vmem(normed.shape, BF),
            vmem(gated.shape, BF),
            vmem(normed.shape, BF),
            vmem(tokens.shape, BF),
            vmem(tokens.shape, F32),
            vmem((peers - 1, local, features), BF),
            vmem((peers - 1, local, features), BF),
            vmem((local, features), F32),
            vmem((half, all_w + LANES), BF),
            vmem((half, all_w + LANES), BF),
            vmem((slots, part, slot_w), F32),
            vmem((slots, part, slot_w), BF),
            vmem((slots, part, slot_w), BF),
            vmem((2, part, slot_w), BF),
            vmem((2, part, slot_w), BF),
            vmem((2, part, slot_w), BF),
            vmem((part, LANES), F32),
            vmem((part, LANES), BF),
            vmem((part, LANES), BF),
            vmem((part, LANES), BF),
            vmem((part, LANES), BF),
            vmem((part, LANES), BF),
            vmem((part, LANES), BF),
            vmem((part, LANES), BF),
            vmem((slots * LANES, half), BF),
            vmem((slots * LANES, half), BF),
            vmem((slots * LANES, part), F32),
            vmem((slots * LANES, part), BF),
            vmem((slots * LANES, part), BF),
            vmem((2, LANES, part), BF),
            vmem((2, LANES, part), BF),
            vmem((2, LANES, part), BF),
            vmem((4, local, part), BF),
            vmem((4, 8, part), F32),
            vmem((6, 4, 8, part), F32),
            vmem((5, 4, 8, part), F32),
            dma((11 + slots,)),
            dma((13,)),
            dma((3,)),
            dma((3,)),
            dma((8,)),
            dma((8,)),
            dma((5,)),
            dma((5,)),
            dma((peers - 1,)),
            dma((peers - 1,)),
            dma((2,)),
            dma((2,)),
            dma((5,)),
            dma((5,)),
            dma((5,)),
            dma((5,)),
            dma((2, 2)),
            dma((2, 2)),
            dma((5,)),
            dma((5,)),
        ],
        compiler_params=pltpu.CompilerParams(
            collective_id=1, has_side_effects=True, vmem_limit_bytes=63 << 20
        ),
        cost_estimate=pl.CostEstimate(
            flops=4 * rows * features * all_w, bytes_accessed=40 << 20, transcendentals=0
        ),
    )(*large, *small)


def middle_kernel(
    ring,
    gated_in,
    w_out_in,
    hid_own_in,
    hid_there_in,
    w_down_in,
    tokens_in,
    teach_prompt_in,
    teach_cont_in,
    valid_ref,
    gain_ref,
    gated_grad,
    residual_grad,
    mixed_grads,
    hid_kept,
    hid_there,
    down_kept,
    down_there,
    error_ref,
    gain_grad,
    gated,
    w_out,
    w_hidden,
    w_down,
    tokens,
    teacher,
    mixed,
    total,
    result_grad,
    normed,
    hidden,
    gate_up,
    result_all,
    mixed_all,
    rs_send,
    rs_land,
    c_down_send,
    c_down_land,
    c_hid_send,
    c_hid_land,
    x_down_send,
    x_hid_send,
    down_sum,
    hid_sum,
    gg_stage,
    load_sem,
    wx_send,
    wx_recv,
    wc_send,
    wc_recv,
    wz_send,
    wz_recv,
    group_send,
    group_recv,
    out_sem,
    rs_send_sem,
    rs_recv_sem,
    ag_send_sem,
    ag_recv_sem,
    c_send_sem,
    c_recv_sem,
    x_send_sem,
    x_recv_sem,
):
    here = Here(ring)
    local, features = tokens.shape
    rows_all = gated.shape[0]
    width = gated.shape[1]
    units = hidden.shape[1]
    half_units = units // 2
    part = features // 4
    peers = len(ring.offsets)
    order = list(range(peers - 1, 0, -1))
    y, c, x = (here.at[a] for a in ("y", "c", "x"))
    down_view = w_down_in.at[
        pl.ds(pl.multiple_of(y * half_units, half_units), half_units),
        pl.ds(pl.multiple_of(c * part, part), part),
    ]

    loads = [
        pltpu.make_async_copy(a, b, load_sem.at[i])
        for i, (a, b) in enumerate(
            (
                (hid_own_in, w_hidden.at[0:part, 0:units]),
                (hid_there_in, w_hidden.at[0:part, units:]),
                (gated_in, gated),
                (w_out_in, w_out),
                (tokens_in, tokens),
                (down_view, w_down.at[0:half_units, 0:part]),
            )
        )
    ]
    for copy in loads:
        copy.start()
    here.greet_group(
        [here.peer(k) for k in range(1, peers)]
        + [here.other("c"), here.other("x"), here.other("zh")]
    )

    z_down = remote(
        down_view, w_down.at[half_units:, 0:part], wz_send, wz_recv, here.other("zh")
    )
    z_down.start()

    def hid_x_copy(i):
        cols = slice(i * units, (i + 1) * units)
        return remote(
            w_hidden.at[0:part, cols],
            w_hidden.at[part : 2 * part, cols],
            wx_send.at[i],
            wx_recv.at[i],
            here.other("x"),
        )

    def hid_c_copy(i):
        cols = slice(i * units, (i + 1) * units)
        return remote(
            w_hidden.at[0 : 2 * part, cols],
            w_hidden.at[2 * part :, cols],
            wc_send.at[i],
            wc_recv.at[i],
            here.other("c"),
        )

    for i in range(2):
        loads[i].wait()
        hid_x_copy(i).start()

    def teach_copies(flip, rows_in, remote_copy):
        kind = x ^ flip
        out = []
        for p in range(2):
            block = (x ^ y) + 2 * (kind ^ p)
            dst = teacher.at[:, pl.ds(pl.multiple_of(block * part, part), part)]
            src = rows_in.at[:, p * part : (p + 1) * part]
            if remote_copy:
                out.append(
                    remote(
                        src, dst, group_send.at[flip, p], group_recv.at[flip, p], here.group_to(flip)
                    )
                )
            else:
                out.append(pltpu.make_async_copy(src, dst, load_sem.at[6 + p]))
        return out

    away = here.group_away()

    def on_teacher(flip, here_too, what):
        for kind, rows_in in ((0, teach_prompt_in), (1, teach_cont_in)):
            mine = (x ^ flip) == kind
            if flip == 1:

                @pl.when(mine)
                def _():
                    for copy in teach_copies(1, rows_in, True):
                        what(copy)

            else:

                @pl.when(mine & away)
                def _():
                    for copy in teach_copies(0, rows_in, True):
                        what(copy)

                if here_too:

                    @pl.when(mine & ~away)
                    def _():
                        for copy in teach_copies(0, rows_in, False):
                            what(copy)

    def teacher_arrival(flip):
        for p in range(2):
            remote(
                teach_prompt_in.at[:, p * part : (p + 1) * part],
                teacher.at[:, p * part : (p + 1) * part],
                group_send.at[flip, p],
                group_recv.at[flip, p],
                here.group_to(flip),
            ).wait_recv()

    def chunk(k):
        return slice(k * local, (k + 1) * local)

    def tiled(count, size, step):
        def body(i, carry):
            step(pl.ds(pl.multiple_of(i * size, size), size))
            return carry

        lax.fori_loop(0, count, body, 0)

    def rs_copy(phase, j):
        return remote(
            rs_send.at[j - 1],
            rs_land.at[j - 1],
            rs_send_sem.at[phase, j - 1],
            rs_recv_sem.at[phase, j - 1],
            here.peer(j),
        )

    def ag_copy(phase, buffer, k):
        return remote(
            buffer.at[chunk(0)],
            buffer.at[chunk(k)],
            ag_send_sem.at[phase, k - 1],
            ag_recv_sem.at[phase, k - 1],
            here.peer(k),
        )

    wide = 512
    wide_count = features // wide

    def send_partial(phase, k, left, right, transposed):
        def step(cols):
            if transposed:
                value = nt_dot(left, right[cols, :])
            else:
                value = nn_dot(left, right[:, cols])
            if k == 0:
                total[:, cols] = value
            else:
                rs_send[ring.back[k] - 1, :, cols] = value.astype(BF)

        if k != 0 and phase > 0:
            rs_copy(phase - 1, ring.back[k]).wait_send()
        tiled(wide_count, wide, step)
        if k != 0:
            rs_copy(phase, ring.back[k]).start()

    def row_tiles(step):
        tiled(local // 32, 32, step)

    def summed(rows):
        value = total[rows, :]
        for j in range(1, peers):
            value = value + rs_land[j - 1, rows, :].astype(F32)
        return value

    loads[2].wait()
    loads[3].wait()
    for k in order + [0]:
        send_partial(0, k, gated[chunk(k), :], w_out, False)
    loads[4].wait()
    loads[5].wait()
    z_down.wait_recv()
    down_x_copy = remote(
        w_down.at[:, 0:part],
        w_down.at[:, part : 2 * part],
        wx_send.at[2],
        wx_recv.at[2],
        here.other("x"),
    )
    down_x_copy.start()
    for j in range(1, peers):
        rs_copy(0, j).wait_recv()

    def second_norm(rows):
        value = tokens[rows, :].astype(F32) + summed(rows)
        mixed[rows, :] = value
        factor = lax.rsqrt(jnp.mean(value * value, axis=-1, keepdims=True) + epsilon)
        normed[rows, :] = (value * factor * gain_ref[...]).astype(BF)

    row_tiles(second_norm)
    for k in order:
        ag_copy(0, normed, k).start()

    for i in range(2):
        hid_x_copy(i).wait_recv()
        hid_c_copy(i).start()
    for f in range(2):
        on_teacher(f, True, lambda copy: copy.start())
    for i in range(2):
        hid_c_copy(i).wait_recv()
    down_x_copy.wait_recv()
    down_c_copy = remote(
        w_down.at[:, 0 : 2 * part],
        w_down.at[:, 2 * part :],
        wc_send.at[2],
        wc_recv.at[2],
        here.other("c"),
    )
    down_c_copy.start()
    tile_u = 256
    per_half = half_units // tile_u

    def forward_chunk(k):
        left = normed[chunk(k), :]

        def step(i, carry):
            half = i // per_half
            sub = lax.rem(i, per_half)
            gate_at = pl.multiple_of(half * units + sub * tile_u, tile_u)
            up_at = pl.multiple_of(half * units + half_units + sub * tile_u, tile_u)
            gate = nn_dot(left, w_hidden[:, pl.ds(gate_at, tile_u)])
            up = nn_dot(left, w_hidden[:, pl.ds(up_at, tile_u)])
            gate_up[chunk(k), pl.ds(gate_at, tile_u)] = gate.astype(BF)
            gate_up[chunk(k), pl.ds(up_at, tile_u)] = up.astype(BF)
            hidden[chunk(k), pl.ds(pl.multiple_of(i * tile_u, tile_u), tile_u)] = (
                gate * jax.nn.sigmoid(gate) * up
            ).astype(BF)
            return carry

        lax.fori_loop(0, 2 * per_half, step, 0)
        if k == 0:
            down_c_copy.wait_recv()
        send_partial(1, k, hidden[chunk(k), :], w_down, False)

    forward_chunk(0)
    for k in range(1, peers):
        ag_copy(0, normed, k).wait_recv()
        forward_chunk(k)
    teacher_arrival(1)

    @pl.when(away)
    def _():
        teacher_arrival(0)

    @pl.when(~away)
    def _():
        for kind, rows_in in ((0, teach_prompt_in), (1, teach_cont_in)):

            @pl.when(x == kind)
            def _():
                for copy in teach_copies(0, rows_in, False):
                    copy.wait()

    for j in range(1, peers):
        rs_copy(1, j).wait_recv()
    error_ref[...] = jnp.zeros(error_ref.shape, F32)
    gain_grad[...] = jnp.zeros(gain_grad.shape, F32)

    def loss_rows(rows):
        deviation = mixed[rows, :] + summed(rows) - teacher[rows, :].astype(F32)
        grad = valid_ref[rows, :] * deviation
        result_grad[rows, :] = grad
        result_all[rows, :] = grad.astype(BF)
        error_ref[0:1, :] += 0.5 * jnp.sum(grad * deviation, axis=0, keepdims=True)

    row_tiles(loss_rows)
    for k in order:
        ag_copy(1, result_all, k).start()

    def backward_chunk(k):
        left = result_all[chunk(k), :]

        def step(i, carry):
            half = i // per_half
            sub = lax.rem(i, per_half)
            gate_at = pl.multiple_of(half * units + sub * tile_u, tile_u)
            up_at = pl.multiple_of(half * units + half_units + sub * tile_u, tile_u)
            grad = nt_dot(left, w_down[pl.ds(pl.multiple_of(i * tile_u, tile_u), tile_u), :])
            gate = gate_up[chunk(k), pl.ds(gate_at, tile_u)].astype(F32)
            up = gate_up[chunk(k), pl.ds(up_at, tile_u)].astype(F32)
            sig = jax.nn.sigmoid(gate)
            gate_up[chunk(k), pl.ds(gate_at, tile_u)] = (
                grad * up * sig * (1.0 + gate * (1.0 - sig))
            ).astype(BF)
            gate_up[chunk(k), pl.ds(up_at, tile_u)] = (grad * gate * sig).astype(BF)
            return carry

        lax.fori_loop(0, 2 * per_half, step, 0)
        send_partial(2, k, gate_up[chunk(k), :], w_hidden, True)

    backward_chunk(0)
    for k in range(1, peers):
        ag_copy(1, result_all, k).wait_recv()
        backward_chunk(k)

    unit_tile = 256

    def down_tile(units_at, cols):
        return tn_dot(hidden[:, units_at], result_all[:, cols])

    def down_c(units_at):
        c_down_send[units_at, :] = down_tile(units_at, slice(2 * part, features)).astype(BF)

    tiled(units // unit_tile, unit_tile, down_c)
    c_down = remote(c_down_send, c_down_land, c_send_sem.at[0], c_recv_sem.at[0], here.other("c"))
    c_down.start()
    feature_tile = 128

    def hid_tile(first, at):
        cols = pl.ds(pl.multiple_of(first + at.start, feature_tile), feature_tile)
        return tn_dot(normed[:, cols], gate_up[...])

    def hid_c(at):
        c_hid_send[at, :] = hid_tile(2 * part, at).astype(BF)

    tiled(2 * part // feature_tile, feature_tile, hid_c)
    c_hid = remote(c_hid_send, c_hid_land, c_send_sem.at[1], c_recv_sem.at[1], here.other("c"))
    c_hid.start()
    c_down.wait_recv()

    def down_x(units_at):
        value = down_tile(units_at, slice(part, 2 * part))
        x_down_send[units_at, :] = (value + c_down_land[units_at, part:].astype(F32)).astype(BF)

    tiled(units // unit_tile, unit_tile, down_x)
    x_down = remote(x_down_send, down_there, x_send_sem.at[0], x_recv_sem.at[0], here.other("x"))
    x_down.start()

    for j in range(1, peers):
        rs_copy(2, j).wait_recv()

    def norm_back(rows):
        value = mixed[rows, :]
        factor = lax.rsqrt(jnp.mean(value * value, axis=-1, keepdims=True) + epsilon)
        scaled_rows = value * factor
        grad = summed(rows)
        e = grad * gain_ref[...]
        mean = jnp.mean(e * scaled_rows, axis=-1, keepdims=True)
        out = result_grad[rows, :] + factor * (e - scaled_rows * mean)
        result_grad[rows, :] = out
        mixed_all[rows, :] = out.astype(BF)
        gain_grad[0:1, :] += jnp.sum(grad * scaled_rows, axis=0, keepdims=True)

    row_tiles(norm_back)
    for k in order:
        ag_copy(2, mixed_all, k).start()
    residual_copy = pltpu.make_async_copy(result_grad, residual_grad, out_sem.at[0])
    residual_copy.start()

    c_hid.wait_recv()

    def hid_x(at):
        land = pl.ds(pl.multiple_of(part + at.start, feature_tile), feature_tile)
        x_hid_send[at, :] = (hid_tile(part, at) + c_hid_land[land, :].astype(F32)).astype(BF)

    tiled(part // feature_tile, feature_tile, hid_x)
    x_hid = remote(x_hid_send, hid_there, x_send_sem.at[1], x_recv_sem.at[1], here.other("x"))
    x_hid.start()

    def gated_chunk(k):
        gg_stage[chunk(k), :] = nt_dot(mixed_all[chunk(k), :], w_out[...])

    gated_chunk(0)

    def down_own(units_at):
        value = down_tile(units_at, slice(0, part))
        down_sum[units_at, :] = value + c_down_land[units_at, :part].astype(F32)

    tiled(units // unit_tile, unit_tile, down_own)

    def hid_own(at):
        hid_sum[at, :] = hid_tile(0, at) + c_hid_land[at, :].astype(F32)

    tiled(part // feature_tile, feature_tile, hid_own)
    sums_out = [
        pltpu.make_async_copy(down_sum, down_kept, out_sem.at[1]),
        pltpu.make_async_copy(hid_sum, hid_kept, out_sem.at[2]),
    ]
    for copy in sums_out:
        copy.start()
    for k in range(1, peers):
        ag_copy(2, mixed_all, k).wait_recv()
        gated_chunk(k)
    finals = [
        pltpu.make_async_copy(gg_stage, gated_grad, out_sem.at[3]),
        pltpu.make_async_copy(mixed_all, mixed_grads, out_sem.at[4]),
    ]
    for copy in finals:
        copy.start()
    for k in range(1, peers):
        rs_copy(2, k).wait_send()
        for phase, buffer in enumerate((normed, result_all, mixed_all)):
            ag_copy(phase, buffer, k).wait_send()
    c_down.wait_send()
    c_hid.wait_send()
    z_down.wait_send()
    for i in range(2):
        hid_x_copy(i).wait_send()
        hid_c_copy(i).wait_send()
        on_teacher(i, False, lambda copy: copy.wait_send())
    down_x_copy.wait_send()
    down_c_copy.wait_send()
    x_down.wait()
    x_hid.wait()
    residual_copy.wait()
    for copy in sums_out + finals:
        copy.wait()


def middle_step(
    ring,
    gated,
    w_out,
    hid_own,
    hid_there,
    w_down,
    tokens,
    teach_prompt,
    teach_cont,
    valid,
    gain,
):
    rows, width = gated.shape
    local, features = tokens.shape
    units = w_down.shape[0]
    part = features // 4
    peers = len(ring.offsets)
    any_spec = pl.BlockSpec(memory_space=pl.ANY)
    vmem_spec = pl.BlockSpec(memory_space=pltpu.VMEM)
    dma = pltpu.SemaphoreType.DMA
    return pl.pallas_call(
        functools.partial(middle_kernel, ring),
        out_shape=(
            jax.ShapeDtypeStruct((rows, width), F32),
            jax.ShapeDtypeStruct((local, features), F32),
            jax.ShapeDtypeStruct((rows, features), BF),
            jax.ShapeDtypeStruct((part, 2 * units), F32),
            jax.ShapeDtypeStruct((part, 2 * units), BF),
            jax.ShapeDtypeStruct((units, part), F32),
            jax.ShapeDtypeStruct((units, part), BF),
            jax.ShapeDtypeStruct((8, features), F32),
            jax.ShapeDtypeStruct((8, features), F32),
        ),
        in_specs=[any_spec] * 8 + [vmem_spec] * 2,
        out_specs=[any_spec] * 7 + [vmem_spec] * 2,
        scratch_shapes=[
            pltpu.VMEM(gated.shape, BF),
            pltpu.VMEM(w_out.shape, BF),
            pltpu.VMEM((features, 2 * units), BF),
            pltpu.VMEM((units, features), BF),
            pltpu.VMEM(tokens.shape, BF),
            pltpu.VMEM(tokens.shape, BF),
            pltpu.VMEM(tokens.shape, F32),
            pltpu.VMEM(tokens.shape, F32),
            pltpu.VMEM(tokens.shape, F32),
            pltpu.VMEM((rows, features), BF),
            pltpu.VMEM((rows, units), BF),
            pltpu.VMEM((rows, 2 * units), BF),
            pltpu.VMEM((rows, features), BF),
            pltpu.VMEM((rows, features), BF),
            pltpu.VMEM((peers - 1, local, features), BF),
            pltpu.VMEM((peers - 1, local, features), BF),
            pltpu.VMEM((units, 2 * part), BF),
            pltpu.VMEM((units, 2 * part), BF),
            pltpu.VMEM((2 * part, 2 * units), BF),
            pltpu.VMEM((2 * part, 2 * units), BF),
            pltpu.VMEM((units, part), BF),
            pltpu.VMEM((part, 2 * units), BF),
            pltpu.VMEM((units, part), F32),
            pltpu.VMEM((part, 2 * units), F32),
            pltpu.VMEM((rows, width), F32),
            dma((8,)),
            dma((3,)),
            dma((3,)),
            dma((3,)),
            dma((3,)),
            dma,
            dma,
            dma((2, 2)),
            dma((2, 2)),
            dma((5,)),
            dma((3, peers - 1)),
            dma((3, peers - 1)),
            dma((3, peers - 1)),
            dma((3, peers - 1)),
            dma((2,)),
            dma((2,)),
            dma((2,)),
            dma((2,)),
        ],
        compiler_params=pltpu.CompilerParams(
            collective_id=2, has_side_effects=True, vmem_limit_bytes=63 << 20
        ),
        cost_estimate=pl.CostEstimate(
            flops=6 * rows * features * (3 * units + width),
            bytes_accessed=60 << 20,
            transcendentals=0,
        ),
    )(
        gated,
        w_out,
        hid_own,
        hid_there,
        w_down,
        tokens,
        teach_prompt,
        teach_cont,
        valid,
        gain,
    )


def first_kernel(
    ring,
    prompt_in,
    cont_in,
    small_in,
    ints_in,
    wq_in,
    wg_in,
    wk_in,
    wv_in,
    w_out_in,
    tokens_out,
    normed_out,
    slots_out,
    w_out_all,
    small_out,
    gains_out,
    forget_w_out,
    ints_out,
    proj_a,
    proj_b,
    proj_c,
    forget_own,
    there_a,
    there_b,
    there_c,
    forget_there,
    tokens,
    normed,
    slot_w,
    project,
    forget,
    small,
    small_x,
    feats,
    forget_f,
    forget_w,
    group_send,
    group_recv,
    ints_send,
    ints_recv,
    small_send,
    small_recv,
    own_sem,
    z_send,
    z_recv,
    x_send,
    x_recv,
    c_send,
    c_recv,
    ag_send,
    ag_recv,
    kv_send,
    kv_recv,
    out_sem,
):
    here = Here(ring)
    y, c, x, zh = (here.at[a] for a in ("y", "c", "x", "zh"))
    local, features = tokens.shape
    part = features // 4
    half = features // 2
    peers = len(ring.offsets)
    owner = zh == y
    row0 = pl.multiple_of(c * part, part)
    first0 = pl.multiple_of(2 * LANES * y, LANES)
    sources = (wq_in, wg_in, wk_in, wv_in)

    here.greet_group([here.peer(k) for k in range(1, peers)] + [here.other(a) for a in "cx"] + [here.other("zh")])

    def group_copies(flip, rows_in, remote_copy):
        kind = x ^ flip
        out = []
        for p in range(2):
            block = (x ^ y) + 2 * (kind ^ p)
            dst = tokens.at[:, pl.ds(pl.multiple_of(block * part, part), part)]
            src = rows_in.at[:, p * part : (p + 1) * part]
            if remote_copy:
                out.append(
                    remote(
                        src, dst, group_send.at[flip, p], group_recv.at[flip, p], here.group_to(flip)
                    )
                )
            else:
                out.append(pltpu.make_async_copy(src, dst, own_sem.at[12 + p]))
        return out

    def ints_copy():
        return remote(ints_in, ints_out, ints_send, ints_recv, here.group_to(0))

    def ints_own():
        return pltpu.make_async_copy(ints_in, ints_out, own_sem.at[14])

    away = here.group_away()

    def on_group(flip, what):
        for kind, rows_in in ((0, prompt_in), (1, cont_in)):
            mine = (x ^ flip) == kind
            if flip == 1:

                @pl.when(mine)
                def _():
                    for copy in group_copies(flip, rows_in, True):
                        what(copy)

            else:

                @pl.when(mine & away)
                def _():
                    for copy in group_copies(flip, rows_in, True):
                        what(copy)

                @pl.when(mine & ~away)
                def _():
                    for copy in group_copies(flip, rows_in, False):
                        what(copy)

    for f in range(2):
        on_group(f, lambda copy: copy.start())

    @pl.when(away)
    def _():
        ints_copy().start()

    @pl.when(~away)
    def _():
        ints_own().start()

    own_small = pltpu.make_async_copy(small_in, small.at[0], own_sem.at[15])
    own_small.start()
    small_z = remote(small_in, small.at[1], small_send.at[0], small_recv.at[0], here.other("zh"))
    small_z.start()

    def own_piece(i, s):
        start = first0 if s == 0 else LANES
        return pltpu.make_async_copy(
            sources[i].at[pl.ds(row0, part), pl.ds(start, LANES)],
            slot_w.at[s, 0:part, i * LANES : (i + 1) * LANES],
            own_sem.at[4 * s + i],
        )

    for i in range(4):
        own_piece(i, 0).start()

    @pl.when(owner)
    def _():
        for i in range(4):
            own_piece(i, 1).start()

    own_out = [
        pltpu.make_async_copy(
            w_out_in.at[pl.ds(first0, LANES), pl.ds(row0, part)],
            w_out_all.at[0:LANES, 0:part],
            own_sem.at[8],
        ),
        pltpu.make_async_copy(
            w_out_in.at[LANES : 2 * LANES, pl.ds(row0, part)],
            w_out_all.at[LANES : 2 * LANES, 0:part],
            own_sem.at[9],
        ),
    ]
    own_out[0].start()

    @pl.when(owner)
    def _():
        own_out[1].start()

    own_small.wait()
    small_z.wait_recv()
    small_over_x = remote(small, small_x, small_send.at[1], small_recv.at[1], here.other("x"))
    small_over_x.start()

    def x_copy(s):
        return remote(
            slot_w.at[s, 0:part],
            slot_w.at[s, part : 2 * part],
            x_send.at[s],
            x_recv.at[s],
            here.other("x"),
        )

    def c_copy(s):
        return remote(
            slot_w.at[s, 0:half],
            slot_w.at[s, half:features],
            c_send.at[s],
            c_recv.at[s],
            here.other("c"),
        )

    for i in range(4):
        own_piece(i, 0).wait()
    x_copy(0).start()
    small_over_x.wait_recv()
    for z in range(2):
        for place in range(2):
            at = pl.multiple_of((c ^ place) * part, part)
            feats[z, :, 2 * place * part : (2 * place + 1) * part] = small[z, :, pl.ds(at, part)]
            feats[z, :, (2 * place + 1) * part : (2 * place + 2) * part] = small_x[
                z, :, pl.ds(at, part)
            ]
    forget_f[...] = jnp.zeros(forget_f.shape, F32)
    for z, rows in ((0, slice(0, 2)), (1, slice(4, 6))):
        forget_f[rows, :] = jnp.where(y == 0, feats[z, 8:10, :], feats[z, 12:14, :])
    forget_f[2:4, :] = jnp.where(owner, feats[0, 10:12, :], feats[1, 10:12, :])
    forget_w[...] = jnp.zeros(forget_w.shape, BF)
    forget_w[0:16, :] = forget_f[...].astype(BF)

    for f in range(2):
        for p in range(2):
            pass

    def arrived(copy):
        if hasattr(copy, "wait_recv"):
            copy.wait_recv()

    def group_arrival(flip):
        for p in range(2):
            remote(
                prompt_in.at[:, p * part : (p + 1) * part],
                tokens.at[:, p * part : (p + 1) * part],
                group_send.at[flip, p],
                group_recv.at[flip, p],
                here.group_to(flip),
            ).wait_recv()

    group_arrival(1)

    @pl.when(away)
    def _():
        group_arrival(0)

    @pl.when(~away)
    def _():
        for kind, rows_in in ((0, prompt_in), (1, cont_in)):

            @pl.when(x == kind)
            def _():
                for copy in group_copies(0, rows_in, False):
                    copy.wait()

    def z_piece(i, s):
        start = first0 if s == 2 else LANES
        return remote(
            sources[i].at[pl.ds(row0, part), pl.ds(start, LANES)],
            slot_w.at[s, 0:part, i * LANES : (i + 1) * LANES],
            z_send.at[s, i],
            z_recv.at[s, i],
            here.other("zh"),
        )

    for i in range(4):
        z_piece(i, 2).start()

    @pl.when(owner)
    def _():
        for i in range(4):
            z_piece(i, 1).start()

    z_out = [
        remote(
            w_out_in.at[pl.ds(first0, LANES), pl.ds(row0, part)],
            w_out_all.at[2 * LANES : 3 * LANES, 0:part],
            z_send.at[0, 0],
            z_recv.at[0, 0],
            here.other("zh"),
        ),
        remote(
            w_out_in.at[LANES : 2 * LANES, pl.ds(row0, part)],
            w_out_all.at[LANES : 2 * LANES, 0:part],
            z_send.at[0, 1],
            z_recv.at[0, 1],
            here.other("zh"),
        ),
    ]
    z_out[0].start()

    @pl.when(owner)
    def _():
        z_out[1].start()

    def norm_rows(i, carry):
        rows = pl.ds(pl.multiple_of(i * 32, 32), 32)
        value = tokens[rows, :].astype(F32)
        factor = lax.rsqrt(jnp.mean(value * value, axis=-1, keepdims=True) + epsilon)
        normed[rows, :] = (value * factor * feats[0, 0:1, :]).astype(BF)
        return carry

    lax.fori_loop(0, local // 32, norm_rows, 0)

    def ag_copy(k):
        return remote(
            normed.at[0:local],
            normed.at[k * local : (k + 1) * local],
            ag_send.at[k - 1],
            ag_recv.at[k - 1],
            here.peer(k),
        )

    for k in range(peers - 1, 0, -1):
        ag_copy(k).start()

    outs = [
        pltpu.make_async_copy(tokens, tokens_out, out_sem.at[0]),
        pltpu.make_async_copy(small, small_out, out_sem.at[1]),
        pltpu.make_async_copy(feats.at[0], gains_out, out_sem.at[2]),
        pltpu.make_async_copy(forget_w, forget_w_out, out_sem.at[3]),
    ]
    for copy in outs:
        copy.start()

    x_copy(0).wait_recv()
    c_copy(0).start()
    for i in range(4):
        z_piece(i, 2).wait_recv()
    x_copy(2).start()

    @pl.when(owner)
    def _():
        for i in range(4):
            own_piece(i, 1).wait()

    @pl.when(~owner)
    def _():
        for i in range(4):
            z_piece(i, 1).wait_recv()

    x_copy(1).start()

    projects = (proj_a, proj_b, proj_c)
    theres = (there_a, there_b, there_c)

    def chunk(k):
        return slice(k * local, (k + 1) * local)

    def kv_copy(k, s):
        return remote(
            project.at[s, chunk(k), 2 * LANES :],
            theres[s].at[chunk(k)],
            kv_send.at[k, s],
            kv_recv.at[k, s],
            here.other("c"),
        )

    def forget_copy(k):
        return remote(
            forget.at[chunk(k)],
            forget_there.at[chunk(k)],
            kv_send.at[k, 3],
            kv_recv.at[k, 3],
            here.other("c"),
        )

    def project_chunk(k, s):
        project[s, chunk(k), :] = nn_dot(normed[chunk(k), :], slot_w[s]).astype(BF)
        kv_copy(k, s).start()

    def forget_chunk(k):
        forget[chunk(k), :] = nt_dot(normed[chunk(k), :], forget_w[...]).astype(BF)
        forget_copy(k).start()

    c_copy(0).wait_recv()
    forget_chunk(0)
    project_chunk(0, 0)
    for k in range(1, peers):
        ag_copy(k).wait_recv()
        forget_chunk(k)
        project_chunk(k, 0)
    normed_copy = pltpu.make_async_copy(normed, normed_out, out_sem.at[4])
    normed_copy.start()
    for s in (2, 1):
        x_copy(s).wait_recv()
        c_copy(s).start()
    own_out[0].wait()
    z_out[0].wait_recv()

    @pl.when(owner)
    def _():
        own_out[1].wait()

    @pl.when(~owner)
    def _():
        z_out[1].wait_recv()

    x_out = remote(
        w_out_all.at[:, 0:part],
        w_out_all.at[:, part : 2 * part],
        x_send.at[3],
        x_recv.at[3],
        here.other("x"),
    )
    x_out.start()
    for s in (2, 1):
        c_copy(s).wait_recv()
        for k in range(peers):
            project_chunk(k, s)
    slots_copy = pltpu.make_async_copy(slot_w, slots_out, out_sem.at[5])
    slots_copy.start()
    finals = [
        pltpu.make_async_copy(project.at[s], projects[s], out_sem.at[6 + s]) for s in range(3)
    ] + [pltpu.make_async_copy(forget, forget_own, out_sem.at[9])]
    for copy in finals:
        copy.start()
    x_out.wait_recv()
    c_out = remote(
        w_out_all.at[:, 0:half],
        w_out_all.at[:, half:features],
        c_send.at[3],
        c_recv.at[3],
        here.other("c"),
    )
    c_out.start()

    on_group(1, lambda copy: copy.wait_send())

    @pl.when(away)
    def _():
        ints_copy().wait()
        for kind, rows_in in ((0, prompt_in), (1, cont_in)):

            @pl.when(x == kind)
            def _():
                for copy in group_copies(0, rows_in, True):
                    copy.wait_send()

    @pl.when(~away)
    def _():
        ints_own().wait()

    small_z.wait_send()
    small_over_x.wait_send()
    for i in range(4):
        z_piece(i, 2).wait_send()
    z_out[0].wait_send()

    @pl.when(owner)
    def _():
        for i in range(4):
            z_piece(i, 1).wait_send()
        z_out[1].wait_send()

    for s in range(3):
        x_copy(s).wait_send()
        c_copy(s).wait_send()
    x_out.wait_send()
    for k in range(1, peers):
        ag_copy(k).wait_send()
    for k in range(peers):
        for s in range(3):
            kv_copy(k, s).wait()
        forget_copy(k).wait()
    c_out.wait()
    for copy in outs + finals + [normed_copy, slots_copy]:
        copy.wait()


def first_step(ring, prompt, cont, small, ints, wq, wg, wk, wv, w_out):
    local, half = prompt.shape
    features = 2 * half
    part = half // 2
    peers = len(ring.offsets)
    rows = peers * local
    slot = 4 * LANES
    any_spec = pl.BlockSpec(memory_space=pl.ANY)
    dma = pltpu.SemaphoreType.DMA
    shapes = [
        ((local, features), BF),
        ((rows, features), BF),
        ((3, features, slot), BF),
        ((3 * LANES, features), BF),
        ((2, 16, half), F32),
        ((16, features), F32),
        ((LANES, features), BF),
        (ints.shape, jnp.int32),
        ((rows, slot), BF),
        ((rows, slot), BF),
        ((rows, slot), BF),
        ((rows, LANES), BF),
        ((rows, 2 * LANES), BF),
        ((rows, 2 * LANES), BF),
        ((rows, 2 * LANES), BF),
        ((rows, LANES), BF),
    ]
    return pl.pallas_call(
        functools.partial(first_kernel, ring),
        out_shape=tuple(jax.ShapeDtypeStruct(*s) for s in shapes),
        in_specs=[any_spec] * 9,
        out_specs=[any_spec] * len(shapes),
        scratch_shapes=[
            pltpu.VMEM((local, features), BF),
            pltpu.VMEM((rows, features), BF),
            pltpu.VMEM((3, features, slot), BF),
            pltpu.VMEM((3, rows, slot), BF),
            pltpu.VMEM((rows, LANES), BF),
            pltpu.VMEM((2, 16, half), F32),
            pltpu.VMEM((2, 16, half), F32),
            pltpu.VMEM((2, 16, features), F32),
            pltpu.VMEM((16, features), F32),
            pltpu.VMEM((LANES, features), BF),
            dma((2, 2)),
            dma((2, 2)),
            dma,
            dma,
            dma((2,)),
            dma((2,)),
            dma((16,)),
            dma((3, 4)),
            dma((3, 4)),
            dma((4,)),
            dma((4,)),
            dma((4,)),
            dma((4,)),
            dma((peers - 1,)),
            dma((peers - 1,)),
            dma((peers, 4)),
            dma((peers, 4)),
            dma((10,)),
        ],
        compiler_params=pltpu.CompilerParams(
            collective_id=3, has_side_effects=True, vmem_limit_bytes=48 << 20
        ),
        cost_estimate=pl.CostEstimate(
            flops=2 * rows * features * 3 * slot, bytes_accessed=40 << 20, transcendentals=0
        ),
    )(prompt, cont, small, ints, wq, wg, wk, wv, w_out)


def ring_body(
    ring,
    x_prompt,
    x_cont,
    teacher_prompt,
    teacher_cont,
    segment_ids,
    offsets,
    prompt_valid,
    cont_valid,
    first_gain,
    w_query,
    w_key,
    w_value,
    w_outgate,
    w_forget,
    forget_bias,
    w_out,
    second_gain,
    w_gate,
    w_up,
    w_down,
):
    y = lax.axis_index("y")
    c = lax.axis_index("c")
    x = lax.axis_index("x")
    zh = lax.axis_index("zh")
    zl = lax.axis_index("zl")
    zl_count = ring.zl_count
    local = x_prompt.shape[1]
    half_d = x_prompt.shape[2]
    part_d = half_d // 2
    local_conts = x_cont.shape[1]
    heads = w_forget.shape[1]
    units_here = w_gate.shape[1]
    half_units = units_here // 2
    width = heads * HEAD_DIM
    slots = heads // 2
    pair_unit = PROMPT // CLEN
    chunk_units = local // CLEN
    own_valid = jnp.where(x == 0, prompt_valid.reshape(-1), cont_valid.reshape(-1))
    small_in = jnp.concatenate([own_valid, segment_ids.reshape(-1), offsets.reshape(-1)])
    int_rows = 16
    ints = jnp.pad(small_in, (0, int_rows * LANES - small_in.shape[0])).reshape(int_rows, LANES)
    packed = jnp.concatenate(
        [
            first_gain[None].astype(F32),
            second_gain[None].astype(F32),
            jnp.pad(forget_bias, (0, half_d - heads))[None],
            jnp.zeros((5, half_d), F32),
            w_forget.T.astype(F32),
            jnp.zeros((8 - heads, half_d), F32),
        ],
        axis=0,
    )
    (
        tokens_b,
        normed_all,
        w_slots,
        w_out_all,
        small_all,
        gains,
        w_forget_rows,
        ints,
        proj_a,
        proj_b,
        proj_c,
        forget_own,
        there_a,
        there_b,
        there_c,
        forget_there,
    ) = first_step(
        ring,
        x_prompt[0],
        x_cont.reshape(local_conts * CLEN, half_d),
        packed,
        ints,
        w_query,
        w_outgate,
        w_key,
        w_value,
        w_out,
    )
    projects = [proj_a, proj_b, proj_c]
    kv_there = [there_a, there_b, there_c]
    ints = ints.reshape(-1)
    validity = ints[:local].astype(F32)
    segment_row = ints[local : local + PROMPT]
    offset_row = ints[local + PROMPT : local + PROMPT + CONTS]
    gain_one = gains[0]
    gain_two = gains[1]

    def head_slots(value):
        first = jnp.where(y == 0, value[:, 0:2], value[:, 4:6])
        slot_a = jnp.where(zh == 0, first[0], first[1])
        slot_c = jnp.where(zh == 0, first[1], first[0])
        slot_b = jnp.where(y == 0, value[0, 2:4], value[1, 2:4])
        return jnp.concatenate([slot_a, slot_b, slot_c], axis=0)

    bias_all = small_all[:, 2, :heads]
    bias_all = jnp.stack(
        [
            jnp.where(zh == 0, bias_all[0], bias_all[1]),
            jnp.where(zh == 0, bias_all[1], bias_all[0]),
        ]
    )
    bias_row = head_slots(bias_all[:, :, None])[:, 0]
    bias_row = jnp.concatenate([bias_row, jnp.zeros((LANES - heads,), F32)])[None]

    proj_a, w_gate, w_up = lax.optimization_barrier((proj_a, w_gate, w_up))
    projects[0] = proj_a
    hid_own = jnp.concatenate(
        [
            lax.dynamic_slice(w, (c * part_d, y * half_units), (part_d, half_units))
            for w in (w_gate, w_up)
        ],
        axis=1,
    )
    hid_there_w = ring.swap(hid_own, "zh")

    dy_all = jnp.array([o[0] for o in ring.offsets], jnp.int32)
    dz_all = jnp.array([o[1] for o in ring.offsets], jnp.int32)
    places = ((y - dy_all) % 2) * zl_count + (zl - dz_all) % zl_count
    unit_no = (places[:, None] * chunk_units + jnp.arange(chunk_units, dtype=jnp.int32)).reshape(-1)
    natural = jnp.arange(pair_unit, dtype=jnp.int32)
    pick = unit_no[:, None] == natural[None, :]
    step = jnp.arange(CLEN, dtype=jnp.int32)
    row_pos = (unit_no[:, None] * CLEN + step[None, :]).reshape(-1)
    seg_rel = jnp.sum(
        jnp.where(pick[:, :, None], segment_row.reshape(1, pair_unit, CLEN), 0), axis=1
    )
    offs_rel = jnp.sum(jnp.where(pick, offset_row[None, :], 0), axis=1)
    last_rel = jnp.sum(
        jnp.where(
            jnp.arange(PROMPT, dtype=jnp.int32)[None, :] == offs_rel[:, None] - 1,
            segment_row[None, :],
            0,
        ),
        axis=1,
    )
    limit = jnp.where(c == 0, unit_no * CLEN, offs_rel)
    doc_row = jnp.where(c == 0, seg_rel, last_rel[:, None]).reshape(-1, 1)
    seg_col = seg_rel.reshape(-1, 1)
    lane = jnp.arange(LANES, dtype=jnp.int32)[None, :]
    unit_col = jnp.repeat(natural, CLEN)[:, None]
    pieces = 3 * heads
    is_doc = (lane >= DOC_LANE) & (lane < DOC_LANE + 4)
    is_unit = (lane >= UNIT_LANE) & (lane < UNIT_LANE + pair_unit)
    limit_lane = jnp.pad(limit, (UNIT_LANE, LANES - UNIT_LANE - pair_unit))[None, :]
    q_base = jnp.where(
        (lane >= FAR_PIECE) & (lane < FAR_PIECE + pieces),
        1.0,
        jnp.where(
            (is_doc & (doc_row != lane - DOC_LANE)) | (is_unit & (unit_col == lane - UNIT_LANE)),
            -NEVER,
            0.0,
        ),
    ).astype(BF)
    near_base = jnp.where(
        (lane < pieces) | (is_doc & (doc_row == lane - DOC_LANE)), 1.0, 0.0
    ).astype(BF)
    far_base = jnp.where(
        (lane < pieces)
        | (is_doc & (seg_col == lane - DOC_LANE))
        | (is_unit & (row_pos[:, None] >= limit_lane)),
        1.0,
        0.0,
    ).astype(BF)
    tri = (step[:, None] >= step[None, :]).astype(F32)
    earlier = (unit_no[None, :] < unit_no[:, None]).astype(F32)
    hot = (row_pos[None, :] == limit[:, None] - 1).astype(F32)
    cont_hot = (row_pos[None, :] == offs_rel[:, None] - 1).astype(F32)

    forget_far = jnp.where(c == 0, forget_own, forget_there)
    flag = c.astype(jnp.int32).reshape(1)
    head_lane = lane < heads

    def keep_log(lin):
        return jnp.where(head_lane, jax.nn.log_sigmoid(lin.astype(F32) + bias_row), 0.0)

    def within(values, matrix):
        return jnp.einsum(
            "ts,ush->uth", matrix, values.reshape(pair_unit, CLEN, LANES), precision=highest
        )

    far_within = within(keep_log(forget_far), tri)
    far_prefix = jnp.dot(earlier, far_within[:, -1], precision=highest)
    cum_far = (far_within + far_prefix[:, None]).reshape(-1, LANES)
    own_base = jnp.dot(hot, cum_far, precision=highest)
    cum_near = (within(keep_log(forget_own), tri) + own_base[:, None]).reshape(-1, LANES)
    keep_slope = jnp.where(
        head_lane, jax.nn.sigmoid(-(forget_own.astype(F32) + bias_row)), 0.0
    )
    gated, attended, logs = attend(
        flag, projects, kv_there, cum_near, cum_far, q_base, near_base, far_base, local, heads
    )
    (
        grad_gated,
        grad_residual,
        grad_residual_all,
        hid_kept,
        hid_there,
        down_kept,
        down_there,
        error_rows,
        gain_two_rows,
    ) = middle_step(
        ring,
        gated,
        w_out_all,
        hid_own,
        hid_there_w,
        w_down,
        tokens_b,
        teacher_prompt[0],
        teacher_cont.reshape(local_conts * CLEN, half_d),
        validity[:, None],
        gain_two[None],
    )
    dqg, dkv_near, dkv_far, row_sum, near_sum, far_sum = attend_back(
        flag,
        projects,
        kv_there,
        cum_near,
        cum_far,
        q_base,
        near_base,
        far_base,
        grad_gated,
        attended,
        logs,
        local,
        heads,
    )

    def low(value):
        return lax.reduce_precision(value, 8, 7).astype(BF)

    def over_zh(value, dim):
        size = value.shape[dim] // 2
        mine = lax.slice_in_dim(value, 0, size, axis=dim)
        theirs = lax.slice_in_dim(value, size, 2 * size, axis=dim)
        return low(mine + ring.swap(theirs.astype(BF), "zh").astype(F32))

    hid_mine = over_zh(hid_kept + hid_there.astype(F32), 1)
    down_mine = over_zh(down_kept + down_there.astype(F32), 0)
    rows_back, proj_all, gate_all, up_all, down_all, out_all, small_sums = last_step(
        ring,
        heads,
        [
            dqg,
            dkv_near,
            dkv_far,
            row_sum,
            near_sum,
            far_sum,
            w_slots,
            normed_all,
            gated,
            grad_residual_all,
            tokens_b,
            grad_residual,
            hid_mine,
            down_mine,
        ],
        [
            gain_one[None],
            w_forget_rows,
            keep_slope,
            cont_hot.T,
            error_rows,
            gain_two_rows,
            validity[:, None],
        ],
    )
    gain_one_sum = small_sums[:, 0].reshape(-1)
    gain_two_sum = small_sums[:, 1].reshape(-1)
    sums = small_sums[0, 2]
    projection_grads = [
        jnp.concatenate(
            [proj_all[:, (4 * s + i) * LANES : (4 * s + i + 1) * LANES] for s in range(slots)],
            axis=1,
        )
        for i in range(4)
    ]
    forget_grad = proj_all[:, 4 * width : 4 * width + heads]
    error_total = sums[0]
    count_total = sums[1]
    groups = ring.sizes["yo"] * ring.sizes["y"] * ring.sizes["c"]
    grad_scale = groups * (PROMPT + CONTS * CLEN) / count_total
    loss_value = error_total / (D * count_total)

    def own_half(value):
        return lax.dynamic_slice_in_dim(value, x * half_d, half_d, value.ndim - 1)

    quarter_no = zh * zl_count + zl
    bias_out = lax.dynamic_slice_in_dim(sums, 2 + quarter_no * heads, heads, 0)

    def scaled(value):
        return value.astype(F32) * grad_scale

    return (
        loss_value,
        scaled(rows_back[0])[None],
        scaled(rows_back[1]).reshape(1, local_conts, CLEN, half_d),
        scaled(own_half(gain_one_sum)),
        scaled(projection_grads[0]),
        scaled(projection_grads[2]),
        scaled(projection_grads[3]),
        scaled(projection_grads[1]),
        scaled(forget_grad),
        scaled(bias_out),
        scaled(out_all),
        scaled(own_half(gain_two_sum)),
        scaled(gate_all),
        scaled(up_all),
        scaled(down_all),
    )


def specs(dp, row, col):
    in_specs = (
        P(dp, col, row),
        P(dp, col, None, row),
        P(dp, col, row),
        P(dp, col, None, row),
        P(dp, None),
        P(dp, None),
        P(dp, col),
        P(dp, col, None),
        P(row),
        P(row, col),
        P(row, col),
        P(row, col),
        P(row, col),
        P(row, col),
        P(col),
        P(col, row),
        P(row),
        P(row, col),
        P(row, col),
        P(col, row),
    )
    out_specs = (
        P(),
        P(dp, col, row),
        P(dp, col, None, row),
        P(row),
        P(row, col),
        P(row, col),
        P(row, col),
        P(row, col),
        P(row, col),
        P(col),
        P(col, row),
        P(row),
        P(row, col),
        P(row, col),
        P(col, row),
    )
    return in_specs, out_specs


def solution(mesh):
    dp, row, col = mesh.shape["dp"], mesh.shape["row"], mesh.shape["col"]
    heads = HEADS // col
    if dp == 4 and row == 2 and col % 2 == 0 and heads == 6:
        sizes = {"yo": dp // 4, "y": 2, "c": 2, "x": 2, "zh": 2, "zl": col // 2}
        ring_mesh = Mesh(mesh.devices.reshape([sizes[a] for a in AX]), AX)
        in_specs, out_specs = specs(("yo", "y", "c"), "x", ("zh", "zl"))
        step = functools.partial(ring_body, Ring(sizes))
        return jax.shard_map(
            step, mesh=ring_mesh, in_specs=in_specs, out_specs=out_specs, check_vma=False
        )
    in_specs, out_specs = specs("dp", "row", "col")
    return jax.shard_map(
        wide_body, mesh=mesh, in_specs=in_specs, out_specs=out_specs, check_vma=False
    )
```

profile of v0, /device:TPU:0, one launch (start us, length us, event | category | flops | bytes accessed | tf_op | source)
XLA Modules:
  0.0 658.5 jit_solution(7483319080154844171)
XLA Ops:
  4.9 1.1 copy-done.5
  6.0 1.1 copy-done.6
  7.0 1.1 copy-done.7
  8.1 1.1 copy-done.8
  11.1 86.4 %shard_map.325 = (bf16[256,1536]{1,0:T(8,128)(2,1)}, bf16[1024,1536]{1,0:T(8,128)(2,1)}, bf16[3,1536,512]{2,1,0:T(8,128)(2,1)}, bf16[384,1536]{1,0:T(8,128)(2,1)...) custom-call(bf16[256,768]{1,0:T(8,128)(2,1)S(1)} %bitcast.68, ...), custom_call_target="tpu_custom_call" | custom-call | flops 4831838208 | bytes 41943040 | tf_op jit(solution)/shard_map/pallas_call | solution.py:2972
  102.8 7.7 %collective-permute-start = (bf16[384,1024]{1,0:T(8,128)(2,1)}, bf16[384,1024]{1,0:T(8,128)(2,1)}, u32[]{:S(2)}, u32[]{:S(2)}) collective-permute-start(bf16[384,1024]{1,0:T(8,128)(2,1)} %pad_maximum_fusion.hid_own_in), channel_id=1, source_target_pairs={{0,2},{1,3},{2,0},{3,1},{4,6},{5,7},{6,4},{7,5},{8,10},{9,11},{10,... | collective-permute-start | bytes 2359304 | tf_op jit(solution)/shard_map/ppermute | solution.py:605
  111.5 1.6 divide_select_fusion
  117.2 1.1 compare_convert_fusion.hot_ref
  118.2 1.0 copy-done.14
  120.3 1.0 copy-done.18
  121.4 20.9 %shard_map.326 = (bf16[1024,384]{1,0:T(8,128)(2,1)S(1)}, f32[1024,384]{1,0:T(8,128)}, f32[1024,128]{1,0:T(8,128)S(1)}) custom-call(s32[1]{0:T(128)} %bitcast.flag, bf16[1024,512]{1,0:T(8,128)(2,1)S(1)} %copy-done.11, bf16[1024,512]{1,0:T(8,128)(2,1)} %get-tuple-element.61.qg_b.near_b.own_b, bf16[1024,512]{1,0:T(8,128)(2,1)} %get-tuple-element.62.qg_c.near_c.own_c, ...), custom_call_target="tpu_custom_call" | custom-call | flops 6039797760 | bytes 7864320 | tf_op jit(solution)/shard_map/pallas_call | solution.py:875
  144.8 283.1 %shard_map.327 = (f32[1024,384]{1,0:T(8,128)}, f32[256,1536]{1,0:T(8,128)}, bf16[1024,1536]{1,0:T(8,128)(2,1)}, f32[384,2048]{1,0:T(8,128)}, bf16[384,2048]{1,0:...) custom-call(bf16[1024,384]{1,0:T(8,128)(2,1)} %copy-done.12, ...), custom_call_target="tpu_custom_call" | custom-call | flops 32614907904 | bytes 62914560 | tf_op jit(solution)/shard_map/pallas_call | solution.py:2408
  428.0 1.9 convert_add_fusion.1
  430.0 4.6 collective-permute-start.2
  435.1 1.1 collective-permute-start.1
  436.2 30.1 %shard_map.328 = (bf16[1024,768]{1,0:T(8,128)(2,1)}, f32[1024,768]{1,0:T(8,128)}, bf16[1024,768]{1,0:T(8,128)(2,1)}, f32[1024,128]{1,0:T(8,128)}, f32[1024,128]{1,0:T(8,128)}, /*index=5*/f32[1024,128]{1,0:T(8,128)}) custom-call(s32[1]{0:T(128)} %bitcast.flag, bf16[1024,512]{1,0:T(8,128)(2,1)} %get-tuple-element.60.qg_a.near_a.own_a, ...), custom_call_target="tpu_custom_call" | custom-call | flops 18119393280 | bytes 15728640 | tf_op jit(solution)/shard_map/pallas_call | solution.py:1057
  467.1 12.7 %collective-permute-done.1 = bf16[384,1024]{1,0:T(8,128)(2,1)S(1)} collective-permute-done((bf16[384,1024]{1,0:T(8,128)(2,1)S(1)}, bf16[384,1024]{1,0:T(8,128)(2,1)S(1)}, u32[]{:S(2)}, u32[]{:S(2)}) %collective-permute-start.1) | collective-permute-done | bytes 786464 | tf_op jit(solution)/shard_map/ppermute | solution.py:605
  479.8 1.1 fusion.1.hid_in
  480.9 149.7 %shard_map.329 = (bf16[2,256,768]{2,1,0:T(8,128)(2,1)}, bf16[768,1664]{1,0:T(8,128)(2,1)}, bf16[768,1024]{1,0:T(8,128)(2,1)}, bf16[768,1024]{1,0:T(8,128)(2,1)},...) custom-call(bf16[1024,768]{1,0:T(8,128)(2,1)} %get-tuple-element.79.dqg_in, ...), custom_call_target="tpu_custom_call" | custom-call | flops 9663676416 | bytes 41943040 | tf_op jit(solution)/shard_map/pallas_call | solution.py:1812
  630.6 1.3 fusion.31
  632.8 1.3 slice.167
  634.1 2.0 fusion.29
  637.8 1.9 convert_multiply_fusion
  639.8 2.1 convert_multiply_fusion.1
  641.9 2.1 convert_multiply_fusion.2
  644.6 2.2 convert_multiply_fusion.3
  648.9 1.3 convert_multiply_fusion.8
  650.8 1.3 multiply_bitcast_fusion
  652.7 1.1 convert_multiply_fusion.4
  653.8 1.1 convert_multiply_fusion.5
  654.9 1.1 convert_multiply_fusion.6
  656.0 1.1 convert_multiply_fusion.7
  (117 shorter events, 26.0 us)
Async XLA Ops:
  4.9 1.1 copy-start.5
  6.0 1.1 copy-start.6
  7.0 1.1 copy-start.7
  8.1 1.1 copy-start.8
  9.1 1.0 copy-start.9
  10.1 1.0 copy-start.10
  97.6 0.8 copy-start.13
  100.7 1.0 dynamic-slice-start
  100.7 1.1 dynamic-slice-start.1
  100.7 9.9 %copy-start.28 = (s32[4]{0:T(128)S(1)}, s32[4]{0:T(128)}, u32[]{:S(2)}) copy-start(s32[4]{0:T(128)} %constant.121) | copy-start | bytes 52
  100.7 9.9 %copy-start.29 = (s32[4]{0:T(128)S(1)}, s32[4]{0:T(128)}, u32[]{:S(2)}) copy-start(s32[4]{0:T(128)} %constant.122) | copy-start | bytes 52
  102.8 42.0 %collective-permute-start = (bf16[384,1024]{1,0:T(8,128)(2,1)}, bf16[384,1024]{1,0:T(8,128)(2,1)}, u32[]{:S(2)}, u32[]{:S(2)}) collective-permute-start(bf16[384,1024]{1,0:T(8,128)(2,1)} %pad_maximum_fusion.hid_own_in), channel_id=1, source_target_pairs={{0,2},{1,3},{2,0},{3,1},{4,6},{5,7},{6,4},{7,5},{8,10},{9,11},{10,... | collective-permute-start | bytes 2359304 | tf_op jit(solution)/shard_map/ppermute | solution.py:605
  113.8 4.5 copy-start
  113.8 4.5 copy-start.11
  116.2 26.1 %copy-start.1 = (f32[8,128,128]{1,2,0:T(8,128)}, f32[8,128,128]{1,2,0:T(8,128)S(1)}, u32[]{:S(2)}) copy-start(f32[8,128,128]{1,2,0:T(8,128)S(1)} %convolution_add_fusion) | copy-start | bytes 1572868
  117.1 25.2 %copy-start.2 = (bf16[1024,128]{1,0:T(8,128)(2,1)}, bf16[1024,128]{1,0:T(8,128)(2,1)S(1)}, u32[]{:S(2)}) copy-start(bf16[1024,128]{1,0:T(8,128)(2,1)S(1)} %get-tuple-element.192.near_base) | copy-start | bytes 786436
  117.2 25.2 %copy-start.3 = (bf16[1024,128]{1,0:T(8,128)(2,1)}, bf16[1024,128]{1,0:T(8,128)(2,1)S(1)}, u32[]{:S(2)}) copy-start(bf16[1024,128]{1,0:T(8,128)(2,1)S(1)} %get-tuple-element.193.q_base) | copy-start | bytes 786436
  117.2 25.2 %copy-start.4 = (bf16[1024,128]{1,0:T(8,128)(2,1)}, bf16[1024,128]{1,0:T(8,128)(2,1)S(1)}, u32[]{:S(2)}) copy-start(bf16[1024,128]{1,0:T(8,128)(2,1)S(1)} %get-tuple-element.194.far_base) | copy-start | bytes 786436
  118.2 1.0 copy-start.14
  119.3 1.0 copy-start.16
  120.3 1.0 copy-start.18
  142.3 0.9 copy-start.12
  143.2 0.8 copy-start.19
  428.0 6.6 copy-start.21
  428.0 6.6 copy-start.25
  430.0 36.3 %collective-permute-start.2 = (bf16[512,384]{1,0:T(8,128)(2,1)S(1)}, bf16[512,384]{1,0:T(8,128)(2,1)S(1)}, u32[]{:S(2)}, u32[]{:S(2)}) collective-permute-start(bf16[512,384]{1,0:T(8,128)(2,1)S(1)} %slice.207), channel_id=1, source_target_pairs={{0,2},{1,3},{2,0},{3,1},{4,6},{5,7},{6,4},{7,5},{8,10},{9,11},{10,... | collective-permute-start | bytes 1179656 | tf_op jit(solution)/shard_map/ppermute | solution.py:605
  435.1 44.7 %collective-permute-start.1 = (bf16[384,1024]{1,0:T(8,128)(2,1)S(1)}, bf16[384,1024]{1,0:T(8,128)(2,1)S(1)}, u32[]{:S(2)}, u32[]{:S(2)}) collective-permute-start(bf16[384,1024]{1,0:T(8,128)(2,1)S(1)} %slice.206), channel_id=1, source_target_pairs={{0,2},{1,3},{2,0},{3,1},{4,6},{5,7},{6,4},{7,5},{8,10},{9,11},{10,... | collective-permute-start | bytes 2359304 | tf_op jit(solution)/shard_map/ppermute | solution.py:605
  634.1 3.7 copy-start.24
  637.8 2.0 copy-start.23
  639.8 2.1 copy-start.22
  644.0 4.9 copy-start.26
  644.6 2.9 copy-start.27
  (3 other events, 2.4 us)
where the time goes:
time: 668 us; the launch traced here: 659 us
  Pallas kernels  570 us (85%)
  other arithmetic  29.5 us (4%)
  local copies, waits for them, and re-layouts  26.2 us (4%)
  waiting for transfers between devices  13.5 us (2%)
  starting transfers between devices  13.4 us (2%)
    pallas_call x1, Pallas kernels, middle_step(): pl.pallas_call(functools.partial(middle_kernel, ring), out_shape=(jax.Sha...  283 us
    pallas_call x1, Pallas kernels, last_step(): pl.pallas_call(functools.partial(last_kernel, ring, heads), out_shape=(ja...  150 us
    pallas_call x1, Pallas kernels, first_step(): pl.pallas_call(functools.partial(first_kernel, ring), out_shape=tuple((ja...  86.4 us
    pallas_call x1, Pallas kernels, attend_back(): pl.pallas_call(functools.partial(attend_back_kernel, heads), grid=(steps,...  30.1 us
    pallas_call x1, Pallas kernels, attend(): pl.pallas_call(functools.partial(attend_kernel, heads), grid=(steps,), ou...  20.9 us
    mul x13, other arithmetic, scaled(): return value.astype(F32) * grad_scale  17.5 us
    unnamed x61, local copies, waits for them, and re-layouts  15.1 us
    ppermute x3, waiting for transfers between devices, move(): return lax.ppermute(value, AX, self.pairs(target, source_ok))  13.5 us
  transfers between devices with their start and end apart: 3, of which 2 were waited for; matrix products, arithmetic and copies ran while one was open for 1% of the time, Pallas kernels for 8%

commit v1 on v0

--- a/solution.py
+++ b/solution.py
@@ -886,7 +886,7 @@
             pltpu.VMEM((heads // 2, total + rows, 2 * LANES), BF),
             pltpu.VMEM((heads, HEAD_DIM + 16, total + rows), BF),
         ],
-        compiler_params=pltpu.CompilerParams(vmem_limit_bytes=48 << 20),
+        compiler_params=pltpu.CompilerParams(vmem_limit_bytes=60 << 20),
         cost_estimate=pl.CostEstimate(
             flops=flops, bytes_accessed=total * width * 20, transcendentals=total * total * heads
         ),
@@ -1081,7 +1081,7 @@
             pltpu.VMEM((heads // 2, total + rows, 2 * LANES), BF),
             pltpu.VMEM((total, 2 * width), F32),
         ],
-        compiler_params=pltpu.CompilerParams(vmem_limit_bytes=56 << 20),
+        compiler_params=pltpu.CompilerParams(vmem_limit_bytes=60 << 20),
         cost_estimate=pl.CostEstimate(
             flops=flops, bytes_accessed=total * width * 40, transcendentals=total * total * heads
         ),
@@ -1178,7 +1178,8 @@
     tokens_in,
     residual_in,
     hid_in,
-    down_in,
+    down_kept_in,
+    down_there_in,
     gain_ref,
     forget_w,
     sig_ref,
@@ -1231,6 +1232,11 @@
     full_f,
     co_send,
     co_land,
+    kept_d,
+    there_d,
+    zd_send,
+    zd_land,
+    final_d,
     kept_o,
     xo_send,
     xo_land,
@@ -1270,7 +1276,7 @@
     slot_w = 4 * LANES
     slots = heads // 2
     all_w = slots * slot_w
-    units = down_in.shape[0]
+    units = down_kept_in.shape[0] // 2
     owner = zh == y
     peers = len(ring.offsets)
     away = here.group_away()
@@ -1289,6 +1295,8 @@
             )
         )
     all_loads += [
+        (down_kept_in, kept_d),
+        (down_there_in, there_d),
         (normed_in, normed),
         (weight_in, weight),
         (gated_in, gated),
@@ -1299,11 +1307,13 @@
     loads = [
         pltpu.make_async_copy(a, b, load_sem.at[i]) for i, (a, b) in enumerate(all_loads)
     ]
-    for copy in loads:
+    first_loads = 8 + slots
+    for copy in loads[:first_loads]:
         copy.start()
     load_row, load_near_col, load_far_col, load_far, load_near = loads[:5]
     load_dqg = loads[5 : 5 + slots]
-    load_normed, load_weight, load_gated, load_mixed, load_tokens, load_residual = loads[5 + slots :]
+    load_kept_d, load_there_d = loads[5 + slots : 7 + slots]
+    load_normed, load_weight, load_gated, load_mixed, load_tokens, load_residual = loads[7 + slots :]
 
     here.greet_group(
         [here.peer(k) for k in range(1, peers)]
@@ -1317,6 +1327,29 @@
         far_col_in, far_col_land, swap_send_sem.at[1], swap_recv_sem.at[1], here.other("c")
     )
     col_swap.start()
+
+    row0 = pl.multiple_of(c * part, part)
+
+    def rows_of(ref, col, width):
+        return ref.at[pl.ds(row0, part), pl.ds(pl.multiple_of(col, LANES), width)]
+
+    def cols_of(ref, row, height):
+        return ref.at[pl.ds(pl.multiple_of(row, LANES), height), pl.ds(row0, part)]
+
+    def y_copy(i, src, dst):
+        return remote(src, dst, y_send_sem.at[i], y_recv_sem.at[i], here.other("y"))
+
+    pieces = [
+        (hid_in.at[:, :units], rows_of(gate_out, y * units, units)),
+        (hid_in.at[:, units:], rows_of(up_out, y * units, units)),
+        (final_d, cols_of(down_out, y * units, units)),
+    ]
+    own_pieces = [
+        pltpu.make_async_copy(src, dst, local_sem.at[i]) for i, (src, dst) in enumerate(pieces)
+    ]
+    y_pieces = [y_copy(i, src, dst) for i, (src, dst) in enumerate(pieces)]
+    for copy in own_pieces[:2] + y_pieces[:2]:
+        copy.start()
 
     lane = lax.broadcasted_iota(jnp.int32, (CLEN, LANES), 1)
     head_lane = lane < heads
@@ -1344,24 +1377,18 @@
     )
     tot_swap.start()
 
-    load_gated.wait()
-    load_mixed.wait()
-    out_rows = slots * LANES
-
-    def out_tile(s, cols):
-        return tn_dot(gated[:, s * LANES : (s + 1) * LANES], mixed[:, cols])
-
-    for s in range(slots):
-        co_send[s * LANES : (s + 1) * LANES, :] = out_tile(
-            s, slice(2 * part, features)
-        ).astype(BF)
-    co_copy = remote(co_send, co_land, c_send_sem.at[1], c_recv_sem.at[1], here.other("c"))
-    co_copy.start()
+    load_kept_d.wait()
+    load_there_d.wait()
+    zd_send[...] = (kept_d[units:, :] + there_d[units:, :].astype(F32)).astype(BF)
+    zd_copy = remote(zd_send, zd_land, z_send_sem.at[5], z_recv_sem.at[5], here.other("zh"))
+    zd_copy.start()
 
     load_far.wait()
     load_near.wait()
     for copy in load_dqg:
         copy.wait()
+    for copy in loads[first_loads:]:
+        copy.start()
     far_swap.wait_recv()
     on_prompt = jnp.where(c == 0, 1.0, 0.0)
 
@@ -1440,6 +1467,27 @@
     c_copy = remote(c_send, c_land, c_send_sem.at[0], c_recv_sem.at[0], here.other("c"))
     c_copy.start()
 
+    load_gated.wait()
+    load_mixed.wait()
+    out_rows = slots * LANES
+
+    def out_tile(s, cols):
+        return tn_dot(gated[:, s * LANES : (s + 1) * LANES], mixed[:, cols])
+
+    for s in range(slots):
+        co_send[s * LANES : (s + 1) * LANES, :] = out_tile(
+            s, slice(2 * part, features)
+        ).astype(BF)
+    co_copy = remote(co_send, co_land, c_send_sem.at[1], c_recv_sem.at[1], here.other("c"))
+    co_copy.start()
+
+    zd_copy.wait_recv()
+    final_d[...] = (
+        kept_d[:units, :] + there_d[:units, :].astype(F32) + zd_land[...].astype(F32)
+    ).astype(BF)
+    for copy in own_pieces[2:] + y_pieces[2:]:
+        copy.start()
+
     load_weight.wait()
     tiles = 3
     tile_w = features // tiles
@@ -1459,22 +1507,19 @@
 
         lax.fori_loop(0, tiles, step, 0)
 
-    rs = []
-    for k in range(peers - 1, 0, -1):
+    moves = RingRows(here, local)
+
+    def rs_copy(i):
+        return moves.sum_copy(rs_send, rs_land, rs_send_sem, rs_recv_sem, i)
+
+    for k in (3, 1, 2):
 
         def store_out(cols, value, k=k):
             rs_send[k - 1, :, cols] = value.astype(BF)
 
-        partial_rows(ring.back[k], store_out)
-        copy = remote(
-            rs_send.at[k - 1],
-            rs_land.at[k - 1],
-            rs_send_sem.at[k - 1],
-            rs_recv_sem.at[k - 1],
-            here.peer(k),
-        )
-        copy.start()
-        rs.append(copy)
+        partial_rows(k, store_out)
+        for i in SUM_STARTS[k]:
+            rs_copy(i).start()
 
     c_copy.wait_recv()
 
@@ -1531,14 +1576,22 @@
     z_forget = z_copy(2, zf_send, zf_land)
     zo_first = z_copy(3, zo_send.at[0], zo_land.at[0])
     zo_mid = z_copy(4, zo_send.at[1], zo_land.at[1])
+    moves.hand_on(rs_send, rs_land, rs_send_sem, rs_recv_sem)
     x_copies[2].wait_recv()
     z_send[0] = (kept[2] + x_land[2].astype(F32)).astype(BF)
     z_first.start()
+    x_copies[1].wait_recv()
+
+    @pl.when(~owner)
+    def _():
+        z_send[1] = (kept[1] + x_land[1].astype(F32)).astype(BF)
+        z_mid.start()
+
 
     load_tokens.wait()
     load_residual.wait()
-    for copy in rs:
-        copy.wait_recv()
+    for i in (0, 2, 4, 5):
+        rs_copy(i).wait_recv()
     gain_sum[...] = jnp.zeros(gain_sum.shape, F32)
     tile_n = 32
 
@@ -1546,7 +1599,7 @@
         rows = pl.ds(pl.multiple_of(i * tile_n, tile_n), tile_n)
         tok = tokens[rows, :].astype(F32)
         grad = total[rows, :]
-        for k in range(peers - 1):
+        for k in (0, 2):
             grad = grad + rs_land[k, rows, :].astype(F32)
         factor = lax.rsqrt(jnp.mean(tok * tok, axis=-1, keepdims=True) + epsilon)
         scaled_tok = tok * factor
@@ -1592,115 +1645,6 @@
     def _():
         for p in range(2):
             back_own(0, p).start()
-
-    row0 = pl.multiple_of(c * part, part)
-
-    def rows_of(ref, col, width):
-        return ref.at[pl.ds(row0, part), pl.ds(pl.multiple_of(col, LANES), width)]
-
-    def cols_of(ref, row, height):
-        return ref.at[pl.ds(pl.multiple_of(row, LANES), height), pl.ds(row0, part)]
-
-    def y_copy(i, src, dst):
-        return remote(src, dst, y_send_sem.at[i], y_recv_sem.at[i], here.other("y"))
-
-    pieces = [
-        (hid_in.at[:, :units], rows_of(gate_out, y * units, units)),
-        (hid_in.at[:, units:], rows_of(up_out, y * units, units)),
-        (down_in, cols_of(down_out, y * units, units)),
-    ]
-    own_pieces = [
-        pltpu.make_async_copy(src, dst, local_sem.at[i]) for i, (src, dst) in enumerate(pieces)
-    ]
-    y_pieces = [y_copy(i, src, dst) for i, (src, dst) in enumerate(pieces)]
-    for copy in own_pieces + y_pieces:
-        copy.start()
-
-    x_copies[1].wait_recv()
-
-    @pl.when(~owner)
-    def _():
-        z_send[1] = (kept[1] + x_land[1].astype(F32)).astype(BF)
-        z_mid.start()
-
-    x_copies[0].wait_recv()
-    kept[0] += x_land[0].astype(F32)
-    xf_copy.wait_recv()
-    kept_f[...] += xf_land[...].astype(F32)
-    zf_send[...] = kept_f[...].astype(BF)
-    z_forget.start()
-    xo_copy.wait_recv()
-    kept_o[...] += xo_land[...].astype(F32)
-    zo_send[0] = kept_o[2 * LANES :, :].astype(BF)
-    zo_first.start()
-
-    @pl.when(~owner)
-    def _():
-        zo_send[1] = kept_o[LANES : 2 * LANES, :].astype(BF)
-        zo_mid.start()
-
-    first_dst = rows_of(proj_out, 2 * y * slot_w, slot_w)
-    mid_dst = rows_of(proj_out, slot_w, slot_w)
-    out_first_dst = cols_of(out_out, 2 * LANES * y, LANES)
-    out_mid_dst = cols_of(out_out, LANES, LANES)
-    y_first = y_copy(3, final.at[0], first_dst)
-    y_mid = y_copy(4, final.at[1], mid_dst)
-    y_forget = y_copy(5, final_f, yf_land)
-    yo_first = y_copy(6, final_o.at[0], out_first_dst)
-    yo_mid = y_copy(7, final_o.at[1], out_mid_dst)
-    own_first = pltpu.make_async_copy(final.at[0], first_dst, local_sem.at[8])
-    own_mid = pltpu.make_async_copy(final.at[1], mid_dst, local_sem.at[9])
-    own_out_first = pltpu.make_async_copy(final_o.at[0], out_first_dst, local_sem.at[10])
-    own_out_mid = pltpu.make_async_copy(final_o.at[1], out_mid_dst, local_sem.at[11])
-    own_forget = pltpu.make_async_copy(
-        full_f, proj_out.at[pl.ds(row0, part), all_w : all_w + LANES], local_sem.at[12]
-    )
-    z_first.wait_recv()
-    final[0] = (kept[0] + z_land[0].astype(F32)).astype(BF)
-    y_first.start()
-    own_first.start()
-
-    @pl.when(owner)
-    def _():
-        z_mid.wait_recv()
-        final[1] = (kept[1] + x_land[1].astype(F32) + z_land[1].astype(F32)).astype(BF)
-        y_mid.start()
-        own_mid.start()
-
-    z_forget.wait_recv()
-    f_lane = lax.broadcasted_iota(jnp.int32, (part, LANES), 1)
-    there_f = zf_land[...].astype(F32)
-    edge = jnp.where(f_lane < 2, kept_f[...] + pltpu.roll(there_f, LANES - 4, 1), 0.0)
-    edge = jnp.where(y == 0, edge, pltpu.roll(edge, 4, 1))
-    mid_f = jnp.where((f_lane >= 2) & (f_lane < 4) & owner, kept_f[...] + there_f, 0.0)
-    final_f[...] = (edge + mid_f).astype(BF)
-    y_forget.start()
-    zo_first.wait_recv()
-    final_o[0] = (kept_o[:LANES, :] + zo_land[0].astype(F32)).astype(BF)
-    yo_first.start()
-    own_out_first.start()
-
-    @pl.when(owner)
-    def _():
-        zo_mid.wait_recv()
-        final_o[1] = (kept_o[LANES : 2 * LANES, :] + zo_land[1].astype(F32)).astype(BF)
-        yo_mid.start()
-        own_out_mid.start()
-
-    for copy in own_pieces:
-        copy.wait()
-    for copy in y_pieces:
-        copy.wait_recv()
-    c2 = []
-
-    def hand_over(i, view):
-        copy = remote(view, view, c2_send_sem.at[i], c2_recv_sem.at[i], here.other("c"))
-        copy.start()
-        c2.append(copy)
-
-    hand_over(0, gate_out.at[pl.ds(row0, part), :])
-    hand_over(1, up_out.at[pl.ds(row0, part), :])
-    hand_over(2, down_out.at[:, pl.ds(row0, part)])
 
     for b in range(4):
         gain_sum[b, 1:2, :] = gain_two_ref[0:1, b * part : (b + 1) * part]
@@ -1722,21 +1666,111 @@
         value = jnp.sum(jnp.where(small_lane == j, bias, 0.0), axis=1, keepdims=True)
         scalars = scalars + jnp.where(wide_lane == dest, value, 0.0)
     gain_nat[0, 0, 2:3, :] = scalars
-    for place, axis in enumerate(("c", "y", "x", "zl", "zh")):
-        copy = remote(
+    gain_axes = ("c", "y", "x", "zl", "zh")
+
+    def gain_step(place):
+        return remote(
             gain_nat.at[place],
             gain_land.at[place],
             gain_send_sem.at[place],
             gain_recv_sem.at[place],
-            here.other(axis),
-        )
+            here.other(gain_axes[place]),
+        )
+
+    def gain_next(place):
+        gain_step(place).wait_recv()
+        gain_nat[place + 1] = gain_nat[place] + gain_land[place]
+        if place < 4:
+            gain_step(place + 1).start()
+
+    gain_step(0).start()
+
+    x_copies[0].wait_recv()
+    kept[0] += x_land[0].astype(F32)
+    gain_next(0)
+    xf_copy.wait_recv()
+    kept_f[...] += xf_land[...].astype(F32)
+    zf_send[...] = kept_f[...].astype(BF)
+    z_forget.start()
+    xo_copy.wait_recv()
+    kept_o[...] += xo_land[...].astype(F32)
+    gain_next(1)
+    zo_send[0] = kept_o[2 * LANES :, :].astype(BF)
+    zo_first.start()
+
+    @pl.when(~owner)
+    def _():
+        zo_send[1] = kept_o[LANES : 2 * LANES, :].astype(BF)
+        zo_mid.start()
+
+    first_dst = rows_of(proj_out, 2 * y * slot_w, slot_w)
+    mid_dst = rows_of(proj_out, slot_w, slot_w)
+    out_first_dst = cols_of(out_out, 2 * LANES * y, LANES)
+    out_mid_dst = cols_of(out_out, LANES, LANES)
+    y_first = y_copy(3, final.at[0], first_dst)
+    y_mid = y_copy(4, final.at[1], mid_dst)
+    y_forget = y_copy(5, final_f, yf_land)
+    yo_first = y_copy(6, final_o.at[0], out_first_dst)
+    yo_mid = y_copy(7, final_o.at[1], out_mid_dst)
+    own_first = pltpu.make_async_copy(final.at[0], first_dst, local_sem.at[8])
+    own_mid = pltpu.make_async_copy(final.at[1], mid_dst, local_sem.at[9])
+    own_out_first = pltpu.make_async_copy(final_o.at[0], out_first_dst, local_sem.at[10])
+    own_out_mid = pltpu.make_async_copy(final_o.at[1], out_mid_dst, local_sem.at[11])
+    own_forget = pltpu.make_async_copy(
+        full_f, proj_out.at[pl.ds(row0, part), all_w : all_w + LANES], local_sem.at[12]
+    )
+    z_first.wait_recv()
+    final[0] = (kept[0] + z_land[0].astype(F32)).astype(BF)
+    y_first.start()
+    own_first.start()
+
+    @pl.when(owner)
+    def _():
+        z_mid.wait_recv()
+        final[1] = (kept[1] + x_land[1].astype(F32) + z_land[1].astype(F32)).astype(BF)
+        y_mid.start()
+        own_mid.start()
+
+    gain_next(2)
+    z_forget.wait_recv()
+    f_lane = lax.broadcasted_iota(jnp.int32, (part, LANES), 1)
+    there_f = zf_land[...].astype(F32)
+    edge = jnp.where(f_lane < 2, kept_f[...] + pltpu.roll(there_f, LANES - 4, 1), 0.0)
+    edge = jnp.where(y == 0, edge, pltpu.roll(edge, 4, 1))
+    mid_f = jnp.where((f_lane >= 2) & (f_lane < 4) & owner, kept_f[...] + there_f, 0.0)
+    final_f[...] = (edge + mid_f).astype(BF)
+    y_forget.start()
+    gain_next(3)
+    zo_first.wait_recv()
+    final_o[0] = (kept_o[:LANES, :] + zo_land[0].astype(F32)).astype(BF)
+    yo_first.start()
+    own_out_first.start()
+
+    @pl.when(owner)
+    def _():
+        zo_mid.wait_recv()
+        final_o[1] = (kept_o[LANES : 2 * LANES, :] + zo_land[1].astype(F32)).astype(BF)
+        yo_mid.start()
+        own_out_mid.start()
+
+    for copy in own_pieces:
+        copy.wait()
+    for copy in y_pieces:
+        copy.wait_recv()
+    c2 = []
+
+    def hand_over(i, view):
+        copy = remote(view, view, c2_send_sem.at[i], c2_recv_sem.at[i], here.other("c"))
         copy.start()
-        copy.wait_recv()
-        gain_nat[place + 1] = gain_nat[place] + gain_land[place]
-        copy.wait_send()
+        c2.append(copy)
+
+    hand_over(0, gate_out.at[pl.ds(row0, part), :])
+    hand_over(1, up_out.at[pl.ds(row0, part), :])
+    hand_over(2, down_out.at[:, pl.ds(row0, part)])
+
+    gain_next(4)
     gain_copy = pltpu.make_async_copy(gain_nat.at[5], small_out, local_sem.at[7])
     gain_copy.start()
-
     y_forget.wait_recv()
     full_f[...] = final_f[...] + yf_land[...]
     own_forget.start()
@@ -1775,9 +1809,13 @@
             back_own(0, p).wait()
 
     gain_copy.wait()
-    for copy in rs + [c_copy, co_copy, x_copies[0], x_copies[1], x_copies[2], xf_copy, xo_copy]:
+    for i in range(5):
+        gain_step(i).wait_send()
+    for i in range(6):
+        rs_copy(i).wait_send()
+    for copy in [c_copy, co_copy, x_copies[0], x_copies[1], x_copies[2], xf_copy, xo_copy]:
         copy.wait_send()
-    for copy in [far_swap, col_swap, tot_swap, z_first, z_forget, zo_first]:
+    for copy in [far_swap, col_swap, tot_swap, z_first, z_forget, zo_first, zd_copy]:
         copy.wait_send()
     for copy in y_pieces + [y_first, y_forget, yo_first]:
         copy.wait_send()
@@ -1798,7 +1836,7 @@
     rows = near.shape[0]
     weight, normed, gated = large[6:9]
     tokens = large[10]
-    units = large[13].shape[0]
+    units = large[13].shape[0] // 2
     local, features = tokens.shape
     part = features // 4
     half = features // 2
@@ -1861,6 +1899,11 @@
             vmem((part, LANES), BF),
             vmem((slots * LANES, half), BF),
             vmem((slots * LANES, half), BF),
+            vmem((2 * units, part), F32),
+            vmem((2 * units, part), BF),
+            vmem((units, part), BF),
+            vmem((units, part), BF),
+            vmem((units, part), BF),
             vmem((slots * LANES, part), F32),
             vmem((slots * LANES, part), BF),
             vmem((slots * LANES, part), BF),
@@ -1871,7 +1914,7 @@
             vmem((4, 8, part), F32),
             vmem((6, 4, 8, part), F32),
             vmem((5, 4, 8, part), F32),
-            dma((11 + slots,)),
+            dma((13 + slots,)),
             dma((13,)),
             dma((3,)),
             dma((3,)),
@@ -1879,14 +1922,14 @@
             dma((8,)),
             dma((5,)),
             dma((5,)),
-            dma((peers - 1,)),
-            dma((peers - 1,)),
+            dma((6,)),
+            dma((6,)),
             dma((2,)),
             dma((2,)),
             dma((5,)),
             dma((5,)),
-            dma((5,)),
-            dma((5,)),
+            dma((6,)),
+            dma((6,)),
             dma((2, 2)),
             dma((2, 2)),
             dma((5,)),
@@ -1901,11 +1944,68 @@
     )(*large, *small)
 
 
+def scale_kernel(
+    full,
+    sums,
+    back,
+    proj,
+    gate,
+    up,
+    down,
+    out,
+    prompt_o,
+    cont_o,
+    query_o,
+    outgate_o,
+    key_o,
+    value_o,
+    gate_o,
+    up_o,
+    down_o,
+    out_o,
+):
+    factor = full / sums[0, 2:3, 1:2]
+    prompt_o[...] = back[0].astype(F32) * factor
+    cont_o[...] = back[1].astype(F32) * factor
+    for i, ref in enumerate((query_o, outgate_o, key_o, value_o)):
+        for s in range(3):
+            at = (4 * s + i) * LANES
+            ref[:, s * LANES : (s + 1) * LANES] = proj[:, at : at + LANES].astype(F32) * factor
+    gate_o[...] = gate[...].astype(F32) * factor
+    up_o[...] = up[...].astype(F32) * factor
+    down_o[...] = down[...].astype(F32) * factor
+    out_o[...] = out[...].astype(F32) * factor
+
+
+def scale_step(full, sums, back, proj, gate, up, down, out):
+    steps = 8
+
+    def cut(shape):
+        return row_block(shape[0] // steps, shape[1])
+
+    local, half = back.shape[1:]
+    width = out.shape[0]
+    shapes = [(local, half)] * 2 + [(half, width)] * 4 + [gate.shape, up.shape, down.shape, out.shape]
+    return pl.pallas_call(
+        functools.partial(scale_kernel, full),
+        grid=(steps,),
+        out_shape=tuple(jax.ShapeDtypeStruct(v, F32) for v in shapes),
+        in_specs=[
+            pl.BlockSpec(sums.shape, lambda i: (0, 0, 0)),
+            pl.BlockSpec((2, local // steps, half), lambda i: (0, i, 0)),
+        ]
+        + [cut(v.shape) for v in (proj, gate, up, down, out)],
+        out_specs=tuple(cut(v) for v in shapes),
+        compiler_params=pltpu.CompilerParams(vmem_limit_bytes=62 << 20),
+    )(sums, back, proj, gate, up, down, out)
+
+
 def middle_kernel(
     ring,
     gated_in,
     w_out_in,
-    hid_own_in,
+    w_gate_in,
+    w_up_in,
     hid_there_in,
     w_down_in,
     tokens_in,
@@ -1974,8 +2074,14 @@
     half_units = units // 2
     part = features // 4
     peers = len(ring.offsets)
-    order = list(range(peers - 1, 0, -1))
     y, c, x = (here.at[a] for a in ("y", "c", "x"))
+    gate_view, up_view = (
+        w.at[
+            pl.ds(pl.multiple_of(c * part, part), part),
+            pl.ds(pl.multiple_of(y * half_units, half_units), half_units),
+        ]
+        for w in (w_gate_in, w_up_in)
+    )
     down_view = w_down_in.at[
         pl.ds(pl.multiple_of(y * half_units, half_units), half_units),
         pl.ds(pl.multiple_of(c * part, part), part),
@@ -1985,7 +2091,8 @@
         pltpu.make_async_copy(a, b, load_sem.at[i])
         for i, (a, b) in enumerate(
             (
-                (hid_own_in, w_hidden.at[0:part, 0:units]),
+                (gate_view, w_hidden.at[0:part, 0:half_units]),
+                (up_view, w_hidden.at[0:part, half_units:units]),
                 (hid_there_in, w_hidden.at[0:part, units:]),
                 (gated_in, gated),
                 (w_out_in, w_out),
@@ -2002,12 +2109,12 @@
     )
 
     z_down = remote(
-        down_view, w_down.at[half_units:, 0:part], wz_send, wz_recv, here.other("zh")
+        down_view, w_down.at[half_units:, 0:part], wz_send.at[0], wz_recv.at[0], here.other("zh")
     )
     z_down.start()
 
     def hid_x_copy(i):
-        cols = slice(i * units, (i + 1) * units)
+        cols = slice(i * half_units, (i + 1) * half_units) if i < 2 else slice(units, 2 * units)
         return remote(
             w_hidden.at[0:part, cols],
             w_hidden.at[part : 2 * part, cols],
@@ -2017,7 +2124,7 @@
         )
 
     def hid_c_copy(i):
-        cols = slice(i * units, (i + 1) * units)
+        cols = slice(i * half_units, (i + 1) * half_units) if i < 2 else slice(units, 2 * units)
         return remote(
             w_hidden.at[0 : 2 * part, cols],
             w_hidden.at[2 * part :, cols],
@@ -2026,7 +2133,7 @@
             here.other("c"),
         )
 
-    for i in range(2):
+    for i in range(3):
         loads[i].wait()
         hid_x_copy(i).start()
 
@@ -2044,7 +2151,7 @@
                     )
                 )
             else:
-                out.append(pltpu.make_async_copy(src, dst, load_sem.at[6 + p]))
+                out.append(pltpu.make_async_copy(src, dst, load_sem.at[7 + p]))
         return out
 
     away = here.group_away()
@@ -2093,23 +2200,13 @@
 
         lax.fori_loop(0, count, body, 0)
 
-    def rs_copy(phase, j):
-        return remote(
-            rs_send.at[j - 1],
-            rs_land.at[j - 1],
-            rs_send_sem.at[phase, j - 1],
-            rs_recv_sem.at[phase, j - 1],
-            here.peer(j),
-        )
-
-    def ag_copy(phase, buffer, k):
-        return remote(
-            buffer.at[chunk(0)],
-            buffer.at[chunk(k)],
-            ag_send_sem.at[phase, k - 1],
-            ag_recv_sem.at[phase, k - 1],
-            here.peer(k),
-        )
+    moves = RingRows(here, local)
+
+    def rs_copy(phase, i):
+        return moves.sum_copy(rs_send, rs_land, rs_send_sem.at[phase], rs_recv_sem.at[phase], i)
+
+    def ag_copy(phase, buffer, i):
+        return moves.gather_copy(buffer, ag_send_sem.at[phase], ag_recv_sem.at[phase], i)
 
     wide = 512
     wide_count = features // wide
@@ -2123,40 +2220,64 @@
             if k == 0:
                 total[:, cols] = value
             else:
-                rs_send[ring.back[k] - 1, :, cols] = value.astype(BF)
+                rs_send[k - 1, :, cols] = value.astype(BF)
 
         if k != 0 and phase > 0:
-            rs_copy(phase - 1, ring.back[k]).wait_send()
+            for i in SUM_READS[k]:
+                rs_copy(phase - 1, i).wait_send()
         tiled(wide_count, wide, step)
         if k != 0:
-            rs_copy(phase, ring.back[k]).start()
-
-    def row_tiles(step):
-        tiled(local // 32, 32, step)
+            for i in SUM_STARTS[k]:
+                rs_copy(phase, i).start()
+
+    def hand_on(phase):
+        moves.hand_on(rs_send, rs_land, rs_send_sem.at[phase], rs_recv_sem.at[phase])
+
+    def sums_arrived(phase):
+        for i in (0, 2, 4, 5):
+            rs_copy(phase, i).wait_recv()
+
+    def half_tiles(phase, buffer, step):
+        for half in range(2):
+
+            def body(i, carry):
+                step(pl.ds(pl.multiple_of(half * (local // 2) + i * 32, 32), 32))
+                return carry
+
+            lax.fori_loop(0, local // 64, body, 0)
+            ag_copy(phase, buffer, half).start()
+            ag_copy(phase, buffer, 2 + half).start()
+
+    def pass_on(phase, buffer):
+        ag_copy(phase, buffer, 2).wait_recv()
+        ag_copy(phase, buffer, 4).start()
+        ag_copy(phase, buffer, 1).wait_recv()
+        ag_copy(phase, buffer, 5).start()
+
+    def rows_arrived(phase, buffer, k):
+        for i in {1: (0,), 2: (3,), 3: (4, 5)}[k]:
+            ag_copy(phase, buffer, i).wait_recv()
 
     def summed(rows):
-        value = total[rows, :]
-        for j in range(1, peers):
-            value = value + rs_land[j - 1, rows, :].astype(F32)
-        return value
-
-    loads[2].wait()
+        return total[rows, :] + rs_land[0, rows, :].astype(F32) + rs_land[2, rows, :].astype(F32)
+
     loads[3].wait()
-    for k in order + [0]:
+    loads[4].wait()
+    for k in (3, 1, 2, 0):
         send_partial(0, k, gated[chunk(k), :], w_out, False)
-    loads[4].wait()
     loads[5].wait()
+    loads[6].wait()
     z_down.wait_recv()
     down_x_copy = remote(
         w_down.at[:, 0:part],
         w_down.at[:, part : 2 * part],
-        wx_send.at[2],
-        wx_recv.at[2],
+        wx_send.at[4],
+        wx_recv.at[4],
         here.other("x"),
     )
     down_x_copy.start()
-    for j in range(1, peers):
-        rs_copy(0, j).wait_recv()
+    hand_on(0)
+    sums_arrived(0)
 
     def second_norm(rows):
         value = tokens[rows, :].astype(F32) + summed(rows)
@@ -2164,26 +2285,15 @@
         factor = lax.rsqrt(jnp.mean(value * value, axis=-1, keepdims=True) + epsilon)
         normed[rows, :] = (value * factor * gain_ref[...]).astype(BF)
 
-    row_tiles(second_norm)
-    for k in order:
-        ag_copy(0, normed, k).start()
-
-    for i in range(2):
+    half_tiles(0, normed, second_norm)
+
+    for i in range(3):
         hid_x_copy(i).wait_recv()
         hid_c_copy(i).start()
     for f in range(2):
         on_teacher(f, True, lambda copy: copy.start())
-    for i in range(2):
+    for i in range(3):
         hid_c_copy(i).wait_recv()
-    down_x_copy.wait_recv()
-    down_c_copy = remote(
-        w_down.at[:, 0 : 2 * part],
-        w_down.at[:, 2 * part :],
-        wc_send.at[2],
-        wc_recv.at[2],
-        here.other("c"),
-    )
-    down_c_copy.start()
     tile_u = 256
     per_half = half_units // tile_u
 
@@ -2205,14 +2315,29 @@
             return carry
 
         lax.fori_loop(0, 2 * per_half, step, 0)
-        if k == 0:
+
+    def forward_sum(k):
+        send_partial(1, k, hidden[chunk(k), :], w_down, False)
+
+    forward_chunk(0)
+    pass_on(0, normed)
+    down_x_copy.wait_recv()
+    down_c_copy = remote(
+        w_down.at[:, 0 : 2 * part],
+        w_down.at[:, 2 * part :],
+        wc_send.at[4],
+        wc_recv.at[4],
+        here.other("c"),
+    )
+    down_c_copy.start()
+    for k in range(1, peers):
+        rows_arrived(0, normed, k)
+        forward_chunk(k)
+        if k == 1:
             down_c_copy.wait_recv()
-        send_partial(1, k, hidden[chunk(k), :], w_down, False)
-
-    forward_chunk(0)
-    for k in range(1, peers):
-        ag_copy(0, normed, k).wait_recv()
-        forward_chunk(k)
+        forward_sum(k)
+    forward_sum(0)
+    hand_on(1)
     teacher_arrival(1)
 
     @pl.when(away)
@@ -2228,8 +2353,7 @@
                 for copy in teach_copies(0, rows_in, False):
                     copy.wait()
 
-    for j in range(1, peers):
-        rs_copy(1, j).wait_recv()
+    sums_arrived(1)
     error_ref[...] = jnp.zeros(error_ref.shape, F32)
     gain_grad[...] = jnp.zeros(gain_grad.shape, F32)
 
@@ -2240,9 +2364,7 @@
         result_all[rows, :] = grad.astype(BF)
         error_ref[0:1, :] += 0.5 * jnp.sum(grad * deviation, axis=0, keepdims=True)
 
-    row_tiles(loss_rows)
-    for k in order:
-        ag_copy(1, result_all, k).start()
+    half_tiles(1, result_all, loss_rows)
 
     def backward_chunk(k):
         left = result_all[chunk(k), :]
@@ -2263,17 +2385,36 @@
             return carry
 
         lax.fori_loop(0, 2 * per_half, step, 0)
+
+    def backward_sum(k):
         send_partial(2, k, gate_up[chunk(k), :], w_hidden, True)
 
     backward_chunk(0)
+    pass_on(1, result_all)
     for k in range(1, peers):
-        ag_copy(1, result_all, k).wait_recv()
+        rows_arrived(1, result_all, k)
         backward_chunk(k)
+        backward_sum(k)
 
     unit_tile = 256
 
     def down_tile(units_at, cols):
         return tn_dot(hidden[:, units_at], result_all[:, cols])
+
+    feature_tile = 128
+
+    def hid_tile(first, at):
+        cols = pl.ds(pl.multiple_of(first + at.start, feature_tile), feature_tile)
+        return tn_dot(normed[:, cols], gate_up[...])
+
+    def hid_c(at):
+        c_hid_send[at, :] = hid_tile(2 * part, at).astype(BF)
+
+    tiled(2 * part // feature_tile, feature_tile, hid_c)
+    c_hid = remote(c_hid_send, c_hid_land, c_send_sem.at[1], c_recv_sem.at[1], here.other("c"))
+    c_hid.start()
+    hand_on(2)
+    backward_sum(0)
 
     def down_c(units_at):
         c_down_send[units_at, :] = down_tile(units_at, slice(2 * part, features)).astype(BF)
@@ -2281,30 +2422,17 @@
     tiled(units // unit_tile, unit_tile, down_c)
     c_down = remote(c_down_send, c_down_land, c_send_sem.at[0], c_recv_sem.at[0], here.other("c"))
     c_down.start()
-    feature_tile = 128
-
-    def hid_tile(first, at):
-        cols = pl.ds(pl.multiple_of(first + at.start, feature_tile), feature_tile)
-        return tn_dot(normed[:, cols], gate_up[...])
-
-    def hid_c(at):
-        c_hid_send[at, :] = hid_tile(2 * part, at).astype(BF)
-
-    tiled(2 * part // feature_tile, feature_tile, hid_c)
-    c_hid = remote(c_hid_send, c_hid_land, c_send_sem.at[1], c_recv_sem.at[1], here.other("c"))
-    c_hid.start()
-    c_down.wait_recv()
-
-    def down_x(units_at):
-        value = down_tile(units_at, slice(part, 2 * part))
-        x_down_send[units_at, :] = (value + c_down_land[units_at, part:].astype(F32)).astype(BF)
-
-    tiled(units // unit_tile, unit_tile, down_x)
-    x_down = remote(x_down_send, down_there, x_send_sem.at[0], x_recv_sem.at[0], here.other("x"))
-    x_down.start()
-
-    for j in range(1, peers):
-        rs_copy(2, j).wait_recv()
+    c_hid.wait_recv()
+
+    def hid_x(at):
+        land = pl.ds(pl.multiple_of(part + at.start, feature_tile), feature_tile)
+        x_hid_send[at, :] = (hid_tile(part, at) + c_hid_land[land, :].astype(F32)).astype(BF)
+
+    tiled(part // feature_tile, feature_tile, hid_x)
+    x_hid = remote(x_hid_send, hid_there, x_send_sem.at[1], x_recv_sem.at[1], here.other("x"))
+    x_hid.start()
+
+    sums_arrived(2)
 
     def norm_back(rows):
         value = mixed[rows, :]
@@ -2318,26 +2446,22 @@
         mixed_all[rows, :] = out.astype(BF)
         gain_grad[0:1, :] += jnp.sum(grad * scaled_rows, axis=0, keepdims=True)
 
-    row_tiles(norm_back)
-    for k in order:
-        ag_copy(2, mixed_all, k).start()
+    half_tiles(2, mixed_all, norm_back)
     residual_copy = pltpu.make_async_copy(result_grad, residual_grad, out_sem.at[0])
     residual_copy.start()
 
-    c_hid.wait_recv()
-
-    def hid_x(at):
-        land = pl.ds(pl.multiple_of(part + at.start, feature_tile), feature_tile)
-        x_hid_send[at, :] = (hid_tile(part, at) + c_hid_land[land, :].astype(F32)).astype(BF)
-
-    tiled(part // feature_tile, feature_tile, hid_x)
-    x_hid = remote(x_hid_send, hid_there, x_send_sem.at[1], x_recv_sem.at[1], here.other("x"))
-    x_hid.start()
-
     def gated_chunk(k):
         gg_stage[chunk(k), :] = nt_dot(mixed_all[chunk(k), :], w_out[...])
 
     gated_chunk(0)
+    c_down.wait_recv()
+
+    def down_x(units_at):
+        value = down_tile(units_at, slice(part, 2 * part))
+        x_down_send[units_at, :] = (value + c_down_land[units_at, part:].astype(F32)).astype(BF)
+
+    tiled(units // unit_tile, unit_tile, down_x)
+    pass_on(2, mixed_all)
 
     def down_own(units_at):
         value = down_tile(units_at, slice(0, part))
@@ -2352,11 +2476,12 @@
     sums_out = [
         pltpu.make_async_copy(down_sum, down_kept, out_sem.at[1]),
         pltpu.make_async_copy(hid_sum, hid_kept, out_sem.at[2]),
+        pltpu.make_async_copy(x_down_send, down_there, out_sem.at[5]),
     ]
     for copy in sums_out:
         copy.start()
     for k in range(1, peers):
-        ag_copy(2, mixed_all, k).wait_recv()
+        rows_arrived(2, mixed_all, k)
         gated_chunk(k)
     finals = [
         pltpu.make_async_copy(gg_stage, gated_grad, out_sem.at[3]),
@@ -2364,20 +2489,20 @@
     ]
     for copy in finals:
         copy.start()
-    for k in range(1, peers):
-        rs_copy(2, k).wait_send()
+    for i in range(6):
+        rs_copy(2, i).wait_send()
         for phase, buffer in enumerate((normed, result_all, mixed_all)):
-            ag_copy(phase, buffer, k).wait_send()
+            ag_copy(phase, buffer, i).wait_send()
     c_down.wait_send()
     c_hid.wait_send()
     z_down.wait_send()
-    for i in range(2):
+    for i in range(3):
         hid_x_copy(i).wait_send()
         hid_c_copy(i).wait_send()
-        on_teacher(i, False, lambda copy: copy.wait_send())
+    for f in range(2):
+        on_teacher(f, False, lambda copy: copy.wait_send())
     down_x_copy.wait_send()
     down_c_copy.wait_send()
-    x_down.wait()
     x_hid.wait()
     residual_copy.wait()
     for copy in sums_out + finals:
@@ -2388,7 +2513,8 @@
     ring,
     gated,
     w_out,
-    hid_own,
+    w_gate,
+    w_up,
     hid_there,
     w_down,
     tokens,
@@ -2418,7 +2544,7 @@
             jax.ShapeDtypeStruct((8, features), F32),
             jax.ShapeDtypeStruct((8, features), F32),
         ),
-        in_specs=[any_spec] * 8 + [vmem_spec] * 2,
+        in_specs=[any_spec] * 9 + [vmem_spec] * 2,
         out_specs=[any_spec] * 7 + [vmem_spec] * 2,
         scratch_shapes=[
             pltpu.VMEM(gated.shape, BF),
@@ -2446,20 +2572,20 @@
             pltpu.VMEM((units, part), F32),
             pltpu.VMEM((part, 2 * units), F32),
             pltpu.VMEM((rows, width), F32),
-            dma((8,)),
-            dma((3,)),
-            dma((3,)),
-            dma((3,)),
-            dma((3,)),
-            dma,
-            dma,
+            dma((9,)),
+            dma((5,)),
+            dma((5,)),
+            dma((5,)),
+            dma((5,)),
+            dma((2,)),
+            dma((2,)),
             dma((2, 2)),
             dma((2, 2)),
-            dma((5,)),
-            dma((3, peers - 1)),
-            dma((3, peers - 1)),
-            dma((3, peers - 1)),
-            dma((3, peers - 1)),
+            dma((6,)),
+            dma((3, 6)),
+            dma((3, 6)),
+            dma((3, 6)),
+            dma((3, 6)),
             dma((2,)),
             dma((2,)),
             dma((2,)),
@@ -2476,7 +2602,8 @@
     )(
         gated,
         w_out,
-        hid_own,
+        w_gate,
+        w_up,
         hid_there,
         w_down,
         tokens,
@@ -2485,6 +2612,66 @@
         valid,
         gain,
     )
+
+
+class RingRows:
+    def __init__(self, here, local):
+        self.zl, self.y = here.peer(1), here.peer(2)
+        self.local = local
+        self.half = local // 2
+
+    def rows(self, place, half=None):
+        base = place * self.local
+        if half is None:
+            return slice(base, base + self.local)
+        return slice(base + half * self.half, base + (half + 1) * self.half)
+
+    def gather_copy(self, buffer, sends, recvs, i):
+        source, target, place, half = (
+            (0, self.zl, 1, 0),
+            (0, self.zl, 1, 1),
+            (0, self.y, 2, 0),
+            (0, self.y, 2, 1),
+            (2, self.zl, 3, 0),
+            (1, self.y, 3, 1),
+        )[i]
+        return remote(
+            buffer.at[self.rows(source, half)],
+            buffer.at[self.rows(place, half)],
+            sends.at[i],
+            recvs.at[i],
+            target,
+        )
+
+    def sum_copy(self, send, land, sends, recvs, i):
+        chunk, half, target, slot = (
+            (0, 0, self.zl, 0),
+            (2, 0, self.zl, 1),
+            (1, 1, self.y, 0),
+            (2, 1, self.y, 1),
+            (1, 0, self.y, 2),
+            (0, 1, self.zl, 2),
+        )[i]
+        return remote(
+            send.at[chunk, self.rows(0, half)],
+            land.at[slot, self.rows(0, half)],
+            sends.at[i],
+            recvs.at[i],
+            target,
+        )
+
+    def hand_on(self, send, land, sends, recvs):
+        for chunk, half, got, i in ((1, 0, 1, 4), (0, 1, 3, 5)):
+            self.sum_copy(send, land, sends, recvs, got).wait_recv()
+            rows = self.rows(0, half)
+            send[chunk, rows, :] = (
+                send[chunk, rows, :].astype(F32) + land[1, rows, :].astype(F32)
+            ).astype(BF)
+            self.sum_copy(send, land, sends, recvs, i).start()
+
+
+SUM_STARTS = {1: (0,), 2: (2,), 3: (1, 3)}
+SUM_READS = {1: (0, 5), 2: (2, 4), 3: (1, 3)}
 
 
 def first_kernel(
@@ -2614,6 +2801,16 @@
     def _():
         ints_own().start()
 
+    def z_piece(i, s):
+        start = first0 if s == 2 else LANES
+        return remote(
+            sources[i].at[pl.ds(row0, part), pl.ds(start, LANES)],
+            slot_w.at[s, 0:part, i * LANES : (i + 1) * LANES],
+            z_send.at[s, i],
+            z_recv.at[s, i],
+            here.other("zh"),
+        )
+
     own_small = pltpu.make_async_copy(small_in, small.at[0], own_sem.at[15])
     own_small.start()
     small_z = remote(small_in, small.at[1], small_send.at[0], small_recv.at[0], here.other("zh"))
@@ -2694,14 +2891,6 @@
     forget_w[...] = jnp.zeros(forget_w.shape, BF)
     forget_w[0:16, :] = forget_f[...].astype(BF)
 
-    for f in range(2):
-        for p in range(2):
-            pass
-
-    def arrived(copy):
-        if hasattr(copy, "wait_recv"):
-            copy.wait_recv()
-
     def group_arrival(flip):
         for p in range(2):
             remote(
@@ -2726,16 +2915,6 @@
             def _():
                 for copy in group_copies(0, rows_in, False):
                     copy.wait()
-
-    def z_piece(i, s):
-        start = first0 if s == 2 else LANES
-        return remote(
-            sources[i].at[pl.ds(row0, part), pl.ds(start, LANES)],
-            slot_w.at[s, 0:part, i * LANES : (i + 1) * LANES],
-            z_send.at[s, i],
-            z_recv.at[s, i],
-            here.other("zh"),
-        )
 
     for i in range(4):
         z_piece(i, 2).start()
@@ -2767,6 +2946,11 @@
     def _():
         z_out[1].start()
 
+    moves = RingRows(here, local)
+
+    def ag_copy(i):
+        return moves.gather_copy(normed, ag_send, ag_recv, i)
+
     def norm_rows(i, carry):
         rows = pl.ds(pl.multiple_of(i * 32, 32), 32)
         value = tokens[rows, :].astype(F32)
@@ -2774,19 +2958,10 @@
         normed[rows, :] = (value * factor * feats[0, 0:1, :]).astype(BF)
         return carry
 
-    lax.fori_loop(0, local // 32, norm_rows, 0)
-
-    def ag_copy(k):
-        return remote(
-            normed.at[0:local],
-            normed.at[k * local : (k + 1) * local],
-            ag_send.at[k - 1],
-            ag_recv.at[k - 1],
-            here.peer(k),
-        )
-
-    for k in range(peers - 1, 0, -1):
-        ag_copy(k).start()
+    for place in range(2):
+        lax.fori_loop(place * (local // 64), (place + 1) * (local // 64), norm_rows, 0)
+        ag_copy(place).start()
+        ag_copy(2 + place).start()
 
     outs = [
         pltpu.make_async_copy(tokens, tokens_out, out_sem.at[0]),
@@ -2850,8 +3025,13 @@
     c_copy(0).wait_recv()
     forget_chunk(0)
     project_chunk(0, 0)
-    for k in range(1, peers):
-        ag_copy(k).wait_recv()
+    ag_copy(2).wait_recv()
+    ag_copy(4).start()
+    ag_copy(1).wait_recv()
+    ag_copy(5).start()
+    for k, arrivals in ((1, (0,)), (2, (3,)), (3, (4, 5))):
+        for i in arrivals:
+            ag_copy(i).wait_recv()
         forget_chunk(k)
         project_chunk(k, 0)
     normed_copy = pltpu.make_async_copy(normed, normed_out, out_sem.at[4])
@@ -2931,8 +3111,8 @@
         x_copy(s).wait_send()
         c_copy(s).wait_send()
     x_out.wait_send()
-    for k in range(1, peers):
-        ag_copy(k).wait_send()
+    for i in range(6):
+        ag_copy(i).wait_send()
     for k in range(peers):
         for s in range(3):
             kv_copy(k, s).wait()
@@ -2998,14 +3178,14 @@
             dma((4,)),
             dma((4,)),
             dma((4,)),
-            dma((peers - 1,)),
-            dma((peers - 1,)),
+            dma((6,)),
+            dma((6,)),
             dma((peers, 4)),
             dma((peers, 4)),
             dma((10,)),
         ],
         compiler_params=pltpu.CompilerParams(
-            collective_id=3, has_side_effects=True, vmem_limit_bytes=48 << 20
+            collective_id=3, has_side_effects=True, vmem_limit_bytes=62 << 20
         ),
         cost_estimate=pl.CostEstimate(
             flops=2 * rows * features * 3 * slot, bytes_accessed=40 << 20, transcendentals=0
@@ -3123,16 +3303,18 @@
     bias_row = head_slots(bias_all[:, :, None])[:, 0]
     bias_row = jnp.concatenate([bias_row, jnp.zeros((LANES - heads,), F32)])[None]
 
-    proj_a, w_gate, w_up = lax.optimization_barrier((proj_a, w_gate, w_up))
+    proj_a, w_gate_late, w_up_late = lax.optimization_barrier((proj_a, w_gate, w_up))
     projects[0] = proj_a
-    hid_own = jnp.concatenate(
-        [
-            lax.dynamic_slice(w, (c * part_d, y * half_units), (part_d, half_units))
-            for w in (w_gate, w_up)
-        ],
-        axis=1,
-    )
-    hid_there_w = ring.swap(hid_own, "zh")
+    hid_there_w = ring.swap(
+        jnp.concatenate(
+            [
+                lax.dynamic_slice(w, (c * part_d, y * half_units), (part_d, half_units))
+                for w in (w_gate_late, w_up_late)
+            ],
+            axis=1,
+        ),
+        "zh",
+    )
 
     dy_all = jnp.array([o[0] for o in ring.offsets], jnp.int32)
     dz_all = jnp.array([o[1] for o in ring.offsets], jnp.int32)
@@ -3224,7 +3406,8 @@
         ring,
         gated,
         w_out_all,
-        hid_own,
+        w_gate,
+        w_up,
         hid_there_w,
         w_down,
         tokens_b,
@@ -3259,7 +3442,7 @@
         return low(mine + ring.swap(theirs.astype(BF), "zh").astype(F32))
 
     hid_mine = over_zh(hid_kept + hid_there.astype(F32), 1)
-    down_mine = over_zh(down_kept + down_there.astype(F32), 0)
+    down_there = ring.swap(down_there, "x")
     rows_back, proj_all, gate_all, up_all, down_all, out_all, small_sums = last_step(
         ring,
         heads,
@@ -3277,7 +3460,8 @@
             tokens_b,
             grad_residual,
             hid_mine,
-            down_mine,
+            down_kept,
+            down_there,
         ],
         [
             gain_one[None],
@@ -3292,19 +3476,33 @@
     gain_one_sum = small_sums[:, 0].reshape(-1)
     gain_two_sum = small_sums[:, 1].reshape(-1)
     sums = small_sums[0, 2]
-    projection_grads = [
-        jnp.concatenate(
-            [proj_all[:, (4 * s + i) * LANES : (4 * s + i + 1) * LANES] for s in range(slots)],
-            axis=1,
-        )
-        for i in range(4)
-    ]
     forget_grad = proj_all[:, 4 * width : 4 * width + heads]
     error_total = sums[0]
     count_total = sums[1]
     groups = ring.sizes["yo"] * ring.sizes["y"] * ring.sizes["c"]
     grad_scale = groups * (PROMPT + CONTS * CLEN) / count_total
     loss_value = error_total / (D * count_total)
+    (
+        prompt_grad,
+        cont_grad,
+        query_grad,
+        outgate_grad,
+        key_grad,
+        value_grad,
+        gate_grad,
+        up_grad,
+        down_grad,
+        out_grad,
+    ) = scale_step(
+        float(groups * (PROMPT + CONTS * CLEN)),
+        small_sums,
+        rows_back,
+        proj_all,
+        gate_all,
+        up_all,
+        down_all,
+        out_all,
+    )
 
     def own_half(value):
         return lax.dynamic_slice_in_dim(value, x * half_d, half_d, value.ndim - 1)
@@ -3317,20 +3515,20 @@
 
     return (
         loss_value,
-        scaled(rows_back[0])[None],
-        scaled(rows_back[1]).reshape(1, local_conts, CLEN, half_d),
+        prompt_grad[None],
+        cont_grad.reshape(1, local_conts, CLEN, half_d),
         scaled(own_half(gain_one_sum)),
-        scaled(projection_grads[0]),
-        scaled(projection_grads[2]),
-        scaled(projection_grads[3]),
-        scaled(projection_grads[1]),
+        query_grad,
+        key_grad,
+        value_grad,
+        outgate_grad,
         scaled(forget_grad),
         scaled(bias_out),
-        scaled(out_all),
+        out_grad,
         scaled(own_half(gain_two_sum)),
-        scaled(gate_all),
-        scaled(up_all),
-        scaled(down_all),
+        gate_grad,
+        up_grad,
+        down_grad,
     )
 
 

time: 668 us -> 533 us (0.80)
  Pallas kernels: 570 us -> 474 us
  local copies, waits for them, and re-layouts: 26.2 us -> 11.3 us
  other arithmetic: 29.5 us -> 16.8 us
  waiting for transfers between devices: 13.5 us -> 2.11 us
    pallas_call x1, Pallas kernels: 283 us -> 195 us  [middle_step(): pl.pallas_call(functools.partial(middle_kernel, ring), out_shape=(jax.Sha...]
    pallas_call x1, Pallas kernels: 150 us -> 129 us  [last_step(): pl.pallas_call(functools.partial(last_kernel, ring, heads), out_shape=(ja...]
    mul x13 -> x4, other arithmetic: 17.5 us -> 2.88 us  [scaled(): return value.astype(F32) * grad_scale]
    unnamed x61 -> x13, local copies, waits for them, and re-layouts: 15.1 us -> 0.79 us
    ppermute x3, waiting for transfers between devices: 13.5 us -> 2.11 us  [move(): return lax.ppermute(value, AX, self.pairs(target, source_ok))]
    pallas_call x0 -> x1, Pallas kernels: none -> 10.5 us  [scale_step(): pl.pallas_call(functools.partial(scale_kernel, full), grid=(steps,), out_...]
  transfers between devices with their start and end apart: 3 -> 3, of which waited for: 2 -> 2; matrix products, arithmetic and copies ran while one was open for 1% -> 3% of each run, Pallas kernels for 8% -> 10%
where the time goes in v1:
time: 533 us; the launch traced here: 527 us
  Pallas kernels  474 us (89%)
  other arithmetic  16.8 us (3%)
  starting transfers between devices  16.6 us (3%)
  local copies, waits for them, and re-layouts  11.3 us (2%)
    pallas_call x1, Pallas kernels, middle_step(): pl.pallas_call(functools.partial(middle_kernel, ring), out_shape=(jax.Sha...  195 us
    pallas_call x1, Pallas kernels, last_step(): pl.pallas_call(functools.partial(last_kernel, ring, heads), out_shape=(ja...  129 us
    pallas_call x1, Pallas kernels, first_step(): pl.pallas_call(functools.partial(first_kernel, ring), out_shape=tuple((ja...  87.3 us
    pallas_call x1, Pallas kernels, attend_back(): pl.pallas_call(functools.partial(attend_back_kernel, heads), grid=(steps,...  30.1 us
    pallas_call x1, Pallas kernels, attend(): pl.pallas_call(functools.partial(attend_kernel, heads), grid=(steps,), ou...  22.2 us
    ppermute x3, starting transfers between devices, move(): return lax.ppermute(value, AX, self.pairs(target, source_ok))  16.6 us
  transfers between devices with their start and end apart: 3, of which 2 were waited for; matrix products, arithmetic and copies ran while one was open for 3% of the time, Pallas kernels for 10%

profile of v1, /device:TPU:0, one launch (start us, length us, event | category | flops | bytes accessed | tf_op | source)
XLA Modules:
  0.0 526.9 jit_solution(13990116567750847400)
XLA Ops:
  0.7 0.7 bitcast_select_fusion.1
  1.4 0.7 pad_add_fusion
  2.7 0.7 convert_bitcast_fusion
  4.0 0.7 reshape.407
  4.7 0.7 reshape.408
  5.4 1.3 concatenate.15.small_in
  6.7 87.3 %shard_map.325 = (bf16[256,1536]{1,0:T(8,128)(2,1)}, bf16[1024,1536]{1,0:T(8,128)(2,1)}, bf16[3,1536,512]{2,1,0:T(8,128)(2,1)}, bf16[384,1536]{1,0:T(8,128)(2,1)...) custom-call(bf16[256,768]{1,0:T(8,128)(2,1)} %bitcast.79, ...), custom_call_target="tpu_custom_call" | custom-call | flops 4831838208 | bytes 41943040 | tf_op jit(solution)/shard_map/pallas_call | solution.py:3152
  94.1 0.9 dynamic-slice-done
  95.2 7.5 %collective-permute-start = (bf16[384,1024]{1,0:T(8,128)(2,1)S(1)}, bf16[384,1024]{1,0:T(8,128)(2,1)}, u32[]{:S(2)}, u32[]{:S(2)}) collective-permute-start(bf16[384,1024]{1,0:T(8,128)(2,1)S(1)} %pad_maximum_fusion), channel_id=1, source_target_pairs={{0,2},{1,3},{2,0},{3,1},{4,6},{5,7},{6,4},{7,5},{8,10},{9,11},{10,... | collective-permute-start | bytes 2359304 | tf_op jit(solution)/shard_map/ppermute | solution.py:605
  103.4 0.7 fusion.24
  104.4 1.6 divide_select_fusion
  106.7 0.8 copy.44.valid_ref
  107.5 1.5 fusion.27
  109.6 1.2 convolution_add_fusion
  110.8 2.0 select_convert_fusion.1
  112.8 1.0 compare_convert_fusion.hot_ref
  113.9 22.2 %shard_map.326 = (bf16[1024,384]{1,0:T(8,128)(2,1)}, f32[1024,384]{1,0:T(8,128)}, f32[1024,128]{1,0:T(8,128)}) custom-call(s32[1]{0:T(128)} %bitcast.flag, bf16[1024,512]{1,0:T(8,128)(2,1)} %get-tuple-element.70.qg_a.near_a.own_a, bf16[1024,512]{1,0:T(8,128)(2,1)} %get-tuple-element.71.qg_b.near_b.own_b, ...), custom_call_target="tpu_custom_call" | custom-call | flops 6039797760 | bytes 7864320 | tf_op jit(solution)/shard_map/pallas_call | solution.py:875
  136.1 1.7 collective-permute-done.hid_there_in
  137.7 195.0 %shard_map.327 = (f32[1024,384]{1,0:T(8,128)}, f32[256,1536]{1,0:T(8,128)}, bf16[1024,1536]{1,0:T(8,128)(2,1)}, f32[384,2048]{1,0:T(8,128)}, bf16[384,2048]{1,0:...) custom-call(bf16[1024,384]{1,0:T(8,128)(2,1)} %get-tuple-element.80.gate, ...), custom_call_target="tpu_custom_call" | custom-call | flops 32614907904 | bytes 62914560 | tf_op jit(solution)/shard_map/pallas_call | solution.py:2534
  332.7 3.0 convert_add_fusion
  335.8 6.5 %collective-permute-start.1 = (bf16[384,1024]{1,0:T(8,128)(2,1)S(1)}, bf16[384,1024]{1,0:T(8,128)(2,1)}, u32[]{:S(2)}, u32[]{:S(2)}) collective-permute-start(bf16[384,1024]{1,0:T(8,128)(2,1)S(1)} %slice.131), channel_id=1, source_target_pairs={{0,2},{1,3},{2,0},{3,1},{4,6},{5,7},{6,4},{7,5},{8,10},{9,11},{10,... | collective-permute-start | bytes 2359304 | tf_op jit(solution)/shard_map/ppermute | solution.py:605
  342.4 2.6 collective-permute-start.2
  344.9 30.1 %shard_map.328 = (bf16[1024,768]{1,0:T(8,128)(2,1)}, f32[1024,768]{1,0:T(8,128)}, bf16[1024,768]{1,0:T(8,128)(2,1)}, f32[1024,128]{1,0:T(8,128)}, f32[1024,128]{1,0:T(8,128)}, /*index=5*/f32[1024,128]{1,0:T(8,128)}) custom-call(s32[1]{0:T(128)} %bitcast.flag, bf16[1024,512]{1,0:T(8,128)(2,1)} %get-tuple-element.70.qg_a.near_a.own_a, ...), custom_call_target="tpu_custom_call" | custom-call | flops 18119393280 | bytes 15728640 | tf_op jit(solution)/shard_map/pallas_call | solution.py:1057
  375.5 2.3 fusion.1.hid_in
  377.7 128.6 %shard_map.329 = (bf16[2,256,768]{2,1,0:T(8,128)(2,1)}, bf16[768,1664]{1,0:T(8,128)(2,1)}, bf16[768,1024]{1,0:T(8,128)(2,1)}, bf16[768,1024]{1,0:T(8,128)(2,1)},...) custom-call(bf16[1024,768]{1,0:T(8,128)(2,1)} %get-tuple-element.89.dqg_in, ...), custom_call_target="tpu_custom_call" | custom-call | flops 9663676416 | bytes 41943040 | tf_op jit(solution)/shard_map/pallas_call | solution.py:1850
  506.3 0.9 slice_reduce_fusion
  507.2 1.3 fusion.28
  508.6 0.7 slice.102
  510.0 1.0 convert_multiply_fusion
  511.0 0.8 copy.47
  511.7 0.7 dynamic-slice_multiply_fusion
  515.0 10.5 %shard_map.330 = (f32[256,768]{1,0:T(8,128)}, f32[256,768]{1,0:T(8,128)}, f32[768,384]{1,0:T(8,128)}, f32[768,384]{1,0:T(8,128)}, f32[768,384]{1,0:T(8,128)}, /*...) custom-call(f32[4,8,384]{2,1,0:T(8,128)} %get-tuple-element.106.sums, ...), custom_call_target="tpu_custom_call" | custom-call | tf_op jit(solution)/shard_map/pallas_call | solution.py:1989
  (57 shorter events, 5.5 us)
Async XLA Ops:
  94.0 1.0 dynamic-slice-start
  94.0 1.1 dynamic-slice-start.1
  94.0 8.7 %copy-start.3 = (s32[16,128]{1,0:T(8,128)S(1)}, s32[16,128]{1,0:T(8,128)}, u32[]{:S(2)}) copy-start(s32[16,128]{1,0:T(8,128)} %get-tuple-element.78) | copy-start | bytes 24580
  94.0 8.8 %copy-start.4 = (s32[4]{0:T(128)S(1)}, s32[4]{0:T(128)}, u32[]{:S(2)}) copy-start(s32[4]{0:T(128)} %constant.121) | copy-start | bytes 52
  94.0 8.8 %copy-start.5 = (s32[4]{0:T(128)S(1)}, s32[4]{0:T(128)}, u32[]{:S(2)}) copy-start(s32[4]{0:T(128)} %constant.122) | copy-start | bytes 52
  94.1 10.3 %copy-start.1 = (bf16[1024,128]{1,0:T(8,128)(2,1)S(1)}, bf16[1024,128]{1,0:T(8,128)(2,1)}, u32[]{:S(2)}) copy-start(bf16[1024,128]{1,0:T(8,128)(2,1)} %get-tuple-element.76) | copy-start | bytes 786436
  94.1 10.3 %copy-start.2 = (bf16[1024,128]{1,0:T(8,128)(2,1)S(1)}, bf16[1024,128]{1,0:T(8,128)(2,1)}, u32[]{:S(2)}) copy-start(bf16[1024,128]{1,0:T(8,128)(2,1)} %get-tuple-element.79) | copy-start | bytes 786436
  95.2 42.5 %collective-permute-start = (bf16[384,1024]{1,0:T(8,128)(2,1)S(1)}, bf16[384,1024]{1,0:T(8,128)(2,1)}, u32[]{:S(2)}, u32[]{:S(2)}) collective-permute-start(bf16[384,1024]{1,0:T(8,128)(2,1)S(1)} %pad_maximum_fusion), channel_id=1, source_target_pairs={{0,2},{1,3},{2,0},{3,1},{4,6},{5,7},{6,4},{7,5},{8,10},{9,11},{10,... | collective-permute-start | bytes 2359304 | tf_op jit(solution)/shard_map/ppermute | solution.py:605
  106.7 7.2 %copy-start = (f32[8,128,128]{2,1,0:T(8,128)}, f32[8,128,128]{2,1,0:T(8,128)S(1)}, u32[]{:S(2)}) copy-start(f32[8,128,128]{2,1,0:T(8,128)S(1)} %broadcast_add_fusion) | copy-start | bytes 1572868
  335.8 39.6 %collective-permute-start.1 = (bf16[384,1024]{1,0:T(8,128)(2,1)S(1)}, bf16[384,1024]{1,0:T(8,128)(2,1)}, u32[]{:S(2)}, u32[]{:S(2)}) collective-permute-start(bf16[384,1024]{1,0:T(8,128)(2,1)S(1)} %slice.131), channel_id=1, source_target_pairs={{0,2},{1,3},{2,0},{3,1},{4,6},{5,7},{6,4},{7,5},{8,10},{9,11},{10,... | collective-permute-start | bytes 2359304 | tf_op jit(solution)/shard_map/ppermute | solution.py:605
  342.4 35.4 %collective-permute-start.2 = (bf16[1024,384]{1,0:T(8,128)(2,1)}, bf16[1024,384]{1,0:T(8,128)(2,1)}, u32[]{:S(2)}, u32[]{:S(2)}) collective-permute-start(bf16[1024,384]{1,0:T(8,128)(2,1)} %get-tuple-element.102), channel_id=1, source_target_pairs={{0,4},{1,5},{2,6},{3,7},{4,0},{5,1},{6,2},{7,3},{8,12},{9,13},{10,... | collective-permute-start | bytes 2359304 | tf_op jit(solution)/shard_map/ppermute | solution.py:605

commit v2 on v1

--- a/solution.py
+++ b/solution.py
@@ -1110,6 +1110,9 @@
 
     def other(self, axis):
         return {axis: 1 - self.at[axis]}
+
+    def mid_home(self):
+        return lax.rem(self.at["y"] + self.at["zl"], 2)
 
     def peer(self, k):
         dy, dz = self.ring.offsets[k]
@@ -1277,7 +1280,7 @@
     slots = heads // 2
     all_w = slots * slot_w
     units = down_kept_in.shape[0] // 2
-    owner = zh == y
+    owner = zh == here.mid_home()
     peers = len(ring.offsets)
     away = here.group_away()
     all_loads = [
@@ -1488,6 +1491,26 @@
     for copy in own_pieces[2:] + y_pieces[2:]:
         copy.start()
 
+    c_copy.wait_recv()
+
+    def x_step(i, carry):
+        rows = pl.ds(pl.multiple_of(i * tile_r, tile_r), tile_r)
+        land = pl.ds(pl.multiple_of(part + i * tile_r, tile_r), tile_r)
+        value = weight_tile(part, i) + c_land[land, :].astype(F32)
+        for s in range(slots):
+            x_send[s, rows, :] = value[:, s * slot_w : (s + 1) * slot_w].astype(BF)
+        xf_send[rows, :] = value[:, all_w:].astype(BF)
+        return carry
+
+    lax.fori_loop(0, per_part, x_step, 0)
+    x_copies = {}
+    for s in (2, 1, 0):
+        x_copies[s] = remote(
+            x_send.at[s], x_land.at[s], x_send_sem.at[s], x_recv_sem.at[s], here.other("x")
+        )
+        x_copies[s].start()
+    xf_copy = remote(xf_send, xf_land, x_send_sem.at[3], x_recv_sem.at[3], here.other("x"))
+    xf_copy.start()
     load_weight.wait()
     tiles = 3
     tile_w = features // tiles
@@ -1521,26 +1544,6 @@
         for i in SUM_STARTS[k]:
             rs_copy(i).start()
 
-    c_copy.wait_recv()
-
-    def x_step(i, carry):
-        rows = pl.ds(pl.multiple_of(i * tile_r, tile_r), tile_r)
-        land = pl.ds(pl.multiple_of(part + i * tile_r, tile_r), tile_r)
-        value = weight_tile(part, i) + c_land[land, :].astype(F32)
-        for s in range(slots):
-            x_send[s, rows, :] = value[:, s * slot_w : (s + 1) * slot_w].astype(BF)
-        xf_send[rows, :] = value[:, all_w:].astype(BF)
-        return carry
-
-    lax.fori_loop(0, per_part, x_step, 0)
-    x_copies = {}
-    for s in (2, 1, 0):
-        x_copies[s] = remote(
-            x_send.at[s], x_land.at[s], x_send_sem.at[s], x_recv_sem.at[s], here.other("x")
-        )
-        x_copies[s].start()
-    xf_copy = remote(xf_send, xf_land, x_send_sem.at[3], x_recv_sem.at[3], here.other("x"))
-    xf_copy.start()
     co_copy.wait_recv()
     for s in range(slots):
         rows = slice(s * LANES, (s + 1) * LANES)
@@ -1659,7 +1662,7 @@
         if j < 2:
             quarter, head = zh, 4 * y + j
         elif j < 4:
-            quarter, head = y, j
+            quarter, head = here.mid_home(), j
         else:
             quarter, head = 1 - zh, 4 * y + j - 4
         dest = 2 + (quarter * ring.zl_count + zl) * heads + head
@@ -2736,7 +2739,7 @@
     part = features // 4
     half = features // 2
     peers = len(ring.offsets)
-    owner = zh == y
+    owner = zh == here.mid_home()
     row0 = pl.multiple_of(c * part, part)
     first0 = pl.multiple_of(2 * LANES * y, LANES)
     sources = (wq_in, wg_in, wk_in, wv_in)
@@ -3290,7 +3293,7 @@
         first = jnp.where(y == 0, value[:, 0:2], value[:, 4:6])
         slot_a = jnp.where(zh == 0, first[0], first[1])
         slot_c = jnp.where(zh == 0, first[1], first[0])
-        slot_b = jnp.where(y == 0, value[0, 2:4], value[1, 2:4])
+        slot_b = jnp.where((y + zl) % 2 == 0, value[0, 2:4], value[1, 2:4])
         return jnp.concatenate([slot_a, slot_b, slot_c], axis=0)
 
     bias_all = small_all[:, 2, :heads]

time: 533 us -> 524 us (0.983)
  starting transfers between devices: 16.6 us -> 6.33 us
    ppermute x3, starting transfers between devices: 16.6 us -> 6.33 us  [move(): return lax.ppermute(value, AX, self.pairs(target, source_ok))]
    pallas_call x1, Pallas kernels: 129 us -> 121 us  [last_step(): pl.pallas_call(functools.partial(last_kernel, ring, heads), out_shape=(ja...]
  transfers between devices with their start and end apart: 3 -> 3, of which waited for: 2 -> 1; matrix products, arithmetic and copies ran while one was open for 3% -> 3% of each run, Pallas kernels for 10% -> 10%
where the time goes in v2:
time: 524 us; the launch traced here: 515 us
  Pallas kernels  472 us (90%)
  other arithmetic  16.8 us (3%)
  local copies, waits for them, and re-layouts  11.3 us (2%)
  starting transfers between devices  6.33 us (1%)
    pallas_call x1, Pallas kernels, middle_step(): pl.pallas_call(functools.partial(middle_kernel, ring), out_shape=(jax.Sha...  199 us
    pallas_call x1, Pallas kernels, last_step(): pl.pallas_call(functools.partial(last_kernel, ring, heads), out_shape=(ja...  121 us
    pallas_call x1, Pallas kernels, first_step(): pl.pallas_call(functools.partial(first_kernel, ring), out_shape=tuple((ja...  89.7 us
    pallas_call x1, Pallas kernels, attend_back(): pl.pallas_call(functools.partial(attend_back_kernel, heads), grid=(steps,...  30.1 us
    pallas_call x1, Pallas kernels, attend(): pl.pallas_call(functools.partial(attend_kernel, heads), grid=(steps,), ou...  22.2 us
    pallas_call x1, Pallas kernels, scale_step(): pl.pallas_call(functools.partial(scale_kernel, full), grid=(steps,), out_...  10.5 us
  transfers between devices with their start and end apart: 3, of which 1 were waited for; matrix products, arithmetic and copies ran while one was open for 3% of the time, Pallas kernels for 10%

profile of v2, /device:TPU:0, one launch (start us, length us, event | category | flops | bytes accessed | tf_op | source)
XLA Modules:
  0.0 514.9 jit_solution(8785811324337002557)
XLA Ops:
  0.7 0.7 bitcast_select_fusion.1
  1.4 0.7 pad_add_fusion
  2.7 0.7 convert_bitcast_fusion
  4.0 0.7 reshape.407
  4.7 0.7 reshape.408
  5.4 1.3 concatenate.15.small_in
  6.7 89.7 %shard_map.325 = (bf16[256,1536]{1,0:T(8,128)(2,1)}, bf16[1024,1536]{1,0:T(8,128)(2,1)}, bf16[3,1536,512]{2,1,0:T(8,128)(2,1)}, bf16[384,1536]{1,0:T(8,128)(2,1)...) custom-call(bf16[256,768]{1,0:T(8,128)(2,1)} %bitcast.79, ...), custom_call_target="tpu_custom_call" | custom-call | flops 4831838208 | bytes 41943040 | tf_op jit(solution)/shard_map/pallas_call | solution.py:3155
  96.5 0.9 dynamic-slice-done
  97.6 4.8 collective-permute-start
  103.2 0.7 fusion.24
  104.1 1.6 divide_select_fusion
  106.4 0.8 copy.44.valid_ref
  107.2 1.5 fusion.27
  109.3 1.2 convolution_add_fusion
  110.5 2.0 select_convert_fusion.1
  112.6 1.0 compare_convert_fusion.hot_ref
  113.6 22.2 %shard_map.326 = (bf16[1024,384]{1,0:T(8,128)(2,1)}, f32[1024,384]{1,0:T(8,128)}, f32[1024,128]{1,0:T(8,128)}) custom-call(s32[1]{0:T(128)} %bitcast.flag, bf16[1024,512]{1,0:T(8,128)(2,1)} %get-tuple-element.70.qg_a.near_a.own_a, bf16[1024,512]{1,0:T(8,128)(2,1)} %get-tuple-element.71.qg_b.near_b.own_b, ...), custom_call_target="tpu_custom_call" | custom-call | flops 6039797760 | bytes 7864320 | tf_op jit(solution)/shard_map/pallas_call | solution.py:875
  135.8 198.8 %shard_map.327 = (f32[1024,384]{1,0:T(8,128)}, f32[256,1536]{1,0:T(8,128)}, bf16[1024,1536]{1,0:T(8,128)(2,1)}, f32[384,2048]{1,0:T(8,128)}, bf16[384,2048]{1,0:...) custom-call(bf16[1024,384]{1,0:T(8,128)(2,1)} %get-tuple-element.80.gate, ...), custom_call_target="tpu_custom_call" | custom-call | flops 32614907904 | bytes 62914560 | tf_op jit(solution)/shard_map/pallas_call | solution.py:2537
  334.6 3.0 convert_add_fusion
  337.8 1.4 collective-permute-start.2
  339.2 30.1 %shard_map.328 = (bf16[1024,768]{1,0:T(8,128)(2,1)}, f32[1024,768]{1,0:T(8,128)}, bf16[1024,768]{1,0:T(8,128)(2,1)}, f32[1024,128]{1,0:T(8,128)}, f32[1024,128]{1,0:T(8,128)}, /*index=5*/f32[1024,128]{1,0:T(8,128)}) custom-call(s32[1]{0:T(128)} %bitcast.flag, bf16[1024,512]{1,0:T(8,128)(2,1)} %get-tuple-element.70.qg_a.near_a.own_a, ...), custom_call_target="tpu_custom_call" | custom-call | flops 18119393280 | bytes 15728640 | tf_op jit(solution)/shard_map/pallas_call | solution.py:1057
  369.3 1.9 collective-permute-done.1
  371.2 2.3 fusion.1.hid_in
  373.5 120.9 %shard_map.329 = (bf16[2,256,768]{2,1,0:T(8,128)(2,1)}, bf16[768,1664]{1,0:T(8,128)(2,1)}, bf16[768,1024]{1,0:T(8,128)(2,1)}, bf16[768,1024]{1,0:T(8,128)(2,1)},...) custom-call(bf16[1024,768]{1,0:T(8,128)(2,1)} %get-tuple-element.89.dqg_in, ...), custom_call_target="tpu_custom_call" | custom-call | flops 9663676416 | bytes 41943040 | tf_op jit(solution)/shard_map/pallas_call | solution.py:1853
  494.4 0.9 slice_reduce_fusion
  495.3 1.3 fusion.28
  496.7 0.7 slice.102
  498.1 1.0 convert_multiply_fusion
  499.1 0.8 copy.47
  499.8 0.7 dynamic-slice_multiply_fusion
  500.5 0.7 dynamic-slice_multiply_fusion.1
  503.1 10.5 %shard_map.330 = (f32[256,768]{1,0:T(8,128)}, f32[256,768]{1,0:T(8,128)}, f32[768,384]{1,0:T(8,128)}, f32[768,384]{1,0:T(8,128)}, f32[768,384]{1,0:T(8,128)}, /*...) custom-call(f32[4,8,384]{2,1,0:T(8,128)} %get-tuple-element.106.sums, ...), custom_call_target="tpu_custom_call" | custom-call | tf_op jit(solution)/shard_map/pallas_call | solution.py:1992
  (57 shorter events, 4.5 us)
Async XLA Ops:
  96.4 1.0 dynamic-slice-start
  96.4 1.1 dynamic-slice-start.1
  96.4 6.1 %copy-start.3 = (s32[16,128]{1,0:T(8,128)S(1)}, s32[16,128]{1,0:T(8,128)}, u32[]{:S(2)}) copy-start(s32[16,128]{1,0:T(8,128)} %get-tuple-element.78) | copy-start | bytes 24580
  96.4 6.1 %copy-start.4 = (s32[4]{0:T(128)S(1)}, s32[4]{0:T(128)}, u32[]{:S(2)}) copy-start(s32[4]{0:T(128)} %constant.127) | copy-start | bytes 52
  96.4 6.1 %copy-start.5 = (s32[4]{0:T(128)S(1)}, s32[4]{0:T(128)}, u32[]{:S(2)}) copy-start(s32[4]{0:T(128)} %constant.128) | copy-start | bytes 52
  96.4 7.7 %copy-start.1 = (bf16[1024,128]{1,0:T(8,128)(2,1)S(1)}, bf16[1024,128]{1,0:T(8,128)(2,1)}, u32[]{:S(2)}) copy-start(bf16[1024,128]{1,0:T(8,128)(2,1)} %get-tuple-element.76) | copy-start | bytes 786436
  96.5 7.7 %copy-start.2 = (bf16[1024,128]{1,0:T(8,128)(2,1)S(1)}, bf16[1024,128]{1,0:T(8,128)(2,1)}, u32[]{:S(2)}) copy-start(bf16[1024,128]{1,0:T(8,128)(2,1)} %get-tuple-element.79) | copy-start | bytes 786436
  97.6 38.2 %collective-permute-start = (bf16[384,1024]{1,0:T(8,128)(2,1)S(1)}, bf16[384,1024]{1,0:T(8,128)(2,1)}, u32[]{:S(2)}, u32[]{:S(2)}) collective-permute-start(bf16[384,1024]{1,0:T(8,128)(2,1)S(1)} %pad_maximum_fusion), channel_id=1, source_target_pairs={{0,2},{1,3},{2,0},{3,1},{4,6},{5,7},{6,4},{7,5},{8,10},{9,11},{10,... | collective-permute-start | bytes 2359304 | tf_op jit(solution)/shard_map/ppermute | solution.py:605
  106.4 7.2 %copy-start = (f32[8,128,128]{2,1,0:T(8,128)}, f32[8,128,128]{2,1,0:T(8,128)S(1)}, u32[]{:S(2)}) copy-start(f32[8,128,128]{2,1,0:T(8,128)S(1)} %broadcast_add_fusion) | copy-start | bytes 1572868
  337.7 33.5 %collective-permute-start.1 = (bf16[384,1024]{1,0:T(8,128)(2,1)S(1)}, bf16[384,1024]{1,0:T(8,128)(2,1)}, u32[]{:S(2)}, u32[]{:S(2)}) collective-permute-start(bf16[384,1024]{1,0:T(8,128)(2,1)S(1)} %slice.131), channel_id=1, source_target_pairs={{0,2},{1,3},{2,0},{3,1},{4,6},{5,7},{6,4},{7,5},{8,10},{9,11},{10,... | collective-permute-start | bytes 2359304 | tf_op jit(solution)/shard_map/ppermute | solution.py:605
  337.8 35.7 %collective-permute-start.2 = (bf16[1024,384]{1,0:T(8,128)(2,1)}, bf16[1024,384]{1,0:T(8,128)(2,1)}, u32[]{:S(2)}, u32[]{:S(2)}) collective-permute-start(bf16[1024,384]{1,0:T(8,128)(2,1)} %get-tuple-element.102), channel_id=1, source_target_pairs={{0,4},{1,5},{2,6},{3,7},{4,0},{5,1},{6,2},{7,3},{8,12},{9,13},{10,... | collective-permute-start | bytes 2359304 | tf_op jit(solution)/shard_map/ppermute | solution.py:605

commit v3 on v2

--- a/solution.py
+++ b/solution.py
@@ -1180,7 +1180,9 @@
     mixed_in,
     tokens_in,
     residual_in,
-    hid_in,
+    hid_kept_in,
+    hid_there_in,
+    hid_z_in,
     down_kept_in,
     down_there_in,
     gain_ref,
@@ -1219,6 +1221,8 @@
     total,
     c_send,
     c_land,
+    cf_send,
+    cf_land,
     kept,
     x_send,
     x_land,
@@ -1235,6 +1239,10 @@
     full_f,
     co_send,
     co_land,
+    kept_h,
+    there_h,
+    z_h,
+    final_h,
     kept_d,
     there_d,
     zd_send,
@@ -1298,6 +1306,9 @@
             )
         )
     all_loads += [
+        (hid_kept_in.at[:, : 2 * units], kept_h),
+        (hid_there_in.at[:, : 2 * units], there_h),
+        (hid_z_in, z_h),
         (down_kept_in, kept_d),
         (down_there_in, there_d),
         (normed_in, normed),
@@ -1310,13 +1321,14 @@
     loads = [
         pltpu.make_async_copy(a, b, load_sem.at[i]) for i, (a, b) in enumerate(all_loads)
     ]
-    first_loads = 8 + slots
+    first_loads = 11 + slots
     for copy in loads[:first_loads]:
         copy.start()
     load_row, load_near_col, load_far_col, load_far, load_near = loads[:5]
     load_dqg = loads[5 : 5 + slots]
-    load_kept_d, load_there_d = loads[5 + slots : 7 + slots]
-    load_normed, load_weight, load_gated, load_mixed, load_tokens, load_residual = loads[7 + slots :]
+    load_hid = loads[5 + slots : 8 + slots]
+    load_kept_d, load_there_d = loads[8 + slots : 10 + slots]
+    load_normed, load_weight, load_gated, load_mixed, load_tokens, load_residual = loads[10 + slots :]
 
     here.greet_group(
         [here.peer(k) for k in range(1, peers)]
@@ -1343,14 +1355,21 @@
         return remote(src, dst, y_send_sem.at[i], y_recv_sem.at[i], here.other("y"))
 
     pieces = [
-        (hid_in.at[:, :units], rows_of(gate_out, y * units, units)),
-        (hid_in.at[:, units:], rows_of(up_out, y * units, units)),
+        (final_h.at[0], rows_of(gate_out, y * units, units)),
+        (final_h.at[1], rows_of(up_out, y * units, units)),
         (final_d, cols_of(down_out, y * units, units)),
     ]
     own_pieces = [
         pltpu.make_async_copy(src, dst, local_sem.at[i]) for i, (src, dst) in enumerate(pieces)
     ]
     y_pieces = [y_copy(i, src, dst) for i, (src, dst) in enumerate(pieces)]
+    for copy in load_hid:
+        copy.wait()
+    for i in range(2):
+        cols = slice(i * units, (i + 1) * units)
+        final_h[i] = (
+            kept_h[:, cols] + there_h[:, cols].astype(F32) + z_h[:, cols].astype(F32)
+        ).astype(BF)
     for copy in own_pieces[:2] + y_pieces[:2]:
         copy.start()
 
@@ -1408,6 +1427,27 @@
         return carry
 
     lax.fori_loop(0, all_units, merge, 0)
+    load_normed.wait()
+    tile_r = LANES
+    per_part = part // tile_r
+
+    def weight_tile(first, i):
+        cols = pl.ds(pl.multiple_of(first + i * tile_r, LANES), tile_r)
+        return tn_dot(normed[:, cols], grads[:, :all_w])
+
+    def forget_tile(first, i):
+        cols = pl.ds(pl.multiple_of(first + i * tile_r, LANES), tile_r)
+        return tn_dot(normed[:, cols], grads[:, all_w:])
+
+    def c_step(i, carry):
+        rows = pl.ds(pl.multiple_of(i * tile_r, tile_r), tile_r)
+        c_send[rows, :] = weight_tile(2 * part, i).astype(BF)
+        return carry
+
+    lax.fori_loop(0, 2 * per_part, c_step, 0)
+    c_copy = remote(c_send, c_land, c_send_sem.at[0], c_recv_sem.at[0], here.other("c"))
+    c_copy.start()
+
     load_far_col.wait()
     col_swap.wait_recv()
     tot_swap.wait_recv()
@@ -1453,37 +1493,6 @@
         grads[unit_rows(u), all_w:] = value.astype(BF)
         bias = bias + jnp.sum(value, axis=0, keepdims=True)
 
-    load_normed.wait()
-    tile_r = LANES
-    per_part = part // tile_r
-
-    def weight_tile(first, i):
-        cols = pl.ds(pl.multiple_of(first + i * tile_r, LANES), tile_r)
-        return tn_dot(normed[:, cols], grads[...])
-
-    def c_step(i, carry):
-        rows = pl.ds(pl.multiple_of(i * tile_r, tile_r), tile_r)
-        c_send[rows, :] = weight_tile(2 * part, i).astype(BF)
-        return carry
-
-    lax.fori_loop(0, 2 * per_part, c_step, 0)
-    c_copy = remote(c_send, c_land, c_send_sem.at[0], c_recv_sem.at[0], here.other("c"))
-    c_copy.start()
-
-    load_gated.wait()
-    load_mixed.wait()
-    out_rows = slots * LANES
-
-    def out_tile(s, cols):
-        return tn_dot(gated[:, s * LANES : (s + 1) * LANES], mixed[:, cols])
-
-    for s in range(slots):
-        co_send[s * LANES : (s + 1) * LANES, :] = out_tile(
-            s, slice(2 * part, features)
-        ).astype(BF)
-    co_copy = remote(co_send, co_land, c_send_sem.at[1], c_recv_sem.at[1], here.other("c"))
-    co_copy.start()
-
     zd_copy.wait_recv()
     final_d[...] = (
         kept_d[:units, :] + there_d[:units, :].astype(F32) + zd_land[...].astype(F32)
@@ -1499,7 +1508,6 @@
         value = weight_tile(part, i) + c_land[land, :].astype(F32)
         for s in range(slots):
             x_send[s, rows, :] = value[:, s * slot_w : (s + 1) * slot_w].astype(BF)
-        xf_send[rows, :] = value[:, all_w:].astype(BF)
         return carry
 
     lax.fori_loop(0, per_part, x_step, 0)
@@ -1509,8 +1517,6 @@
             x_send.at[s], x_land.at[s], x_send_sem.at[s], x_recv_sem.at[s], here.other("x")
         )
         x_copies[s].start()
-    xf_copy = remote(xf_send, xf_land, x_send_sem.at[3], x_recv_sem.at[3], here.other("x"))
-    xf_copy.start()
     load_weight.wait()
     tiles = 3
     tile_w = features // tiles
@@ -1544,6 +1550,40 @@
         for i in SUM_STARTS[k]:
             rs_copy(i).start()
 
+    def cf_step(i, carry):
+        rows = pl.ds(pl.multiple_of(i * tile_r, tile_r), tile_r)
+        cf_send[rows, :] = forget_tile(2 * part, i).astype(BF)
+        return carry
+
+    lax.fori_loop(0, 2 * per_part, cf_step, 0)
+    cf_copy = remote(cf_send, cf_land, c_send_sem.at[2], c_recv_sem.at[2], here.other("c"))
+    cf_copy.start()
+
+    load_gated.wait()
+    load_mixed.wait()
+    out_rows = slots * LANES
+
+    def out_tile(s, cols):
+        return tn_dot(gated[:, s * LANES : (s + 1) * LANES], mixed[:, cols])
+
+    for s in range(slots):
+        co_send[s * LANES : (s + 1) * LANES, :] = out_tile(
+            s, slice(2 * part, features)
+        ).astype(BF)
+    co_copy = remote(co_send, co_land, c_send_sem.at[1], c_recv_sem.at[1], here.other("c"))
+    co_copy.start()
+
+    cf_copy.wait_recv()
+
+    def xf_step(i, carry):
+        rows = pl.ds(pl.multiple_of(i * tile_r, tile_r), tile_r)
+        land = pl.ds(pl.multiple_of(part + i * tile_r, tile_r), tile_r)
+        xf_send[rows, :] = (forget_tile(part, i) + cf_land[land, :].astype(F32)).astype(BF)
+        return carry
+
+    lax.fori_loop(0, per_part, xf_step, 0)
+    xf_copy = remote(xf_send, xf_land, x_send_sem.at[3], x_recv_sem.at[3], here.other("x"))
+    xf_copy.start()
     co_copy.wait_recv()
     for s in range(slots):
         rows = slice(s * LANES, (s + 1) * LANES)
@@ -1558,7 +1598,7 @@
         value = weight_tile(0, i) + c_land[rows, :].astype(F32)
         for s in range(slots):
             kept[s, rows, :] = value[:, s * slot_w : (s + 1) * slot_w]
-        kept_f[rows, :] = value[:, all_w:]
+        kept_f[rows, :] = forget_tile(0, i) + cf_land[rows, :].astype(F32)
         return carry
 
     lax.fori_loop(0, per_part, own_step, 0)
@@ -1816,7 +1856,7 @@
         gain_step(i).wait_send()
     for i in range(6):
         rs_copy(i).wait_send()
-    for copy in [c_copy, co_copy, x_copies[0], x_copies[1], x_copies[2], xf_copy, xo_copy]:
+    for copy in [c_copy, cf_copy, co_copy, x_copies[0], x_copies[1], x_copies[2], xf_copy, xo_copy]:
         copy.wait_send()
     for copy in [far_swap, col_swap, tot_swap, z_first, z_forget, zo_first, zd_copy]:
         copy.wait_send()
@@ -1839,7 +1879,7 @@
     rows = near.shape[0]
     weight, normed, gated = large[6:9]
     tokens = large[10]
-    units = large[13].shape[0] // 2
+    units = large[15].shape[0] // 2
     local, features = tokens.shape
     part = features // 4
     half = features // 2
@@ -1884,8 +1924,10 @@
             vmem((peers - 1, local, features), BF),
             vmem((peers - 1, local, features), BF),
             vmem((local, features), F32),
-            vmem((half, all_w + LANES), BF),
-            vmem((half, all_w + LANES), BF),
+            vmem((half, all_w), BF),
+            vmem((half, all_w), BF),
+            vmem((half, LANES), BF),
+            vmem((half, LANES), BF),
             vmem((slots, part, slot_w), F32),
             vmem((slots, part, slot_w), BF),
             vmem((slots, part, slot_w), BF),
@@ -1902,6 +1944,10 @@
             vmem((part, LANES), BF),
             vmem((slots * LANES, half), BF),
             vmem((slots * LANES, half), BF),
+            vmem((part, 2 * units), F32),
+            vmem((part, 2 * units), BF),
+            vmem((part, 2 * units), BF),
+            vmem((2, part, units), BF),
             vmem((2 * units, part), F32),
             vmem((2 * units, part), BF),
             vmem((units, part), BF),
@@ -1917,7 +1963,7 @@
             vmem((4, 8, part), F32),
             vmem((6, 4, 8, part), F32),
             vmem((5, 4, 8, part), F32),
-            dma((13 + slots,)),
+            dma((16 + slots,)),
             dma((13,)),
             dma((3,)),
             dma((3,)),
@@ -1927,8 +1973,8 @@
             dma((5,)),
             dma((6,)),
             dma((6,)),
-            dma((2,)),
-            dma((2,)),
+            dma((3,)),
+            dma((3,)),
             dma((5,)),
             dma((5,)),
             dma((6,)),
@@ -3435,16 +3481,8 @@
         heads,
     )
 
-    def low(value):
-        return lax.reduce_precision(value, 8, 7).astype(BF)
-
-    def over_zh(value, dim):
-        size = value.shape[dim] // 2
-        mine = lax.slice_in_dim(value, 0, size, axis=dim)
-        theirs = lax.slice_in_dim(value, size, 2 * size, axis=dim)
-        return low(mine + ring.swap(theirs.astype(BF), "zh").astype(F32))
-
-    hid_mine = over_zh(hid_kept + hid_there.astype(F32), 1)
+    edge = 2 * half_units
+    hid_z = ring.swap((hid_kept[:, edge:] + hid_there[:, edge:].astype(F32)).astype(BF), "zh")
     down_there = ring.swap(down_there, "x")
     rows_back, proj_all, gate_all, up_all, down_all, out_all, small_sums = last_step(
         ring,
@@ -3462,7 +3500,9 @@
             grad_residual_all,
             tokens_b,
             grad_residual,
-            hid_mine,
+            hid_kept,
+            hid_there,
+            hid_z,
             down_kept,
             down_there,
         ],

time: 524 us -> 521 us (level)
  transfers between devices with their start and end apart: 3 -> 3, of which waited for: 1 -> 1; matrix products, arithmetic and copies ran while one was open for 3% -> 2% of each run, Pallas kernels for 10% -> 10%
where the time goes in v3:
time: 521 us; the launch traced here: 511 us
  Pallas kernels  472 us (91%)
  other arithmetic  13.4 us (3%)
  local copies, waits for them, and re-layouts  12.1 us (2%)
  starting transfers between devices  5.96 us (1%)
    pallas_call x1, Pallas kernels, middle_step(): pl.pallas_call(functools.partial(middle_kernel, ring), out_shape=(jax.Sha...  199 us
    pallas_call x1, Pallas kernels, last_step(): pl.pallas_call(functools.partial(last_kernel, ring, heads), out_shape=(ja...  120 us
    pallas_call x1, Pallas kernels, first_step(): pl.pallas_call(functools.partial(first_kernel, ring), out_shape=tuple((ja...  89.7 us
    pallas_call x1, Pallas kernels, attend_back(): pl.pallas_call(functools.partial(attend_back_kernel, heads), grid=(steps,...  30 us
    pallas_call x1, Pallas kernels, attend(): pl.pallas_call(functools.partial(attend_kernel, heads), grid=(steps,), ou...  22.2 us
    pallas_call x1, Pallas kernels, scale_step(): pl.pallas_call(functools.partial(scale_kernel, full), grid=(steps,), out_...  10.5 us
  transfers between devices with their start and end apart: 3, of which 1 were waited for; matrix products, arithmetic and copies ran while one was open for 2% of the time, Pallas kernels for 10%

profile of v3, /device:TPU:0, one launch (start us, length us, event | category | flops | bytes accessed | tf_op | source)
XLA Modules:
  0.0 510.9 jit_solution(11952867893518903377)
XLA Ops:
  0.7 0.7 reshape.407
  1.3 0.7 reshape.408
  2.7 0.7 convert_bitcast_fusion
  3.4 0.7 bitcast_select_fusion.1
  4.1 0.7 pad_add_fusion
  5.4 1.3 concatenate.15.small_in
  6.7 89.7 %shard_map.325 = (bf16[256,1536]{1,0:T(8,128)(2,1)}, bf16[1024,1536]{1,0:T(8,128)(2,1)}, bf16[3,1536,512]{2,1,0:T(8,128)(2,1)}, bf16[384,1536]{1,0:T(8,128)(2,1)...) custom-call(bf16[256,768]{1,0:T(8,128)(2,1)} %bitcast.79, ...), custom_call_target="tpu_custom_call" | custom-call | flops 4831838208 | bytes 41943040 | tf_op jit(solution)/shard_map/pallas_call | solution.py:3201
  96.4 0.9 dynamic-slice-done
  97.6 4.9 collective-permute-start
  102.6 0.7 fusion.22
  103.6 1.6 divide_select_fusion
  106.5 0.8 copy.44.valid_ref
  107.3 1.5 fusion.25
  109.1 1.2 convolution_add_fusion
  110.6 2.0 select_convert_fusion.1
  112.6 1.0 compare_convert_fusion.hot_ref
  113.6 22.2 %shard_map.326 = (bf16[1024,384]{1,0:T(8,128)(2,1)}, f32[1024,384]{1,0:T(8,128)}, f32[1024,128]{1,0:T(8,128)}) custom-call(s32[1]{0:T(128)} %bitcast.flag, bf16[1024,512]{1,0:T(8,128)(2,1)} %get-tuple-element.70.qg_a.near_a.own_a, bf16[1024,512]{1,0:T(8,128)(2,1)} %get-tuple-element.71.qg_b.near_b.own_b, ...), custom_call_target="tpu_custom_call" | custom-call | flops 6039797760 | bytes 7864320 | tf_op jit(solution)/shard_map/pallas_call | solution.py:875
  135.9 199.1 %shard_map.327 = (f32[1024,384]{1,0:T(8,128)}, f32[256,1536]{1,0:T(8,128)}, bf16[1024,1536]{1,0:T(8,128)(2,1)}, f32[384,2048]{1,0:T(8,128)}, bf16[384,2048]{1,0:...) custom-call(bf16[1024,384]{1,0:T(8,128)(2,1)} %get-tuple-element.80.gate, ...), custom_call_target="tpu_custom_call" | custom-call | flops 32614907904 | bytes 62914560 | tf_op jit(solution)/shard_map/pallas_call | solution.py:2583
  335.0 1.9 add_convert_fusion
  337.0 1.0 collective-permute-start.2
  338.0 30.0 %shard_map.328 = (bf16[1024,768]{1,0:T(8,128)(2,1)}, f32[1024,768]{1,0:T(8,128)}, bf16[1024,768]{1,0:T(8,128)(2,1)}, f32[1024,128]{1,0:T(8,128)}, f32[1024,128]{1,0:T(8,128)}, /*index=5*/f32[1024,128]{1,0:T(8,128)}) custom-call(s32[1]{0:T(128)} %bitcast.flag, bf16[1024,512]{1,0:T(8,128)(2,1)} %get-tuple-element.70.qg_a.near_a.own_a, ...), custom_call_target="tpu_custom_call" | custom-call | flops 18119393280 | bytes 15728640 | tf_op jit(solution)/shard_map/pallas_call | solution.py:1057
  368.0 1.5 collective-permute-done.1.hid_z_in
  369.5 0.9 copy-done.6
  370.4 120.0 %shard_map.329 = (bf16[2,256,768]{2,1,0:T(8,128)(2,1)}, bf16[768,1664]{1,0:T(8,128)(2,1)}, bf16[768,1024]{1,0:T(8,128)(2,1)}, bf16[768,1024]{1,0:T(8,128)(2,1)},...) custom-call(bf16[1024,768]{1,0:T(8,128)(2,1)} %get-tuple-element.89.dqg_in, ...), custom_call_target="tpu_custom_call" | custom-call | flops 9663676416 | bytes 41943040 | tf_op jit(solution)/shard_map/pallas_call | solution.py:1893
  490.4 1.3 fusion.26
  491.8 0.9 slice_reduce_fusion
  492.7 0.7 slice.101
  494.7 1.0 convert_multiply_fusion
  495.7 0.8 copy.47
  496.5 0.7 dynamic-slice_multiply_fusion.1
  497.1 0.7 dynamic-slice_multiply_fusion
  499.0 10.5 %shard_map.330 = (f32[256,768]{1,0:T(8,128)}, f32[256,768]{1,0:T(8,128)}, f32[768,384]{1,0:T(8,128)}, f32[768,384]{1,0:T(8,128)}, f32[768,384]{1,0:T(8,128)}, /*...) custom-call(f32[4,8,384]{2,1,0:T(8,128)} %get-tuple-element.106.sums, ...), custom_call_target="tpu_custom_call" | custom-call | tf_op jit(solution)/shard_map/pallas_call | solution.py:2038
  (59 shorter events, 4.4 us)
Async XLA Ops:
  96.4 1.0 dynamic-slice-start
  96.4 1.1 dynamic-slice-start.1
  96.4 6.2 %copy-start.3 = (s32[16,128]{1,0:T(8,128)S(1)}, s32[16,128]{1,0:T(8,128)}, u32[]{:S(2)}) copy-start(s32[16,128]{1,0:T(8,128)} %get-tuple-element.78) | copy-start | bytes 24580
  96.4 7.1 %copy-start.1 = (bf16[1024,128]{1,0:T(8,128)(2,1)S(1)}, bf16[1024,128]{1,0:T(8,128)(2,1)}, u32[]{:S(2)}) copy-start(bf16[1024,128]{1,0:T(8,128)(2,1)} %get-tuple-element.76) | copy-start | bytes 786436
  96.4 7.1 %copy-start.2 = (bf16[1024,128]{1,0:T(8,128)(2,1)S(1)}, bf16[1024,128]{1,0:T(8,128)(2,1)}, u32[]{:S(2)}) copy-start(bf16[1024,128]{1,0:T(8,128)(2,1)} %get-tuple-element.79) | copy-start | bytes 786436
  97.6 38.3 %collective-permute-start = (bf16[384,1024]{1,0:T(8,128)(2,1)S(1)}, bf16[384,1024]{1,0:T(8,128)(2,1)}, u32[]{:S(2)}, u32[]{:S(2)}) collective-permute-start(bf16[384,1024]{1,0:T(8,128)(2,1)S(1)} %pad_maximum_fusion), channel_id=1, source_target_pairs={{0,2},{1,3},{2,0},{3,1},{4,6},{5,7},{6,4},{7,5},{8,10},{9,11},{10,... | collective-permute-start | bytes 2359304 | tf_op jit(solution)/shard_map/ppermute | solution.py:605
  103.5 2.1 copy-start.4
  103.6 2.1 copy-start.5
  106.1 7.5 %copy-start = (f32[8,128,128]{2,1,0:T(8,128)}, f32[8,128,128]{2,1,0:T(8,128)S(1)}, u32[]{:S(2)}) copy-start(f32[8,128,128]{2,1,0:T(8,128)S(1)} %broadcast_add_fusion) | copy-start | bytes 1572868
  335.0 2.0 copy-start.7
  336.9 32.6 %collective-permute-start.1 = (bf16[384,1024]{1,0:T(8,128)(2,1)S(1)}, bf16[384,1024]{1,0:T(8,128)(2,1)S(1)}, u32[]{:S(2)}, u32[]{:S(2)}) collective-permute-start(bf16[384,1024]{1,0:T(8,128)(2,1)S(1)} %add_convert_fusion), channel_id=1, source_target_pairs={{0,2},{1,3},{2,0},{3,1},{4,6},{5,7},{6,4},{7,5},{8,10},{9,11},{10,... | collective-permute-start | bytes 2359304 | tf_op jit(solution)/shard_map/ppermute | solution.py:605
  337.0 32.5 %collective-permute-start.2 = (bf16[1024,384]{1,0:T(8,128)(2,1)S(1)}, bf16[1024,384]{1,0:T(8,128)(2,1)}, u32[]{:S(2)}, u32[]{:S(2)}) collective-permute-start(bf16[1024,384]{1,0:T(8,128)(2,1)S(1)} %copy-done.7), channel_id=1, source_target_pairs={{0,4},{1,5},{2,6},{3,7},{4,0},{5,1},{6,2},{7,3},{8,12},{9,13},{10,... | collective-permute-start | bytes 2359304 | tf_op jit(solution)/shard_map/ppermute | solution.py:605
  369.5 0.9 copy-start.6

commit v4 on v3

--- a/solution.py
+++ b/solution.py
@@ -2968,11 +2968,6 @@
     for i in range(4):
         z_piece(i, 2).start()
 
-    @pl.when(owner)
-    def _():
-        for i in range(4):
-            z_piece(i, 1).start()
-
     z_out = [
         remote(
             w_out_in.at[pl.ds(first0, LANES), pl.ds(row0, part)],
@@ -3025,6 +3020,11 @@
     c_copy(0).start()
     for i in range(4):
         z_piece(i, 2).wait_recv()
+    @pl.when(owner)
+    def _():
+        for i in range(4):
+            z_piece(i, 1).start()
+
     x_copy(2).start()
 
     @pl.when(owner)

time: 521 us -> 524 us (level)
  the two profiles are of different devices: /device:TPU:0 before, /device:TPU:27 now
where the time goes in v4:
time: 524 us; the launch traced here: 517 us
  Pallas kernels  475 us (91%)
  other arithmetic  13.4 us (3%)
  local copies, waits for them, and re-layouts  12.1 us (2%)
  waiting for transfers between devices  9.87 us (2%)
    pallas_call x1, Pallas kernels, middle_step(): pl.pallas_call(functools.partial(middle_kernel, ring), out_shape=(jax.Sha...  198 us
    pallas_call x1, Pallas kernels, last_step(): pl.pallas_call(functools.partial(last_kernel, ring, heads), out_shape=(ja...  126 us
    pallas_call x1, Pallas kernels, first_step(): pl.pallas_call(functools.partial(first_kernel, ring), out_shape=tuple((ja...  88.4 us
    pallas_call x1, Pallas kernels, attend_back(): pl.pallas_call(functools.partial(attend_back_kernel, heads), grid=(steps,...  30.1 us
    pallas_call x1, Pallas kernels, attend(): pl.pallas_call(functools.partial(attend_kernel, heads), grid=(steps,), ou...  22.2 us
    pallas_call x1, Pallas kernels, scale_step(): pl.pallas_call(functools.partial(scale_kernel, full), grid=(steps,), out_...  10.5 us
  transfers between devices with their start and end apart: 3, of which 2 were waited for; matrix products, arithmetic and copies ran while one was open for 2% of the time, Pallas kernels for 10%

profile of v4, /device:TPU:27, one launch (start us, length us, event | category | flops | bytes accessed | tf_op | source)
XLA Modules:
  0.0 516.5 jit_solution(17808825099814652167)
XLA Ops:
  0.7 0.7 reshape.407
  1.3 0.7 reshape.408
  2.0 0.7 pad.13
  2.7 0.7 convert_bitcast_fusion
  3.4 0.7 bitcast_select_fusion.1
  4.1 0.7 pad_add_fusion
  5.4 1.3 concatenate.15.small_in
  6.7 88.4 %shard_map.325 = (bf16[256,1536]{1,0:T(8,128)(2,1)}, bf16[1024,1536]{1,0:T(8,128)(2,1)}, bf16[3,1536,512]{2,1,0:T(8,128)(2,1)}, bf16[384,1536]{1,0:T(8,128)(2,1)...) custom-call(bf16[256,768]{1,0:T(8,128)(2,1)} %bitcast.79, ...), custom_call_target="tpu_custom_call" | custom-call | flops 4831838208 | bytes 41943040 | tf_op jit(solution)/shard_map/pallas_call | solution.py:3201
  95.1 0.9 dynamic-slice-done
  96.5 0.7 fusion.22
  97.4 1.6 divide_select_fusion
  100.3 0.8 copy.44.valid_ref
  101.1 1.5 fusion.25
  102.9 1.2 convolution_add_fusion
  104.5 2.0 select_convert_fusion.1
  106.5 1.0 compare_convert_fusion.hot_ref
  107.5 22.2 %shard_map.326 = (bf16[1024,384]{1,0:T(8,128)(2,1)}, f32[1024,384]{1,0:T(8,128)}, f32[1024,128]{1,0:T(8,128)}) custom-call(s32[1]{0:T(128)} %bitcast.flag, bf16[1024,512]{1,0:T(8,128)(2,1)} %get-tuple-element.70.qg_a.near_a.own_a, bf16[1024,512]{1,0:T(8,128)(2,1)} %get-tuple-element.71.qg_b.near_b.own_b, ...), custom_call_target="tpu_custom_call" | custom-call | flops 6039797760 | bytes 7864320 | tf_op jit(solution)/shard_map/pallas_call | solution.py:875
  129.7 3.6 collective-permute-done.hid_there_in
  133.3 197.7 %shard_map.327 = (f32[1024,384]{1,0:T(8,128)}, f32[256,1536]{1,0:T(8,128)}, bf16[1024,1536]{1,0:T(8,128)(2,1)}, f32[384,2048]{1,0:T(8,128)}, bf16[384,2048]{1,0:...) custom-call(bf16[1024,384]{1,0:T(8,128)(2,1)} %get-tuple-element.80.gate, ...), custom_call_target="tpu_custom_call" | custom-call | flops 32614907904 | bytes 62914560 | tf_op jit(solution)/shard_map/pallas_call | solution.py:2583
  331.0 1.9 add_convert_fusion
  333.1 30.1 %shard_map.328 = (bf16[1024,768]{1,0:T(8,128)(2,1)}, f32[1024,768]{1,0:T(8,128)}, bf16[1024,768]{1,0:T(8,128)(2,1)}, f32[1024,128]{1,0:T(8,128)}, f32[1024,128]{1,0:T(8,128)}, /*index=5*/f32[1024,128]{1,0:T(8,128)}) custom-call(s32[1]{0:T(128)} %bitcast.flag, bf16[1024,512]{1,0:T(8,128)(2,1)} %get-tuple-element.70.qg_a.near_a.own_a, ...), custom_call_target="tpu_custom_call" | custom-call | flops 18119393280 | bytes 15728640 | tf_op jit(solution)/shard_map/pallas_call | solution.py:1057
  363.2 6.3 %collective-permute-done.1.hid_z_in = bf16[384,1024]{1,0:T(8,128)(2,1)S(1)} collective-permute-done((bf16[384,1024]{1,0:T(8,128)(2,1)S(1)}, bf16[384,1024]{1,0:T(8,128)(2,1)S(1)}, u32[]{:S(2)}, u32[]{:S(2)}) %collective-permute-start.1) | collective-permute-done | bytes 786464 | tf_op jit(solution)/shard_map/ppermute | solution.py:605
  369.5 0.9 copy-done.6
  370.4 125.7 %shard_map.329 = (bf16[2,256,768]{2,1,0:T(8,128)(2,1)}, bf16[768,1664]{1,0:T(8,128)(2,1)}, bf16[768,1024]{1,0:T(8,128)(2,1)}, bf16[768,1024]{1,0:T(8,128)(2,1)},...) custom-call(bf16[1024,768]{1,0:T(8,128)(2,1)} %get-tuple-element.89.dqg_in, ...), custom_call_target="tpu_custom_call" | custom-call | flops 9663676416 | bytes 41943040 | tf_op jit(solution)/shard_map/pallas_call | solution.py:1893
  496.1 1.3 fusion.26
  497.4 0.9 slice_reduce_fusion
  498.3 0.7 slice.101
  500.4 1.0 convert_multiply_fusion
  501.3 0.8 copy.47
  502.1 0.7 dynamic-slice_multiply_fusion.1
  502.8 0.7 dynamic-slice_multiply_fusion
  504.7 10.5 %shard_map.330 = (f32[256,768]{1,0:T(8,128)}, f32[256,768]{1,0:T(8,128)}, f32[768,384]{1,0:T(8,128)}, f32[768,384]{1,0:T(8,128)}, f32[768,384]{1,0:T(8,128)}, /*...) custom-call(f32[4,8,384]{2,1,0:T(8,128)} %get-tuple-element.106.sums, ...), custom_call_target="tpu_custom_call" | custom-call | tf_op jit(solution)/shard_map/pallas_call | solution.py:2038
  (59 shorter events, 3.9 us)
Async XLA Ops:
  95.0 1.0 dynamic-slice-start
  95.0 1.1 dynamic-slice-start.1
  95.1 1.4 copy-start.3
  95.1 2.3 copy-start.1
  95.1 2.3 copy-start.2
  96.3 37.0 %collective-permute-start = (bf16[384,1024]{1,0:T(8,128)(2,1)S(1)}, bf16[384,1024]{1,0:T(8,128)(2,1)}, u32[]{:S(2)}, u32[]{:S(2)}) collective-permute-start(bf16[384,1024]{1,0:T(8,128)(2,1)S(1)} %pad_maximum_fusion), channel_id=1, source_target_pairs={{0,2},{1,3},{2,0},{3,1},{4,6},{5,7},{6,4},{7,5},{8,10},{9,11},{10,... | collective-permute-start | bytes 2359304 | tf_op jit(solution)/shard_map/ppermute | solution.py:605
  97.4 2.1 copy-start.4
  97.4 2.1 copy-start.5
  100.0 7.5 %copy-start = (f32[8,128,128]{2,1,0:T(8,128)}, f32[8,128,128]{2,1,0:T(8,128)S(1)}, u32[]{:S(2)}) copy-start(f32[8,128,128]{2,1,0:T(8,128)S(1)} %broadcast_add_fusion) | copy-start | bytes 1572868
  331.0 2.0 copy-start.7
  333.0 36.5 %collective-permute-start.1 = (bf16[384,1024]{1,0:T(8,128)(2,1)S(1)}, bf16[384,1024]{1,0:T(8,128)(2,1)S(1)}, u32[]{:S(2)}, u32[]{:S(2)}) collective-permute-start(bf16[384,1024]{1,0:T(8,128)(2,1)S(1)} %add_convert_fusion), channel_id=1, source_target_pairs={{0,2},{1,3},{2,0},{3,1},{4,6},{5,7},{6,4},{7,5},{8,10},{9,11},{10,... | collective-permute-start | bytes 2359304 | tf_op jit(solution)/shard_map/ppermute | solution.py:605
  333.1 36.5 %collective-permute-start.2 = (bf16[1024,384]{1,0:T(8,128)(2,1)S(1)}, bf16[1024,384]{1,0:T(8,128)(2,1)}, u32[]{:S(2)}, u32[]{:S(2)}) collective-permute-start(bf16[1024,384]{1,0:T(8,128)(2,1)S(1)} %copy-done.7), channel_id=1, source_target_pairs={{0,4},{1,5},{2,6},{3,7},{4,0},{5,1},{6,2},{7,3},{8,12},{9,13},{10,... | collective-permute-start | bytes 2359304 | tf_op jit(solution)/shard_map/ppermute | solution.py:605
  369.5 0.9 copy-start.6
